TPU v7x, 32 devices: a whole 2x2x4 slice. The times are simulated.
32 devices in a mesh: lat: 8 (over z, y), depth: 4 (over x, core).
Axes of the slice: x: 2, y: 2, z: 4, core: 2. Of those that a mesh axis runs over, the one named last changes fastest.
Arguments:
- grade_field: float32 [64, 128, 2048], P('depth', 'lat'), may hold values from 0 to 1
- amplitude: float32 [64, 128, 2048], P('depth', 'lat'), may hold values from -6 to 6
- tf_table: int32 [4, 128], replicated, may hold values from 0 to 65535
- brick_mask: int32 [8, 16, 8], P('depth', 'lat'), may hold values 0 or 1
Outputs:
- frame: float32 [4, 128, 2048], P(None, 'lat', 'depth')
All inputs are finite; a program needn't handle non-finite values. No bound on the sum of `brick_mask` on one device may be relied on, other than what follows from the above.
Results may differ from a plain program's by a relative error of at most 0.00073.
Values sent between devices are 32-bit elements; how exact they have to be, the bound alone decides.
No kernel may reach another device: no remote copies, remote signals or barrier semaphores. Data moves between devices by JAX's collectives and lax.ppermute only.
A program may use at most 128 MiB of HBM per device.

v0:
```python
import jax
import jax.numpy as jnp
from jax import lax
from jax.sharding import PartitionSpec as P

MZ = 8
MX = 8
MY = 256


def with_halo(shard, sides, width):
    for axis, dim in sides:
        size, length = (lax.axis_size(axis), shard.shape[dim])
        up = [(i, (i + 1) % size) for i in range(size - 1)]
        down = [(j, i) for i, j in up]
        last = lax.slice_in_dim(shard, length - width, length, axis=dim)
        first = lax.slice_in_dim(shard, 0, width, axis=dim)
        before = lax.ppermute(last, axis, up)
        after = lax.ppermute(first, axis, down)
        shard = jnp.concatenate([before, shard, after], axis=dim)
    return shard


def partner(shard, axis, distance):
    return lax.ppermute(shard, axis, [(i, i ^ 1 << distance) for i in range(lax.axis_size(axis))])


def table_lookup(grade_flat, table_scaled, bin_count):
    bin_points = jnp.arange(bin_count).astype(jnp.float32)[:, None]
    position = grade_flat[None, :] * (bin_count - 1.0)
    hat_weights = jnp.maximum(0.0, 1.0 - jnp.abs(position - bin_points)).astype(jnp.bfloat16)
    return jnp.dot(table_scaled, hat_weights, preferred_element_type=jnp.float32)


def stencil(lower_two, lower_one, upper_one, upper_two):
    return (lower_two - 8.0 * lower_one + 8.0 * upper_one - upper_two) / 12.0


def classify_dense(grade_field, table_scaled, bin_count):
    slice_count, row_count, col_count = grade_field.shape
    blocks = grade_field.reshape(slice_count // MZ, MZ * row_count * col_count)

    def one_block(block_vals):
        return table_lookup(block_vals, table_scaled, bin_count)

    result = lax.map(one_block, blocks)
    return jnp.moveaxis(result, 1, 0).reshape(4, slice_count, row_count, col_count)


def local(grade_field, amplitude, tf_table, brick_mask):
    depth_count = lax.axis_size("depth")
    depth_rank = lax.axis_index("depth")
    slice_count, row_count, col_count = grade_field.shape
    bin_count = tf_table.shape[1]
    opacity_scale = 4.0 / (slice_count * depth_count)
    table_scaled = (tf_table.astype(jnp.float32) / 65535.0).astype(jnp.bfloat16)
    fields = jnp.stack([grade_field, amplitude])
    padded = with_halo(fields, (("lat", 2), ("depth", 1)), 2)
    padded = jnp.pad(padded, ((0, 0), (0, 0), (0, 0), (2, 2)))
    grad_z = stencil(
        padded[:, 0:-4, 2:-2, 2:-2],
        padded[:, 1:-3, 2:-2, 2:-2],
        padded[:, 3:-1, 2:-2, 2:-2],
        padded[:, 4:, 2:-2, 2:-2],
    )
    grad_x = stencil(
        padded[:, 2:-2, 0:-4, 2:-2],
        padded[:, 2:-2, 1:-3, 2:-2],
        padded[:, 2:-2, 3:-1, 2:-2],
        padded[:, 2:-2, 4:, 2:-2],
    )
    grad_y = stencil(
        padded[:, 2:-2, 2:-2, 0:-4],
        padded[:, 2:-2, 2:-2, 1:-3],
        padded[:, 2:-2, 2:-2, 3:-1],
        padded[:, 2:-2, 2:-2, 4:],
    )
    classes = classify_dense(grade_field, table_scaled, bin_count)
    z_blocks, x_blocks, y_blocks = brick_mask.shape
    cover_mask = jnp.broadcast_to(
        brick_mask[:, None, :, None, :, None], (z_blocks, MZ, x_blocks, MX, y_blocks, MY)
    )
    cover_mask = cover_mask.reshape(slice_count, row_count, col_count).astype(jnp.float32)
    edge_weight = 1.0 - 1.0 / jnp.sqrt(
        grad_x[1] * grad_x[1] + grad_y[1] * grad_y[1] + grad_z[1] * grad_z[1] + 1.0
    )
    opacity = opacity_scale * classes[3] * edge_weight * cover_mask
    normal_len = jnp.sqrt(
        grad_x[0] * grad_x[0] + grad_y[0] * grad_y[0] + grad_z[0] * grad_z[0] + 0.25
    )
    shading = 0.3 + 0.7 * jnp.abs(grad_z[0]) / normal_len
    colors = classes[0:3] * shading[None]
    log_step = jnp.log1p(-opacity)
    running = jnp.cumsum(log_step, 0)
    before = jnp.concatenate([jnp.zeros((1, row_count, col_count), jnp.float32), running[:-1]], 0)
    color_local = jnp.sum((jnp.exp(before) * opacity)[None] * colors, 1)
    log_local = running[-1]
    piece_width = col_count // depth_count
    rgb_part = color_local.reshape(3, row_count, depth_count, piece_width)
    log_part = log_local.reshape(1, row_count, depth_count, piece_width)
    held_count = depth_count
    for level_bit in range(depth_count.bit_length() - 1):
        own_bit = depth_rank // (1 << level_bit) % 2
        keep_first = own_bit == 0
        rgb_pairs = rgb_part.reshape(3, row_count, held_count // 2, 2, piece_width)
        log_pairs = log_part.reshape(1, row_count, held_count // 2, 2, piece_width)
        rgb_keep = jnp.where(keep_first, rgb_pairs[:, :, :, 0], rgb_pairs[:, :, :, 1])
        rgb_send = jnp.where(keep_first, rgb_pairs[:, :, :, 1], rgb_pairs[:, :, :, 0])
        log_keep = jnp.where(keep_first, log_pairs[:, :, :, 0], log_pairs[:, :, :, 1])
        log_send = jnp.where(keep_first, log_pairs[:, :, :, 1], log_pairs[:, :, :, 0])
        rgb_got, log_got = partner((rgb_send, log_send), "depth", level_bit)
        rgb_front = jnp.where(keep_first, rgb_keep, rgb_got)
        rgb_back = jnp.where(keep_first, rgb_got, rgb_keep)
        log_front = jnp.where(keep_first, log_keep, log_got)
        log_back = jnp.where(keep_first, log_got, log_keep)
        rgb_part = rgb_front + jnp.exp(log_front) * rgb_back
        log_part = log_front + log_back
        held_count = held_count // 2
    rgb_final = rgb_part.reshape(3, row_count, piece_width)
    log_final = log_part.reshape(1, row_count, piece_width)
    return jnp.concatenate([rgb_final, 1.0 - jnp.exp(log_final)], 0)


def solution(mesh):
    placed = (P("depth", "lat", None), P("depth", "lat", None), P(), P("depth", "lat", None))
    return jax.shard_map(
        local, mesh=mesh, in_specs=placed, out_specs=P(None, "lat", "depth"), check_vma=False
    )
```

profile of v0, /device:TPU:0, one launch (start us, length us, event | category | flops | bytes accessed | tf_op | source)
XLA Modules:
  0.0 178.3 jit_solution(4003564876777735207)
XLA Ops:
  0.0 3.9 %pad_maximum_fusion.7 = (f32[2,16,2,2048]{3,2,1,0:T(2,128)}, f32[2,16,2,2048]{3,2,1,0:T(2,128)}) fusion(f32[1,16,16,2048]{3,2,1,0:T(8,128)} %bitcast.98, f32[1,16,16,2048]{3,2,1,0:T(8,128)} %bitcast.93), kind=kLoop, calls=%fused_computation.73 | loop fusion | flops 262144 | bytes 5242880 | tf_op jit(solution)/shard_map/slice | solution.py:16
  3.9 5.6 %collective-permute-start = (f32[2,16,2,2048]{3,2,1,0:T(2,128)}, f32[2,16,2,2048]{3,2,1,0:T(2,128)}, u32[]{:S(2)}, u32[]{:S(2)}) collective-permute-start(f32[2,16,2,2048]{3,2,1,0:T(2,128)} %get-tuple-element.42), channel_id=1, source_target_pairs={{0,4},{4,8},{8,12},{12,16},{16,20},{20,24},{24,28},{1,5},{5,9},{9,... | collective-permute-start | bytes 1572872 | tf_op jit(solution)/shard_map/ppermute | solution.py:18
  9.6 1.3 collective-permute-start.1
  10.9 0.0 copy-done
  10.9 3.2 %reshape.191 = f32[2,262144]{1,0:T(2,128)} reshape(f32[16,16,2048]{2,1,0:T(8,128)S(1)} %copy-done) | data formatting | bytes 4194304 | tf_op jit(solution)/shard_map/reshape | solution.py:41
  14.0 0.0 copy-done.6
  14.1 47.1 %while.10 = (s32[]{:T(128)}, f32[2,4,262144]{2,1,0:T(4,128)}, f32[2,262144]{1,0:T(2,128)}, bf16[4,128]{1,0:T(4,128)(2,1)S(1)}, s32[]{:T(128)}) while((s32[]{:T(128)}, f32[2,4,262144]{2,1,0:T(4,128)}, f32[2,262144]{1,0:T(2,128)}, bf16[4,128]{1,0:T(4,128)(2,1)S(1)}, s32[]{:T(128)}) %tuple.28), condition=%wide.region_1.2_spmd, body=%wide.region_0.1_spmd.sunk | while | flops 436469888 | bytes 7342657 | solution.py:46
  14.1 2.3 %dynamic-slice_multiply_fusion.2 = f32[1,262144]{1,0:T(1,128)S(1)} fusion(f32[2,262144]{1,0:T(2,128)} %get-tuple-element.92, s32[]{:T(128)} %get-tuple-element.85), kind=kLoop, calls=%fused_computation.7.clone.1 | loop fusion | flops 262144 | bytes 2097156 | tf_op jit(solution)/shard_map/while/body/eval_jaxpr/mul | solution.py:30
  16.4 21.2 %fusion.53 = f32[2,4,262144]{2,1,0:T(4,128)} fusion(f32[2,4,262144]{2,1,0:T(4,128)} %get-tuple-element.86, s32[]{:T(128)} %get-tuple-element.85, bf16[4,128]{1,0:T(4,128)(2,1)S(1)} %get-tuple-element.93, f32[128]{0:T(128)S(1)} %iota_convert_fusion.2, f32[262144]{0:T(1024)S(1)} %bitcast.103), kind=kOutput, calls=%fused_computation.1.clone.1 | convolution fusion | flops 436207616 | bytes 5244928 | tf_op jit(solution)/shard_map/while/body/eval_jaxpr/dot_general | solution.py:32
  37.6 2.3 %dynamic-slice_multiply_fusion.2 = f32[1,262144]{1,0:T(1,128)S(1)} fusion(f32[2,262144]{1,0:T(2,128)} %get-tuple-element.92, s32[]{:T(128)} %get-tuple-element.85), kind=kLoop, calls=%fused_computation.7.clone.1 | loop fusion | flops 262144 | bytes 2097156 | tf_op jit(solution)/shard_map/while/body/eval_jaxpr/mul | solution.py:30
  39.9 21.2 %fusion.53 = f32[2,4,262144]{2,1,0:T(4,128)} fusion(f32[2,4,262144]{2,1,0:T(4,128)} %get-tuple-element.86, s32[]{:T(128)} %get-tuple-element.85, bf16[4,128]{1,0:T(4,128)(2,1)S(1)} %get-tuple-element.93, f32[128]{0:T(128)S(1)} %iota_convert_fusion.2, f32[262144]{0:T(1024)S(1)} %bitcast.103), kind=kOutput, calls=%fused_computation.1.clone.1 | convolution fusion | flops 436207616 | bytes 5244928 | tf_op jit(solution)/shard_map/while/body/eval_jaxpr/dot_general | solution.py:32
  61.2 9.3 %fusion.32 = f32[2,262144]{1,0:T(2,128)S(1)} fusion(f32[4,2,262144]{2,0,1:T(4,128)} %bitcast.106), kind=kLoop, calls=%fused_computation.63 | loop fusion | flops 524288 | bytes 4194304 | tf_op jit(solution)/shard_map/mul | solution.py:87
  70.5 3.2 %mul.110 = f32[16,16,2048]{2,1,0:T(8,128)} reshape(f32[2,262144]{1,0:T(2,128)S(1)} %fusion.32) | data formatting | bytes 4194304 | tf_op jit(solution)/shard_map/mul | solution.py:87
  73.6 11.4 %copy.25 = f32[3,2,262144]{2,1,0:T(2,128)} copy(f32[3,2,262144]{2,0,1:T(4,128)} %bitcast.107) | data formatting | bytes 12582912 | tf_op jit(solution)/shard_map/slice | solution.py:92
  85.0 9.0 %slice.163 = f32[3,16,16,2048]{3,2,1,0:T(8,128)} reshape(f32[3,2,262144]{2,1,0:T(2,128)} %copy.25) | data formatting | bytes 12582912 | tf_op jit(solution)/shard_map/slice | solution.py:92
  94.0 0.0 collective-permute-done
  94.0 0.0 collective-permute-done.1
  94.0 0.0 copy-done.1
  94.0 1.6 pad_maximum_fusion.5
  95.6 0.5 copy.19
  96.1 1.5 collective-permute-start.2
  97.6 0.5 copy.20
  98.1 1.3 collective-permute-start.3
  99.4 2.4 %maximum_maximum_fusion.1 = (f32[2,16,18,2048]{3,2,1,0:T(8,128)S(1)}, f32[2,16,18,2048]{3,2,1,0:T(8,128)S(1)}) fusion(f32[1,16,16,2048]{3,2,1,0:T(8,128)S(1)} %bitcast.100, f32[1,16,16,2048]{3,2,1,0:T(8,128)S(1)} %bitcast.95, f32[2,16,2,2048]{3,2,1,0:T(2,128)} %collective-permute-done, f32[2,16,2,2048]{3,2,1,0:T(2,128)} %collective-permute-done.1), kind=kLoop, calls=%fused_computation.21 | loop fusion | flops 4718592 | bytes 14680064 | tf_op jit(solution)/shard_map/concatenate | solution.py:20
  101.8 3.0 %fusion.14 = f32[2,16,16,2048]{3,2,1,0:T(8,128)} fusion(f32[2,16,18,2048]{3,2,1,0:T(8,128)S(1)} %get-tuple-element.41, f32[2,16,18,2048]{3,2,1,0:T(8,128)S(1)} %get-tuple-element.40), kind=kLoop, calls=%fused_computation.37 | loop fusion | flops 6291456 | bytes 20971520 | tf_op jit(solution)/shard_map/div | solution.py:36
  104.8 0.0 collective-permute-done.2
  104.8 0.4 copy.21
  105.2 0.0 collective-permute-done.3
  105.2 0.4 copy.22
  105.6 7.4 %maximum_maximum_fusion = (f32[2,18,20,2048]{3,2,1,0:T(8,128)}, f32[2,18,20,2048]{3,2,1,0:T(8,128)}) fusion(f32[2,16,2,2048]{3,2,1,0:T(2,128)} %collective-permute-done.1, f32[1,16,16,2048]{3,2,1,0:T(8,128)S(1)} %bitcast.101, f32[1,16,16,2048]{3,2,1,0:T(8,128)S(1)} %bitcast.96, f32[2,16,2,2048]{3,2,1,0:T(2,128)} %collective-permute-done, ...), kind=kLoop, calls=%fused_computation.19 | loop fusion | flops 11796480 | bytes 18350080 | tf_op jit(solution)/shard_map/concatenate | solution.py:20
  113.1 11.9 %select_maximum_fusion = f32[2,20,20,2052]{3,2,1,0:T(8,128)} fusion(f32[2,2,20,2048]{3,2,1,0:T(8,128)S(1)} %copy.22, f32[2,2,20,2048]{3,2,1,0:T(8,128)S(1)} %copy.21, f32[2,16,2,2048]{3,2,1,0:T(2,128)} %collective-permute-done.1, f32[2,16,2,2048]{3,2,1,0:T(2,128)} %collective-permute-done, f32[1,16,16,2048]{3,2,1,0:T(8,128)S(1)} %bitcast.102, ...), kind=kLoop, calls=%fused_computation.13 | loop fusion | flops 22982400 | bytes 13120000 | tf_op jit(solution)/shard_map/concatenate | solution.py:20
  125.0 24.7 %fusion.8 = (f32[2,16,16,2048]{3,2,1,0:T(8,128)}, f32[2,16,16,2048]{3,2,1,0:T(8,128)}) fusion(f32[2,18,20,2048]{3,2,1,0:T(8,128)} %get-tuple-element.37, f32[2,18,20,2048]{3,2,1,0:T(8,128)} %get-tuple-element.36, f32[2,20,20,2052]{3,2,1,0:T(8,128)} %select_maximum_fusion), kind=kLoop, calls=%fused_computation.25 | loop fusion | flops 12582912 | bytes 41943040 | tf_op jit(solution)/shard_map/div | solution.py:36
  149.8 3.8 %fusion.23 = f32[16,16,2048]{2,1,0:T(8,128)S(1)} fusion(f32[2,16,16,2048]{3,2,1,0:T(8,128)} %get-tuple-element.54, f32[2,16,16,2048]{3,2,1,0:T(8,128)} %fusion.14, f32[2,16,16,2048]{3,2,1,0:T(8,128)} %get-tuple-element.53), kind=kLoop, calls=%fused_computation.49 | loop fusion | flops 5242880 | bytes 8388608 | tf_op jit(solution)/shard_map/mul | solution.py:92
  153.6 0.2 broadcast_in_dim.11
  153.8 0.0 copy-done.3
  153.8 1.3 copy-done.4
  155.1 0.6 copy-done.5
  155.7 2.7 %fusion.30 = f32[16,16,2048]{2,1,0:T(8,128)S(1)} fusion(f32[16,16,2048]{2,1,0:T(8,128)S(1)} %bitcast.108, f32[16,16,2048]{2,1,0:T(8,128)S(1)} %copy-done.5, f32[2,16,16,2048]{3,2,1,0:T(8,128)S(1)} %copy-done.4, f32[2,16,16,2048]{3,2,1,0:T(8,128)} %get-tuple-element.54, f32[2,16,16,2048]{3,2,1,0:T(8,128)S(1)} %copy-done.3), kind=kLoop, calls=%fused_computation.58 | loop fusion | flops 4718592 | bytes 12582912 | tf_op jit(solution)/shard_map/mul | solution.py:87
  158.4 0.0 slice-start
  158.4 1.1 fusion.33
  159.5 0.0 slice-start.1
  159.5 0.2 slice.192
  159.8 0.4 exponential_multiply_fusion
  160.2 0.3 slice-done
  160.6 0.9 slice-done.1
  161.5 1.3 multiply_reduce_fusion
  162.8 0.3 reshape_reshape.3
  163.1 0.1 reshape_reshape_squeeze.3
  163.2 0.1 fusion.48
  163.4 6.9 %collective-permute-start.5 = (f32[1,16,2,512]{3,1,2,0:T(8,128)S(1)}, f32[1,16,2,512]{3,1,2,0:T(8,128)S(1)}, u32[]{:S(2)}, u32[]{:S(2)}) collective-permute-start(f32[1,16,2,512]{3,1,2,0:T(8,128)S(1)} %select_bitcast_fusion), channel_id=1, source_target_pairs={{0,1},{1,0},{2,3},{3,2},{4,5},{5,4},{6,7},{7,6},{8,9},{9,8},{10,11... | collective-permute-start | bytes 196616 | tf_op jit(solution)/shard_map/ppermute | solution.py:25
  170.2 0.3 fusion.47
  170.6 0.1 copy.65
  170.7 0.1 collective-permute-start.4
  170.8 0.4 collective-permute-done.5
  171.2 0.1 copy.32
  171.2 0.1 collective-permute-start.7
  171.4 0.8 collective-permute-done.4
  172.2 0.2 add_bitcast_fusion
  172.4 0.1 fusion.40
  172.5 1.2 collective-permute-start.6
  173.7 1.5 collective-permute-done.7
  175.2 2.2 %collective-permute-done.6 = f32[3,16,1,512]{3,2,1,0:T(1,128)S(1)} collective-permute-done((f32[3,16,1,512]{3,2,1,0:T(1,128)S(1)}, f32[3,16,1,512]{3,2,1,0:T(1,128)S(1)}, u32[]{:S(2)}, u32[]{:S(2)}) %collective-permute-start.6) | collective-permute-done | bytes 98336 | tf_op jit(solution)/shard_map/ppermute | solution.py:25
  177.4 0.2 fusion.37
  177.6 0.7 pad_maximum_fusion.8
  (22 shorter events, 0.1 us)
Async XLA Ops:
  0.0 10.9 %copy-start = (f32[16,16,2048]{2,1,0:T(8,128)S(1)}, f32[16,16,2048]{2,1,0:T(8,128)}, u32[]{:S(2)}) copy-start(f32[16,16,2048]{2,1,0:T(8,128)} %param.6) | copy-start | bytes 6291460
  0.0 14.0 %copy-start.6 = (s32[4,128]{1,0:T(4,128)S(1)}, s32[4,128]{1,0:T(4,128)}, u32[]{:S(2)}) copy-start(s32[4,128]{1,0:T(4,128)} %param.8) | copy-start | bytes 6148
  3.9 90.1 %collective-permute-start = (f32[2,16,2,2048]{3,2,1,0:T(2,128)}, f32[2,16,2,2048]{3,2,1,0:T(2,128)}, u32[]{:S(2)}, u32[]{:S(2)}) collective-permute-start(f32[2,16,2,2048]{3,2,1,0:T(2,128)} %get-tuple-element.42), channel_id=1, source_target_pairs={{0,4},{4,8},{8,12},{12,16},{16,20},{20,24},{24,28},{1,5},{5,9},{9,... | collective-permute-start | bytes 1572872 | tf_op jit(solution)/shard_map/ppermute | solution.py:18
  9.6 84.5 %collective-permute-start.1 = (f32[2,16,2,2048]{3,2,1,0:T(2,128)}, f32[2,16,2,2048]{3,2,1,0:T(2,128)}, u32[]{:S(2)}, u32[]{:S(2)}) collective-permute-start(f32[2,16,2,2048]{3,2,1,0:T(2,128)} %get-tuple-element.43), channel_id=1, source_target_pairs={{4,0},{8,4},{12,8},{16,12},{20,16},{24,20},{28,24},{5,1},{9,5},{13... | collective-permute-start | bytes 1572872 | tf_op jit(solution)/shard_map/ppermute | solution.py:19
  61.2 12.5 %copy-start.7 = (s32[2,2,8]{2,1,0:T(2,128)S(1)}, s32[2,2,8]{2,1,0:T(2,128)}, u32[]{:S(2)}) copy-start(s32[2,2,8]{2,1,0:T(2,128)} %param.9) | copy-start | bytes 388
  85.0 9.0 %copy-start.1 = (f32[16,16,2048]{2,1,0:T(8,128)S(1)}, f32[16,16,2048]{2,1,0:T(8,128)}, u32[]{:S(2)}) copy-start(f32[16,16,2048]{2,1,0:T(8,128)} %param.6) | copy-start | bytes 6291460
  94.0 5.4 %copy-start.2 = (f32[16,16,2048]{2,1,0:T(8,128)S(1)}, f32[16,16,2048]{2,1,0:T(8,128)}, u32[]{:S(2)}) copy-start(f32[16,16,2048]{2,1,0:T(8,128)} %param.7) | copy-start | bytes 6291460
  96.1 8.7 %collective-permute-start.2 = (f32[2,2,20,2048]{3,1,2,0:T(2,128)S(1)}, f32[2,2,20,2048]{3,1,2,0:T(2,128)S(1)}, u32[]{:S(2)}, u32[]{:S(2)}) collective-permute-start(f32[2,2,20,2048]{3,1,2,0:T(2,128)S(1)} %copy.19), channel_id=1, source_target_pairs={{0,1},{1,2},{2,3},{4,5},{5,6},{6,7},{8,9},{9,10},{10,11},{12,13},{... | collective-permute-start | bytes 1966088 | tf_op jit(solution)/shard_map/ppermute | solution.py:18
  98.1 7.1 %collective-permute-start.3 = (f32[2,2,20,2048]{3,1,2,0:T(2,128)S(1)}, f32[2,2,20,2048]{3,1,2,0:T(2,128)S(1)}, u32[]{:S(2)}, u32[]{:S(2)}) collective-permute-start(f32[2,2,20,2048]{3,1,2,0:T(2,128)S(1)} %copy.20), channel_id=1, source_target_pairs={{1,0},{2,1},{3,2},{5,4},{6,5},{7,6},{9,8},{10,9},{11,10},{13,12},{... | collective-permute-start | bytes 1966088 | tf_op jit(solution)/shard_map/ppermute | solution.py:19
  149.8 4.1 %copy-start.3 = (f32[2,16,16,2048]{3,2,1,0:T(8,128)S(1)}, f32[2,16,16,2048]{3,2,1,0:T(8,128)}, u32[]{:S(2)}) copy-start(f32[2,16,16,2048]{3,2,1,0:T(8,128)} %fusion.14) | copy-start | bytes 12582916
  149.8 5.3 %copy-start.4 = (f32[2,16,16,2048]{3,2,1,0:T(8,128)S(1)}, f32[2,16,16,2048]{3,2,1,0:T(8,128)}, u32[]{:S(2)}) copy-start(f32[2,16,16,2048]{3,2,1,0:T(8,128)} %get-tuple-element.53) | copy-start | bytes 12582916
  149.8 5.9 %copy-start.5 = (f32[16,16,2048]{2,1,0:T(8,128)S(1)}, f32[16,16,2048]{2,1,0:T(8,128)}, u32[]{:S(2)}) copy-start(f32[16,16,2048]{2,1,0:T(8,128)} %mul.110) | copy-start | bytes 6291460
  158.4 2.2 %slice-start = ((s8[6291456]{0:T(1024)(128)(4,1)}), s8[4194304]{0:T(1024)(128)(4,1)S(1)}, s32[]{:S(2)}) async-start(s8[6291456]{0:T(1024)(128)(4,1)} %bitcast.104), calls=%async_computation | async-start | bytes 8388608
  159.5 1.9 %slice-start.1 = ((s8[6291456]{0:T(1024)(128)(4,1)}), s8[2097152]{0:T(1024)(128)(4,1)S(1)}, s32[]{:S(2)}) async-start(s8[6291456]{0:T(1024)(128)(4,1)} %bitcast.104), calls=%async_computation.1 | async-start | bytes 4194304
  163.4 7.8 %collective-permute-start.5 = (f32[1,16,2,512]{3,1,2,0:T(8,128)S(1)}, f32[1,16,2,512]{3,1,2,0:T(8,128)S(1)}, u32[]{:S(2)}, u32[]{:S(2)}) collective-permute-start(f32[1,16,2,512]{3,1,2,0:T(8,128)S(1)} %select_bitcast_fusion), channel_id=1, source_target_pairs={{0,1},{1,0},{2,3},{3,2},{4,5},{5,4},{6,7},{7,6},{8,9},{9,8},{10,11... | collective-permute-start | bytes 196616 | tf_op jit(solution)/shard_map/ppermute | solution.py:25
  170.7 1.5 collective-permute-start.4
  171.2 4.0 %collective-permute-start.7 = (f32[1,16,1,512]{3,1,2,0:T(8,128)S(1)}, f32[1,16,1,512]{3,1,2,0:T(8,128)S(1)}, u32[]{:S(2)}, u32[]{:S(2)}) collective-permute-start(f32[1,16,1,512]{3,1,2,0:T(8,128)S(1)} %select_bitcast_fusion.1), channel_id=1, source_target_pairs={{0,2},{1,3},{2,0},{3,1},{4,6},{5,7},{6,4},{7,5},{8,10},{9,11},{10,... | collective-permute-start | bytes 98312 | tf_op jit(solution)/shard_map/ppermute | solution.py:25
  172.5 4.9 %collective-permute-start.6 = (f32[3,16,1,512]{3,2,1,0:T(1,128)S(1)}, f32[3,16,1,512]{3,2,1,0:T(1,128)S(1)}, u32[]{:S(2)}, u32[]{:S(2)}) collective-permute-start(f32[3,16,1,512]{3,2,1,0:T(1,128)S(1)} %fusion.40), channel_id=1, source_target_pairs={{0,2},{1,3},{2,0},{3,1},{4,6},{5,7},{6,4},{7,5},{8,10},{9,11},{10,... | collective-permute-start | bytes 294920 | tf_op jit(solution)/shard_map/ppermute | solution.py:25
where the time goes:
time: 179 us; the launch traced here: 178 us
  other arithmetic  79.9 us (45%)
  matrix products  42.4 us (24%)
  local copies, waits for them, and re-layouts  32.8 us (18%)
  starting transfers between devices  18 us (10%)
  waiting for transfers between devices  4.85 us (3%)
    dot_general x2, matrix products, table_lookup(): jnp.dot(table_scaled, hat_weights, preferred_element_type=jnp.float32)  42.4 us
    div x2, other arithmetic, stencil(): return (lower_two - 8.0 * lower_one + 8.0 * upper_one - upper_two) / 12.0  27.8 us
    concatenate x3, other arithmetic, with_halo(): shard = jnp.concatenate([before, shard, after], axis=dim)  21.7 us
    slice x2, local copies, waits for them, and re-layouts, local(): colors = classes[0:3] * shading[None]  20.4 us
    mul x2, other arithmetic, local(): opacity = opacity_scale * classes[3] * edge_weight * cover_mask  12 us
    ppermute x4, starting transfers between devices, partner(): lax.ppermute(shard, axis, [(i, i ^ 1 << distance) for i in range(lax.axis...  8.3 us
    ppermute x2, starting transfers between devices, with_halo(): before = lax.ppermute(last, axis, up)  7.15 us
    slice x2, other arithmetic, with_halo(): last = lax.slice_in_dim(shard, length - width, length, axis=dim)  5.46 us
  transfers between devices with their start and end apart: 8, of which 4 were waited for; matrix products, arithmetic and copies ran while one was open for 51% of the time, Pallas kernels for 0%

commit v1 on v0

v1 whole, which is shorter than its diff:
```python
import functools

import jax
import jax.numpy as jnp
from jax import lax
from jax.experimental import pallas as pl
from jax.experimental.pallas import tpu as pltpu
from jax.sharding import PartitionSpec as P

MZ = 8
MX = 8
MY = 256
LANES = 128
SUB = 8
TOP = 8


def pack_kernel(grade_ref, amp_ref, up_ref, down_ref, front_ref, back_ref):
    slices, rows = grade_ref.shape[:2]
    for f, ref in enumerate((grade_ref, amp_ref)):
        for z in range(slices):
            at = 2 * (z % 4)
            up_ref[f, z // 4, at:at + 2, :] = ref[z, rows - 2:rows, :]
            down_ref[f, z // 4, at:at + 2, :] = ref[z, 0:2, :]
        front_ref[f] = ref[slices - 2:slices]
        back_ref[f] = ref[0:2]


def round_weight(w):
    return w.astype(jnp.bfloat16).astype(jnp.float32)


def march_kernel(scale, pieces, mask_ref, rank_ref, grade_hbm, amp_hbm, above_ref, below_ref, front_hbm,
                 back_hbm, table_ref, *rest):
    outs, (grid_g, grid_a, acc_ref, low_ref, high_ref, sems) = rest[:pieces], rest[pieces:]
    slices, rows, cols = grade_hbm.shape
    strips = cols // LANES
    copies = []
    for f, (src, grid) in enumerate(((grade_hbm, grid_g), (amp_hbm, grid_a))):
        for s in range(strips):
            lanes = pl.ds(s * LANES, LANES)
            body = pl.ds(TOP, rows)
            trio = (
                (src.at[:, :, lanes], grid.at[pl.ds(2, slices), s + 1, body, :]),
                (front_hbm.at[f, :, :, lanes], grid.at[pl.ds(0, 2), s + 1, body, :]),
                (back_hbm.at[f, :, :, lanes], grid.at[pl.ds(slices + 2, 2), s + 1, body, :]),
            )
            for k, (here, there) in enumerate(trio):
                copies.append(pltpu.make_async_copy(here, there, sems.at[f, s, k]))
    for copy in copies:
        copy.start()
    for f, grid in enumerate((grid_g, grid_a)):
        zero = jnp.zeros((rows, LANES), jnp.float32)
        for z in range(slices):
            grid[z + 2, 0, TOP:TOP + rows, :] = zero
            grid[z + 2, strips + 1, TOP:TOP + rows, :] = zero
            at = 2 * (z % 4)
            for s in range(strips):
                lanes = slice(s * LANES, (s + 1) * LANES)
                grid[z + 2, s + 1, TOP - 2:TOP, :] = above_ref[f, z // 4, at:at + 2, lanes]
                grid[z + 2, s + 1, TOP + rows:TOP + rows + 2, :] = below_ref[f, z // 4, at:at + 2, lanes]
    bins = table_ref.shape[1]
    table = (table_ref[...].astype(jnp.float32) / 65535.0).astype(jnp.bfloat16).astype(jnp.float32)
    row = lax.broadcasted_iota(jnp.int32, table.shape, 0)
    table = jnp.where(row == 3, table * scale, table)
    column = lax.broadcasted_iota(jnp.int32, table.shape, 1)
    following = jnp.where(column == bins - 1, 0.0, pltpu.roll(table, bins - 1, 1))
    for c in range(4):
        low_ref[c] = jnp.broadcast_to(table[c:c + 1, :], (SUB, bins))
        high_ref[c] = jnp.broadcast_to(following[c:c + 1, :], (SUB, bins))
    for copy in copies:
        copy.wait()
    lane = lax.broadcasted_iota(jnp.int32, (SUB, LANES), 1)
    per_block = MY // LANES
    piece_blocks = cols // pieces // MY

    def gather(ref, c, index):
        return jnp.take_along_axis(ref[c], index, axis=1)

    def stencil(m2, m1, p1, p2):
        return (m2 - p2) + 8.0 * (p1 - m1)

    def derivs(grid, z, s, r0):
        mid = grid[z, s, r0:r0 + SUB, :]
        left = grid[z, s - 1, r0:r0 + SUB, :]
        right = grid[z, s + 1, r0:r0 + SUB, :]
        dy = stencil(
            pltpu.roll(jnp.where(lane >= LANES - 2, left, mid), 2, 1),
            pltpu.roll(jnp.where(lane >= LANES - 1, left, mid), 1, 1),
            pltpu.roll(jnp.where(lane < 1, right, mid), LANES - 1, 1),
            pltpu.roll(jnp.where(lane < 2, right, mid), LANES - 2, 1),
        )
        dz = stencil(*(grid[z + k, s, r0:r0 + SUB, :] for k in (-2, -1, 1, 2)))
        dx = stencil(*(grid[z, s, r0 + k:r0 + k + SUB, :] for k in (-2, -1, 1, 2)))
        return mid, dx * dx + dy * dy + dz * dz, dz

    def block(cb, carry):
        owner = lax.bitwise_xor(cb // piece_blocks, rank_ref[0])
        lanes = pl.ds(pl.multiple_of(lax.rem(cb, piece_blocks) * MY, MY), MY)
        for rt in range(rows // MX):
            r0 = TOP + rt * MX
            for j in range(per_block):
                for c in range(3):
                    acc_ref[j, c] = jnp.zeros((SUB, LANES), jnp.float32)
                acc_ref[j, 3] = jnp.ones((SUB, LANES), jnp.float32)
            for zb in range(slices // MZ):
                @pl.when(mask_ref[zb, rt, cb] != 0)
                def _():
                    for j in range(per_block):
                        s = cb * per_block + j + 1
                        red, green, blue, trans = (acc_ref[j, c] for c in range(4))
                        for zi in range(MZ):
                            z = 2 + zb * MZ + zi
                            grade, g_sq, gz = derivs(grid_g, z, s, r0)
                            _, a_sq, _ = derivs(grid_a, z, s, r0)
                            edge = 1.0 - 12.0 * lax.rsqrt(a_sq + 144.0)
                            shade = 0.3 + 0.7 * (jnp.abs(gz) * lax.rsqrt(g_sq + 36.0))
                            position = grade * (bins - 1.0)
                            index = jnp.minimum(position.astype(jnp.int32), bins - 1)
                            w_low = 1.0 - (position - index.astype(jnp.float32))
                            w_high = round_weight(1.0 - w_low)
                            w_low = round_weight(w_low)
                            cls = [
                                w_low * gather(low_ref, c, index) + w_high * gather(high_ref, c, index)
                                for c in range(4)
                            ]
                            weight = trans * (cls[3] * edge)
                            trans = trans - weight
                            weight = weight * shade
                            red = red + weight * cls[0]
                            green = green + weight * cls[1]
                            blue = blue + weight * cls[2]
                        for c, value in enumerate((red, green, blue, trans)):
                            acc_ref[j, c] = value
            for k in range(pieces):
                @pl.when(owner == k)
                def _():
                    for c in range(4):
                        value = jnp.concatenate([acc_ref[j, c] for j in range(per_block)], axis=1)
                        outs[k][c, rt * SUB:(rt + 1) * SUB, lanes] = value
        return carry

    lax.fori_loop(0, cols // MY, block, 0)


def shift(x, axis, step):
    size = lax.axis_size(axis)
    return lax.ppermute(x, axis, [(i, i + step) for i in range(size) if 0 <= i + step < size])


def local(grade_field, amplitude, tf_table, brick_mask):
    slices, rows, cols = grade_field.shape
    pieces = lax.axis_size("depth")
    rank = lax.axis_index("depth")
    scale = 4.0 / (slices * pieces)
    strips = cols // LANES
    f32 = jnp.float32
    vmem = pl.BlockSpec(memory_space=pltpu.VMEM)
    smem = pl.BlockSpec(memory_space=pltpu.SMEM)
    hbm = pl.BlockSpec(memory_space=pl.ANY)
    big = pltpu.CompilerParams(vmem_limit_bytes=48 << 20)
    lat_halo = jax.ShapeDtypeStruct((2, slices // 4, SUB, cols), f32)
    depth_halo = jax.ShapeDtypeStruct((2, 2, rows, cols), f32)
    up, down, front, back = pl.pallas_call(
        pack_kernel,
        out_shape=(lat_halo, lat_halo, depth_halo, depth_halo),
        in_specs=[vmem, vmem],
        out_specs=[vmem] * 4,
        compiler_params=big,
        name="pack",
    )(grade_field, amplitude)
    above = shift(up, "lat", 1)
    below = shift(down, "lat", -1)
    front = shift(front, "depth", 1)
    back = shift(back, "depth", -1)
    piece = jax.ShapeDtypeStruct((4, rows, cols // pieces), f32)
    grid = pltpu.VMEM((slices + 4, strips + 2, TOP + rows + SUB, LANES), f32)
    parts = pl.pallas_call(
        functools.partial(march_kernel, scale, pieces),
        out_shape=(piece,) * pieces,
        in_specs=[smem, smem, hbm, hbm, vmem, vmem, hbm, hbm, vmem],
        out_specs=[vmem] * pieces,
        scratch_shapes=[
            grid,
            grid,
            pltpu.VMEM((MY // LANES, 4, SUB, LANES), f32),
            pltpu.VMEM((4, SUB, tf_table.shape[1]), f32),
            pltpu.VMEM((4, SUB, tf_table.shape[1]), f32),
            pltpu.SemaphoreType.DMA((2, strips, 3)),
        ],
        compiler_params=big,
        name="march",
    )(brick_mask, rank.reshape(1).astype(jnp.int32), grade_field, amplitude, above, below, front, back, tf_table)
    held = [parts[0]] + [
        lax.ppermute(parts[k], "depth", [(i, i ^ k) for i in range(pieces)]) for k in range(1, pieces)
    ]
    level = 0
    while len(held) > 1:
        first = (rank >> level) % 2 == 0
        merged = []
        for mine, other in zip(held[0::2], held[1::2]):
            ahead = jnp.where(first, mine, other)
            behind = jnp.where(first, other, mine)
            rgb = ahead[0:3] + ahead[3:4] * behind[0:3]
            merged.append(jnp.concatenate([rgb, ahead[3:4] * behind[3:4]], 0))
        held = merged
        level += 1
    return jnp.concatenate([held[0][0:3], 1.0 - held[0][3:4]], 0)


def solution(mesh):
    placed = (P("depth", "lat", None), P("depth", "lat", None), P(), P("depth", "lat", None))
    return jax.shard_map(
        local, mesh=mesh, in_specs=placed, out_specs=P(None, "lat", "depth"), check_vma=False
    )
```

time: 179 us -> 55.6 us (0.31)
  the two profiles are of different devices: /device:TPU:0 before, /device:TPU:25 now
where the time goes in v1:
time: 55.6 us; the launch traced here: 54.8 us
  waiting for transfers between devices  21.4 us (38%)
  Pallas kernels  16.4 us (29%)
  starting transfers between devices  14.5 us (26%)
  local copies, waits for them, and re-layouts  1.6 us (3%)
  other arithmetic  0.81 us (1%)
    ppermute x4, waiting for transfers between devices, shift(): lax.ppermute(x, axis, [(i, i + step) for i in range(size) if 0 <= i + ste...  15.7 us
    pallas_call x1, Pallas kernels, local(): pl.pallas_call(functools.partial(march_kernel, scale, pieces), out_shape=...  12.9 us
    ppermute x4, starting transfers between devices, shift(): lax.ppermute(x, axis, [(i, i + step) for i in range(size) if 0 <= i + ste...  12.3 us
    ppermute x3, waiting for transfers between devices, local(): lax.ppermute(parts[k], 'depth', [(i, i ^ k) for i in range(pieces)])  5.69 us
    pallas_call x1, Pallas kernels, local(): pl.pallas_call(pack_kernel, out_shape=(lat_halo, lat_halo, depth_halo, de...  3.52 us
    ppermute x3, starting transfers between devices, local(): lax.ppermute(parts[k], 'depth', [(i, i ^ k) for i in range(pieces)])  2.17 us
    unnamed x8, local copies, waits for them, and re-layouts  1.6 us
  transfers between devices with their start and end apart: 7, of which 4 were waited for; matrix products, arithmetic and copies ran while one was open for 0% of the time, Pallas kernels for 0%

profile of v1, /device:TPU:25, one launch (start us, length us, event | category | flops | bytes accessed | tf_op | source)
XLA Modules:
  0.0 54.8 jit_solution(5309674419834473615)
XLA Ops:
  0.0 0.0 copy-start
  0.0 1.6 %copy-done = f32[16,16,2048]{2,1,0:T(8,128)S(1)} copy-done((f32[16,16,2048]{2,1,0:T(8,128)S(1)}, f32[16,16,2048]{2,1,0:T(8,128)}, u32[]{:S(2)}) %copy-start) | copy-done | bytes 2097176
  1.6 0.0 copy-start.1
  1.6 0.0 copy-start.2
  1.6 0.0 copy-start.3
  1.6 3.5 %pack.1 = (f32[2,4,8,2048]{3,2,1,0:T(8,128)}, f32[2,4,8,2048]{3,2,1,0:T(8,128)}, f32[2,2,16,2048]{3,2,1,0:T(8,128)}, f32[2,2,16,2048]{3,2,1,0:T(8,128)}) custom-call(f32[16,16,2048]{2,1,0:T(8,128)S(1)} %copy-done, f32[16,16,2048]{2,1,0:T(8,128)} %amp_hbm.1), custom_call_target="tpu_custom_call" | custom-call | tf_op jit(solution)/shard_map/pack/pallas_call | solution.py:164
  5.1 3.1 %collective-permute-start = (f32[2,4,8,2048]{3,2,1,0:T(8,128)}, f32[2,4,8,2048]{3,2,1,0:T(8,128)S(1)}, u32[]{:S(2)}, u32[]{:S(2)}) collective-permute-start(f32[2,4,8,2048]{3,2,1,0:T(8,128)} %get-tuple-element.13), channel_id=1, source_target_pairs={{0,4},{4,8},{8,12},{12,16},{16,20},{20,24},{24,28},{1,5},{5,9},{9,... | collective-permute-start | bytes 1572872 | tf_op jit(solution)/shard_map/ppermute | solution.py:148
  8.3 3.0 %collective-permute-start.1 = (f32[2,4,8,2048]{3,2,1,0:T(8,128)}, f32[2,4,8,2048]{3,2,1,0:T(8,128)S(1)}, u32[]{:S(2)}, u32[]{:S(2)}) collective-permute-start(f32[2,4,8,2048]{3,2,1,0:T(8,128)} %get-tuple-element.14), channel_id=1, source_target_pairs={{4,0},{8,4},{12,8},{16,12},{20,16},{24,20},{28,24},{5,1},{9,5},{13... | collective-permute-start | bytes 1572872 | tf_op jit(solution)/shard_map/ppermute | solution.py:148
  11.3 4.2 %collective-permute-start.2 = (f32[2,2,16,2048]{3,2,1,0:T(8,128)}, f32[2,2,16,2048]{3,2,1,0:T(8,128)}, u32[]{:S(2)}, u32[]{:S(2)}) collective-permute-start(f32[2,2,16,2048]{3,2,1,0:T(8,128)} %get-tuple-element.15), channel_id=1, source_target_pairs={{0,1},{1,2},{2,3},{4,5},{5,6},{6,7},{8,9},{9,10},{10,11},{12,13},{... | collective-permute-start | bytes 1572872 | tf_op jit(solution)/shard_map/ppermute | solution.py:148
  15.6 1.9 %collective-permute-start.3 = (f32[2,2,16,2048]{3,2,1,0:T(8,128)}, f32[2,2,16,2048]{3,2,1,0:T(8,128)}, u32[]{:S(2)}, u32[]{:S(2)}) collective-permute-start(f32[2,2,16,2048]{3,2,1,0:T(8,128)} %get-tuple-element.16), channel_id=1, source_target_pairs={{1,0},{2,1},{3,2},{5,4},{6,5},{7,6},{9,8},{10,9},{11,10},{13,12},{... | collective-permute-start | bytes 1572872 | tf_op jit(solution)/shard_map/ppermute | solution.py:148
  17.5 3.5 %collective-permute-done.above_ref = f32[2,4,8,2048]{3,2,1,0:T(8,128)S(1)} collective-permute-done((f32[2,4,8,2048]{3,2,1,0:T(8,128)}, f32[2,4,8,2048]{3,2,1,0:T(8,128)S(1)}, u32[]{:S(2)}, u32[]{:S(2)}) %collective-permute-start) | collective-permute-done | bytes 524320 | tf_op jit(solution)/shard_map/ppermute | solution.py:148
  20.9 12.2 %collective-permute-done.1.below_ref = f32[2,4,8,2048]{3,2,1,0:T(8,128)S(1)} collective-permute-done((f32[2,4,8,2048]{3,2,1,0:T(8,128)}, f32[2,4,8,2048]{3,2,1,0:T(8,128)S(1)}, u32[]{:S(2)}, u32[]{:S(2)}) %collective-permute-start.1) | collective-permute-done | bytes 524320 | tf_op jit(solution)/shard_map/ppermute | solution.py:148
  33.2 0.0 collective-permute-done.2.front_hbm
  33.2 0.0 collective-permute-done.3.back_hbm
  33.2 0.0 copy-done.1
  33.2 0.0 copy-done.2
  33.2 0.0 copy-done.3
  33.2 12.9 %march.1 = (f32[4,16,512]{2,1,0:T(8,128)S(1)}, f32[4,16,512]{2,1,0:T(8,128)S(1)}, f32[4,16,512]{2,1,0:T(8,128)}, f32[4,16,512]{2,1,0:T(8,128)S(1)}) custom-call(s32[2,2,8]{2,1,0:T(2,128)S(1)} %copy-done.2, s32[1]{0:T(128)} %bitcast.rank_ref, f32[16,16,2048]{2,1,0:T(8,128)S(1)} %copy-done.1, f32[16,16,2048]{2,1,0:T(8,128)} %amp_hbm.1, ...), custom_call_target="tpu_custom_call" | custom-call | tf_op jit(solution)/shard_map/march/pallas_call | solution.py:178
  46.1 1.7 %collective-permute-start.5 = (f32[4,16,512]{2,1,0:T(8,128)}, f32[4,16,512]{2,1,0:T(8,128)S(1)}, u32[]{:S(2)}, u32[]{:S(2)}) collective-permute-start(f32[4,16,512]{2,1,0:T(8,128)} %get-tuple-element.19), channel_id=1, source_target_pairs={{0,2},{1,3},{2,0},{3,1},{4,6},{5,7},{6,4},{7,5},{8,10},{9,11},{10,... | collective-permute-start | bytes 393224 | tf_op jit(solution)/shard_map/ppermute | solution.py:195
  47.8 0.0 collective-permute-start.6
  47.8 0.5 collective-permute-start.4
  48.3 3.2 %collective-permute-done.5 = f32[4,16,512]{2,1,0:T(8,128)S(1)} collective-permute-done((f32[4,16,512]{2,1,0:T(8,128)}, f32[4,16,512]{2,1,0:T(8,128)S(1)}, u32[]{:S(2)}, u32[]{:S(2)}) %collective-permute-start.5) | collective-permute-done | bytes 131104 | tf_op jit(solution)/shard_map/ppermute | solution.py:195
  51.4 2.5 %collective-permute-done.6 = f32[4,16,512]{2,1,0:T(8,128)S(1)} collective-permute-done((f32[4,16,512]{2,1,0:T(8,128)S(1)}, f32[4,16,512]{2,1,0:T(8,128)S(1)}, u32[]{:S(2)}, u32[]{:S(2)}) %collective-permute-start.6) | collective-permute-done | bytes 131104 | tf_op jit(solution)/shard_map/ppermute | solution.py:195
  54.0 0.0 collective-permute-done.4
  54.2 0.7 %pad_maximum_fusion.2 = f32[4,16,512]{2,1,0:T(8,128)} fusion(f32[1,16,512]{2,1,0:T(8,128)S(1)} %get-tuple-element.28, f32[3,16,512]{2,1,0:T(8,128)S(1)} %fusion.2), kind=kLoop, calls=%fused_computation.2 | loop fusion | flops 32768 | bytes 262144 | tf_op jit(solution)/shard_map/concatenate | solution.py:208
  (8 shorter events, 0.1 us)
Async XLA Ops:
  0.0 1.6 %copy-start = (f32[16,16,2048]{2,1,0:T(8,128)S(1)}, f32[16,16,2048]{2,1,0:T(8,128)}, u32[]{:S(2)}) copy-start(f32[16,16,2048]{2,1,0:T(8,128)} %grade_hbm.1) | copy-start | bytes 6291460
  1.6 31.6 %copy-start.1 = (f32[16,16,2048]{2,1,0:T(8,128)S(1)}, f32[16,16,2048]{2,1,0:T(8,128)}, u32[]{:S(2)}) copy-start(f32[16,16,2048]{2,1,0:T(8,128)} %grade_hbm.1) | copy-start | bytes 6291460
  1.6 31.6 %copy-start.2 = (s32[2,2,8]{2,1,0:T(2,128)S(1)}, s32[2,2,8]{2,1,0:T(2,128)}, u32[]{:S(2)}) copy-start(s32[2,2,8]{2,1,0:T(2,128)} %mask_ref.1) | copy-start | bytes 388
  1.6 31.6 %copy-start.3 = (s32[4,128]{1,0:T(4,128)S(1)}, s32[4,128]{1,0:T(4,128)}, u32[]{:S(2)}) copy-start(s32[4,128]{1,0:T(4,128)} %table_ref.1) | copy-start | bytes 6148
  5.1 15.8 %collective-permute-start = (f32[2,4,8,2048]{3,2,1,0:T(8,128)}, f32[2,4,8,2048]{3,2,1,0:T(8,128)S(1)}, u32[]{:S(2)}, u32[]{:S(2)}) collective-permute-start(f32[2,4,8,2048]{3,2,1,0:T(8,128)} %get-tuple-element.13), channel_id=1, source_target_pairs={{0,4},{4,8},{8,12},{12,16},{16,20},{20,24},{24,28},{1,5},{5,9},{9,... | collective-permute-start | bytes 1572872 | tf_op jit(solution)/shard_map/ppermute | solution.py:148
  8.3 24.9 %collective-permute-start.1 = (f32[2,4,8,2048]{3,2,1,0:T(8,128)}, f32[2,4,8,2048]{3,2,1,0:T(8,128)S(1)}, u32[]{:S(2)}, u32[]{:S(2)}) collective-permute-start(f32[2,4,8,2048]{3,2,1,0:T(8,128)} %get-tuple-element.14), channel_id=1, source_target_pairs={{4,0},{8,4},{12,8},{16,12},{20,16},{24,20},{28,24},{5,1},{9,5},{13... | collective-permute-start | bytes 1572872 | tf_op jit(solution)/shard_map/ppermute | solution.py:148
  11.3 21.9 %collective-permute-start.2 = (f32[2,2,16,2048]{3,2,1,0:T(8,128)}, f32[2,2,16,2048]{3,2,1,0:T(8,128)}, u32[]{:S(2)}, u32[]{:S(2)}) collective-permute-start(f32[2,2,16,2048]{3,2,1,0:T(8,128)} %get-tuple-element.15), channel_id=1, source_target_pairs={{0,1},{1,2},{2,3},{4,5},{5,6},{6,7},{8,9},{9,10},{10,11},{12,13},{... | collective-permute-start | bytes 1572872 | tf_op jit(solution)/shard_map/ppermute | solution.py:148
  15.6 17.6 %collective-permute-start.3 = (f32[2,2,16,2048]{3,2,1,0:T(8,128)}, f32[2,2,16,2048]{3,2,1,0:T(8,128)}, u32[]{:S(2)}, u32[]{:S(2)}) collective-permute-start(f32[2,2,16,2048]{3,2,1,0:T(8,128)} %get-tuple-element.16), channel_id=1, source_target_pairs={{1,0},{2,1},{3,2},{5,4},{6,5},{7,6},{9,8},{10,9},{11,10},{13,12},{... | collective-permute-start | bytes 1572872 | tf_op jit(solution)/shard_map/ppermute | solution.py:148
  46.1 5.3 %collective-permute-start.5 = (f32[4,16,512]{2,1,0:T(8,128)}, f32[4,16,512]{2,1,0:T(8,128)S(1)}, u32[]{:S(2)}, u32[]{:S(2)}) collective-permute-start(f32[4,16,512]{2,1,0:T(8,128)} %get-tuple-element.19), channel_id=1, source_target_pairs={{0,2},{1,3},{2,0},{3,1},{4,6},{5,7},{6,4},{7,5},{8,10},{9,11},{10,... | collective-permute-start | bytes 393224 | tf_op jit(solution)/shard_map/ppermute | solution.py:195
  47.8 6.2 %collective-permute-start.6 = (f32[4,16,512]{2,1,0:T(8,128)S(1)}, f32[4,16,512]{2,1,0:T(8,128)S(1)}, u32[]{:S(2)}, u32[]{:S(2)}) collective-permute-start(f32[4,16,512]{2,1,0:T(8,128)S(1)} %get-tuple-element.20), channel_id=1, source_target_pairs={{0,3},{1,2},{2,1},{3,0},{4,7},{5,6},{6,5},{7,4},{8,11},{9,10},{10,... | collective-permute-start | bytes 393224 | tf_op jit(solution)/shard_map/ppermute | solution.py:195
  47.8 6.2 %collective-permute-start.4 = (f32[4,16,512]{2,1,0:T(8,128)S(1)}, f32[4,16,512]{2,1,0:T(8,128)S(1)}, u32[]{:S(2)}, u32[]{:S(2)}) collective-permute-start(f32[4,16,512]{2,1,0:T(8,128)S(1)} %get-tuple-element.18), channel_id=1, source_target_pairs={{0,1},{1,0},{2,3},{3,2},{4,5},{5,4},{6,7},{7,6},{8,9},{9,8},{10,11... | collective-permute-start | bytes 393224 | tf_op jit(solution)/shard_map/ppermute | solution.py:195

commit v2 on v1

v2 whole, which is shorter than its diff:
```python
import functools

import jax
import jax.numpy as jnp
from jax import lax
from jax.experimental import pallas as pl
from jax.experimental.pallas import tpu as pltpu
from jax.sharding import PartitionSpec as P

MZ = 8
MX = 8
MY = 256
LANES = 128
SUB = 8
TOP = 8
TERMS = 9


def sublane(shape):
    return lax.broadcasted_iota(jnp.int32, shape, len(shape) - 2)


def pack_kernel(lat_ref, depth_ref, grade_hbm, amp_hbm, pair_ref, cross_ref, near_hbm, far_hbm, held, sems, depth_sems):
    slices, rows, cols = grade_hbm.shape
    fields = (grade_hbm, amp_hbm)
    loads = {}
    for k in range(4):
        for f, src in enumerate(fields):
            for q in range(4):
                z = k + 4 * q
                loads[f, z] = pltpu.make_async_copy(src.at[z], held.at[f, z], sems.at[f, z])
                loads[f, z].start()
    odd_depth = lax.rem(depth_ref[0], 2)
    last, first = (1 - odd_depth) * (slices - 2), odd_depth * (slices - 2)
    others = []
    for f, src in enumerate(fields):
        others.append(pltpu.make_async_copy(src.at[pl.ds(last, 2)], near_hbm.at[f], depth_sems.at[f, 0]))
        others.append(pltpu.make_async_copy(src.at[pl.ds(first, 2)], far_hbm.at[f], depth_sems.at[f, 1]))
    for copy in others:
        copy.start()
    sub = sublane((SUB, cols))
    odd_row = lax.rem(sub, 2) == 1
    is_even = jnp.broadcast_to(lax.rem(lat_ref[0], 2), (SUB, cols)) == 0
    for k in range(4):
        for f in range(2):
            for q in range(4):
                loads[f, k + 4 * q].wait()
            high = [held[f, k + 4 * q, rows - SUB:rows, :] for q in range(4)]
            low = [held[f, k + 4 * q, 0:SUB, :] for q in range(4)]
            raw = jnp.where(
                sub < 4,
                jnp.where(sub < 2, pltpu.roll(high[0], 2, 0), pltpu.roll(high[3], 4, 0)),
                jnp.where(sub < 6, pltpu.roll(high[2], 6, 0), high[1]),
            )
            above = jnp.where(odd_row, raw, raw - 8.0 * pltpu.roll(raw, SUB - 1, 0))
            raw = jnp.where(
                sub < 4,
                jnp.where(sub < 2, low[3], pltpu.roll(low[2], 2, 0)),
                jnp.where(sub < 6, pltpu.roll(low[1], 4, 0), pltpu.roll(low[0], 6, 0)),
            )
            below = jnp.where(odd_row, 8.0 * pltpu.roll(raw, 1, 0) - raw, -raw)
            pair_ref[f, k] = jnp.where(is_even, above, below)
            cross_ref[f, k] = jnp.where(is_even, below, above)
    for copy in others:
        copy.wait()


def round_weight(w):
    return w.astype(jnp.bfloat16).astype(jnp.float32)


def march_kernel(scale, pieces, mask_ref, depth_ref, grade_hbm, amp_hbm, near_hbm, far_hbm, table_ref, *rest):
    outs, kept_ref = rest[:pieces], rest[pieces]
    grid_g, grid_a, acc_ref, low_ref, high_ref, sems = rest[pieces + 1:]
    slices, rows, cols = grade_hbm.shape
    strips = cols // LANES
    fields = ((grade_hbm, grid_g), (amp_hbm, grid_a))
    body = pl.ds(TOP, rows)
    odd_depth = lax.rem(depth_ref[0], 2)
    near_at = (1 - odd_depth) * (slices + 2)
    far_at = odd_depth * (slices + 2)

    def copies(s):
        lanes = pl.ds(s * LANES, LANES) if isinstance(s, int) else pl.ds(pl.multiple_of(s * LANES, LANES), LANES)
        made = []
        for f, (src, grid) in enumerate(fields):
            trio = (
                (src.at[:, :, lanes], grid.at[pl.ds(2, slices), s + 1, body, :]),
                (near_hbm.at[f, :, :, lanes], grid.at[pl.ds(near_at, 2), s + 1, body, :]),
                (far_hbm.at[f, :, :, lanes], grid.at[pl.ds(far_at, 2), s + 1, body, :]),
            )
            made += [pltpu.make_async_copy(here, there, sems.at[f, s, k]) for k, (here, there) in enumerate(trio)]
        return made

    for s in range(strips):
        for copy in copies(s):
            copy.start()
    zero = jnp.zeros((SUB, LANES), jnp.float32)
    for _, grid in fields:
        for z in range(slices):
            for r in range(0, rows, SUB):
                grid[z + 2, 0, TOP + r:TOP + r + SUB, :] = zero
                grid[z + 2, strips + 1, TOP + r:TOP + r + SUB, :] = zero
            for s in range(strips):
                grid[z + 2, s + 1, 0:TOP, :] = zero
                grid[z + 2, s + 1, TOP + rows:TOP + rows + SUB, :] = zero
    bins = table_ref.shape[1]
    table = (table_ref[...].astype(jnp.float32) / 65535.0).astype(jnp.bfloat16).astype(jnp.float32)
    table = jnp.where(sublane(table.shape) == 3, table * scale, table)
    column = lax.broadcasted_iota(jnp.int32, table.shape, 1)
    following = jnp.where(column == bins - 1, 0.0, pltpu.roll(table, bins - 1, 1))
    for c in range(4):
        low_ref[c] = jnp.broadcast_to(table[c:c + 1, :], (SUB, bins))
        high_ref[c] = jnp.broadcast_to(following[c:c + 1, :], (SUB, bins))
    lane = lax.broadcasted_iota(jnp.int32, (SUB, LANES), 1)
    per_block = MY // LANES
    piece_blocks = cols // pieces // MY

    def gather(ref, c, index):
        return jnp.take_along_axis(ref[c], index, axis=1)

    def stencil(m2, m1, p1, p2):
        return (m2 - p2) + 8.0 * (p1 - m1)

    def derivs(grid, z, s, r0):
        mid = grid[z, s, r0:r0 + SUB, :]
        left = grid[z, s - 1, r0:r0 + SUB, :]
        right = grid[z, s + 1, r0:r0 + SUB, :]
        dy = stencil(
            pltpu.roll(jnp.where(lane >= LANES - 2, left, mid), 2, 1),
            pltpu.roll(jnp.where(lane >= LANES - 1, left, mid), 1, 1),
            pltpu.roll(jnp.where(lane < 1, right, mid), LANES - 1, 1),
            pltpu.roll(jnp.where(lane < 2, right, mid), LANES - 2, 1),
        )
        dz = stencil(*(grid[z + k, s, r0:r0 + SUB, :] for k in (-2, -1, 1, 2)))
        dx = stencil(*(grid[z, s, r0 + k:r0 + k + SUB, :] for k in (-2, -1, 1, 2)))
        return mid, dx, dy * dy + dz * dz, dz

    def block(cb, carry):
        @pl.when(cb == 0)
        def _():
            for copy in copies(0):
                copy.wait()

        for j in range(1, per_block + 1):
            @pl.when(cb * per_block + j < strips)
            def _():
                for copy in copies(cb * per_block + j):
                    copy.wait()

        owner = lax.bitwise_xor(cb // piece_blocks, depth_ref[0])
        lanes = pl.ds(pl.multiple_of(lax.rem(cb, piece_blocks) * MY, MY), MY)
        for rt in range(rows // MX):
            r0 = TOP + rt * MX
            edge_rows = slice(0, 2) if rt == 0 else slice(SUB - 2, SUB)
            for j in range(per_block):
                for c in range(3):
                    acc_ref[j, c] = zero
                acc_ref[j, 3] = zero + 1.0
            for zb in range(slices // MZ):
                at = ((0, 4), (6, 2))[rt][zb]

                @pl.when(mask_ref[zb, rt, cb] != 0)
                def _():
                    for j in range(per_block):
                        s = cb * per_block + j + 1
                        red, green, blue, trans = (acc_ref[j, c] for c in range(4))
                        for zi in range(MZ):
                            z = 2 + zb * MZ + zi
                            grade, g_x, g_yz, g_z = derivs(grid_g, z, s, r0)
                            _, a_x, a_yz, _ = derivs(grid_a, z, s, r0)
                            g_yz = g_yz + 36.0
                            a_yz = a_yz + 144.0
                            steep = 0.7 * jnp.abs(g_z)
                            position = grade * (bins - 1.0)
                            index = jnp.minimum(position.astype(jnp.int32), bins - 1)
                            w_low = 1.0 - (position - index.astype(jnp.float32))
                            w_high = round_weight(1.0 - w_low)
                            w_low = round_weight(w_low)
                            cls = [
                                w_low * gather(low_ref, c, index) + w_high * gather(high_ref, c, index)
                                for c in range(4)
                            ]
                            for n, term in enumerate((g_x, a_x, g_yz, a_yz, steep, *cls)):
                                kept_ref[zi, s - 1, n, at:at + 2, :] = term[edge_rows, :]
                            edge = 1.0 - 12.0 * lax.rsqrt(a_x * a_x + a_yz)
                            shade = 0.3 + steep * lax.rsqrt(g_x * g_x + g_yz)
                            weight = trans * (cls[3] * edge)
                            trans = trans - weight
                            weight = weight * shade
                            red = red + weight * cls[0]
                            green = green + weight * cls[1]
                            blue = blue + weight * cls[2]
                        for c, value in enumerate((red, green, blue, trans)):
                            acc_ref[j, c] = value
            for k in range(pieces):
                @pl.when(owner == k)
                def _():
                    for c in range(4):
                        for j in range(per_block):
                            part = pl.ds(pl.multiple_of(lax.rem(cb, piece_blocks) * MY + j * LANES, LANES), LANES)
                            outs[k][c, rt * SUB:(rt + 1) * SUB, part] = acc_ref[j, c]
        return carry

    lax.fori_loop(0, cols // MY, block, 0)


def edge_kernel(pieces, mask_ref, depth_ref, lat_ref, kept_ref, pair_ref, cross_ref, *outs):
    half = kept_ref.shape[0]
    strips = kept_ref.shape[1]
    sub = sublane((SUB, LANES))
    is_first = lax.rem((sub + 2) // 4, 2) == 0
    odd_lat = jnp.broadcast_to(lax.rem(lat_ref[0], 2), (SUB, LANES))
    from_pair = lax.rem(sub // 2, 2) != odd_lat
    piece_strips = strips // pieces
    packs = piece_strips // 2

    def halo(f, zi, lanes):
        pair, cross = pair_ref[f, zi % 4, :, lanes], cross_ref[f, zi % 4, :, lanes]
        if zi < 4:
            return jnp.where(from_pair, pair, cross)
        return pltpu.roll(jnp.where(from_pair, cross, pair), 2, 0)

    def strip(s):
        lanes = pl.ds(pl.multiple_of(s * LANES, LANES), LANES)
        cb = s // (MY // LANES)
        full = [[jnp.broadcast_to(mask_ref[zb, rt, cb], (SUB, LANES)) for rt in range(2)] for zb in range(2)]
        live = jnp.where(
            sub < 4, jnp.where(sub < 2, full[0][0], full[1][1]), jnp.where(sub < 6, full[1][0], full[0][1])
        ) != 0
        zero = jnp.zeros((SUB, LANES), jnp.float32)
        total = [zero, zero, zero]
        trans = zero + 1.0
        for zi in range(half):
            g_x, a_x, g_yz, a_yz, steep, red, green, blue, alpha = (kept_ref[zi, s, n] for n in range(TERMS))
            g_x = g_x + halo(0, zi, lanes)
            a_x = a_x + halo(1, zi, lanes)
            edge = 1.0 - 12.0 * lax.rsqrt(a_x * a_x + a_yz)
            shade = 0.3 + steep * lax.rsqrt(g_x * g_x + g_yz)
            weight = jnp.where(live, trans * (alpha * edge), 0.0)
            trans = trans - weight
            weight = weight * shade
            total = [t + jnp.where(live, weight * c, 0.0) for t, c in zip(total, (red, green, blue))]
        out = [t + trans * pltpu.roll(t, 4, 0) for t in total]
        return out + [trans * pltpu.roll(trans, 4, 0)]

    def piece(p, carry):
        results = [strip(p * piece_strips + j) for j in range(piece_strips)]
        owner = lax.bitwise_xor(p, depth_ref[0])
        for j in range(packs):
            packed = [
                jnp.where(is_first, one, pltpu.roll(two, 4, 0)) for one, two in zip(results[j], results[j + packs])
            ]
            for k in range(pieces):
                @pl.when(owner == k)
                def _():
                    for c in range(4):
                        outs[k][c, :, j * LANES:(j + 1) * LANES] = packed[c]
        return carry

    lax.fori_loop(0, pieces, piece, 0)


def fold(parts, rank):
    level = 0
    while len(parts) > 1:
        first = lax.rem(lax.shift_right_logical(rank, level), 2) == 0
        merged = []
        for mine, other in zip(parts[0::2], parts[1::2]):
            first_here = jnp.broadcast_to(first, mine[3].shape)
            clear = jnp.where(first_here, mine[3], other[3])
            merged.append(
                [jnp.where(first_here, m, o) + clear * jnp.where(first_here, o, m) for m, o in zip(mine[:3], other[:3])]
                + [mine[3] * other[3]]
            )
        parts = merged
        level += 1
    return parts[0][:3] + [1.0 - parts[0][3]]


def finish_kernel(pieces, depth_ref, *refs):
    inner, edges, out_ref = refs[:pieces], refs[pieces:2 * pieces], refs[-1]
    rows, cols = out_ref.shape[1:]
    rank = depth_ref[0]
    frame = fold([[ref[c] for c in range(4)] for ref in inner], rank)
    rim = fold([[ref[c] for c in range(4)] for ref in edges], rank)
    for c in range(4):
        packed = rim[c]
        wide = jnp.concatenate([packed, pltpu.roll(packed, 4, 0)], axis=1)
        sub = sublane(wide.shape)
        out_ref[c, 0:SUB, :] = jnp.where(sub < 2, wide, frame[c][0:SUB, :])
        out_ref[c, rows - SUB:rows, :] = jnp.where(sub >= SUB - 2, wide, frame[c][rows - SUB:rows, :])


def swap_near(x, axis):
    return lax.ppermute(x, axis, [(i, i ^ 1) for i in range(lax.axis_size(axis))])


def swap_far(x, axis):
    size = lax.axis_size(axis)
    return lax.ppermute(x, axis, [(i, j) for k in range(1, size - 1, 2) for i, j in ((k, k + 1), (k + 1, k))])


def local(grade_field, amplitude, tf_table, brick_mask):
    slices, rows, cols = grade_field.shape
    assert (slices, rows) == (2 * MZ, 2 * MX)
    pieces = lax.axis_size("depth")
    depth_rank = lax.axis_index("depth").astype(jnp.int32).reshape(1)
    lat_rank = lax.axis_index("lat").astype(jnp.int32).reshape(1)
    scale = 4.0 / (slices * pieces)
    strips = cols // LANES
    f32 = jnp.float32
    vmem = pl.BlockSpec(memory_space=pltpu.VMEM)
    smem = pl.BlockSpec(memory_space=pltpu.SMEM)
    hbm = pl.BlockSpec(memory_space=pltpu.MemorySpace.HBM)
    lat_halo = jax.ShapeDtypeStruct((2, slices // 4, SUB, cols), f32)
    depth_halo = jax.ShapeDtypeStruct((2, 2, rows, cols), f32)
    pair, cross, near, far = pl.pallas_call(
        pack_kernel,
        out_shape=(lat_halo, lat_halo, depth_halo, depth_halo),
        in_specs=[smem, smem, hbm, hbm],
        out_specs=[vmem, vmem, hbm, hbm],
        scratch_shapes=[
            pltpu.VMEM((2, slices, rows, cols), f32),
            pltpu.SemaphoreType.DMA((2, slices)),
            pltpu.SemaphoreType.DMA((2, 2)),
        ],
        compiler_params=pltpu.CompilerParams(vmem_limit_bytes=16 << 20),
        name="pack",
    )(lat_rank, depth_rank, grade_field, amplitude)
    pair = swap_near(pair, "lat")
    cross = swap_far(cross, "lat")
    near = swap_near(near, "depth")
    far = swap_far(far, "depth")
    piece = jax.ShapeDtypeStruct((4, rows, cols // pieces), f32)
    kept = jax.ShapeDtypeStruct((MZ, strips, TERMS, SUB, LANES), f32)
    grid = pltpu.VMEM((slices + 4, strips + 2, TOP + rows + SUB, LANES), f32)
    table = pltpu.VMEM((4, SUB, tf_table.shape[1]), f32)
    *parts, kept = pl.pallas_call(
        functools.partial(march_kernel, scale, pieces),
        out_shape=(piece,) * pieces + (kept,),
        in_specs=[smem, smem, hbm, hbm, hbm, hbm, vmem],
        out_specs=[vmem] * (pieces + 1),
        scratch_shapes=[
            grid,
            grid,
            pltpu.VMEM((MY // LANES, 4, SUB, LANES), f32),
            table,
            table,
            pltpu.SemaphoreType.DMA((2, strips, 3)),
        ],
        compiler_params=pltpu.CompilerParams(vmem_limit_bytes=24 << 20),
        name="march",
    )(brick_mask, depth_rank, grade_field, amplitude, near, far, tf_table)

    def exchange(parts):
        return [parts[0]] + [
            lax.ppermute(parts[k], "depth", [(i, i ^ k) for i in range(pieces)]) for k in range(1, pieces)
        ]

    inner = exchange(parts)
    rim = jax.ShapeDtypeStruct((4, SUB, cols // pieces // 2), f32)
    rims = pl.pallas_call(
        functools.partial(edge_kernel, pieces),
        out_shape=(rim,) * pieces,
        in_specs=[smem, smem, smem, vmem, vmem, vmem],
        out_specs=[vmem] * pieces,
        compiler_params=pltpu.CompilerParams(vmem_limit_bytes=16 << 20),
        name="edges",
    )(brick_mask, depth_rank, lat_rank, kept, pair, cross)
    edges = exchange(rims)
    return pl.pallas_call(
        functools.partial(finish_kernel, pieces),
        out_shape=piece,
        in_specs=[smem] + [vmem] * (2 * pieces),
        out_specs=vmem,
        compiler_params=pltpu.CompilerParams(vmem_limit_bytes=4 << 20),
        name="finish",
    )(depth_rank, *inner, *edges)


def solution(mesh):
    placed = (P("depth", "lat", None), P("depth", "lat", None), P(), P("depth", "lat", None))
    return jax.shard_map(
        local, mesh=mesh, in_specs=placed, out_specs=P(None, "lat", "depth"), check_vma=False
    )
```

time: 55.6 us -> 43.7 us (0.79)
  the two profiles are of different devices: /device:TPU:25 before, /device:TPU:0 now
where the time goes in v2:
time: 43.7 us; the launch traced here: 43.4 us
  Pallas kernels  19.2 us (44%)
  starting transfers between devices  18 us (41%)
  local copies, waits for them, and re-layouts  3.2 us (7%)
  waiting for transfers between devices  2.85 us (7%)
    ppermute x6, starting transfers between devices, exchange(): lax.ppermute(parts[k], 'depth', [(i, i ^ k) for i in range(pieces)])  13.5 us
    pallas_call x1, Pallas kernels, local(): pl.pallas_call(functools.partial(march_kernel, scale, pieces), out_shape=...  10.9 us
    pallas_call x1, Pallas kernels, local(): pl.pallas_call(pack_kernel, out_shape=(lat_halo, lat_halo, depth_halo, de...  6.29 us
    unnamed x12, local copies, waits for them, and re-layouts  3.2 us
    ppermute x2, starting transfers between devices, swap_near(): lax.ppermute(x, axis, [(i, i ^ 1) for i in range(lax.axis_size(axis))])  3.12 us
    ppermute x6, waiting for transfers between devices, exchange(): lax.ppermute(parts[k], 'depth', [(i, i ^ k) for i in range(pieces)])  2.46 us
    ppermute x2, starting transfers between devices, swap_far(): lax.ppermute(x, axis, [(i, j) for k in range(1, size - 1, 2) for i, j in...  1.36 us
    pallas_call x1, Pallas kernels, local(): pl.pallas_call(functools.partial(edge_kernel, pieces), out_shape=(rim,) *...  1.28 us
  transfers between devices with their start and end apart: 10, of which 3 were waited for; matrix products, arithmetic and copies ran while one was open for 0% of the time, Pallas kernels for 28%

profile of v2, /device:TPU:0, one launch (start us, length us, event | category | flops | bytes accessed | tf_op | source)
XLA Modules:
  0.0 43.4 jit_solution(568322603524971476)
XLA Ops:
  0.0 0.0 copy-start
  0.0 1.6 %copy-done = f32[16,16,2048]{2,1,0:T(8,128)S(1)} copy-done((f32[16,16,2048]{2,1,0:T(8,128)S(1)}, f32[16,16,2048]{2,1,0:T(8,128)}, u32[]{:S(2)}) %copy-start) | copy-done | bytes 2097176
  1.6 0.0 copy-start.2
  1.6 1.6 %copy-done.2 = f32[16,16,2048]{2,1,0:T(8,128)S(1)} copy-done((f32[16,16,2048]{2,1,0:T(8,128)S(1)}, f32[16,16,2048]{2,1,0:T(8,128)}, u32[]{:S(2)}) %copy-start.2) | copy-done | bytes 2097176
  3.2 0.0 copy-start.1
  3.2 0.0 copy-start.3
  3.2 0.0 copy-start.4
  3.2 0.0 copy-start.5
  3.2 6.3 %pack.1 = (f32[2,4,8,2048]{3,2,1,0:T(8,128)S(1)}, f32[2,4,8,2048]{3,2,1,0:T(8,128)S(1)}, f32[2,2,16,2048]{3,2,1,0:T(8,128)S(1)}, f32[2,2,16,2048]{3,2,1,0:T(8,128)S(1)}) custom-call(s32[1]{0:T(128)} %bitcast.1.lat_ref, s32[1]{0:T(128)} %bitcast.depth_ref, f32[16,16,2048]{2,1,0:T(8,128)S(1)} %copy-done, f32[16,16,2048]{2,1,0:T(8,128)S(1)} %copy-done.2), custom_call_target="tpu_custom_call" | custom-call | tf_op jit(solution)/shard_map/pack/pallas_call | solution.py:318
  9.5 0.5 %collective-permute-start = (f32[2,2,16,2048]{3,2,1,0:T(8,128)S(1)}, f32[2,2,16,2048]{3,2,1,0:T(8,128)S(1)}, u32[]{:S(2)}, u32[]{:S(2)}) collective-permute-start(f32[2,2,16,2048]{3,2,1,0:T(8,128)S(1)} %get-tuple-element.18), channel_id=1, source_target_pairs={{0,1},{1,0},{2,3},{3,2},{4,5},{5,4},{6,7},{7,6},{8,9},{9,8},{10,11... | collective-permute-start | bytes 1572872 | tf_op jit(solution)/shard_map/ppermute | solution.py:296
  10.0 0.7 %collective-permute-start.1 = (f32[2,2,16,2048]{3,2,1,0:T(8,128)S(1)}, f32[2,2,16,2048]{3,2,1,0:T(8,128)S(1)}, u32[]{:S(2)}, u32[]{:S(2)}) collective-permute-start(f32[2,2,16,2048]{3,2,1,0:T(8,128)S(1)} %get-tuple-element.19), channel_id=1, source_target_pairs={{1,2},{2,1},{5,6},{6,5},{9,10},{10,9},{13,14},{14,13},{17,18},{18,... | collective-permute-start | bytes 1572872 | tf_op jit(solution)/shard_map/ppermute | solution.py:301
  10.7 2.6 %collective-permute-start.5 = (f32[2,4,8,2048]{3,2,1,0:T(8,128)S(1)}, f32[2,4,8,2048]{3,2,1,0:T(8,128)S(1)}, u32[]{:S(2)}, u32[]{:S(2)}) collective-permute-start(f32[2,4,8,2048]{3,2,1,0:T(8,128)S(1)} %get-tuple-element.25), channel_id=1, source_target_pairs={{0,4},{4,0},{8,12},{12,8},{16,20},{20,16},{24,28},{28,24},{1,5},{5... | collective-permute-start | bytes 1572872 | tf_op jit(solution)/shard_map/ppermute | solution.py:296
  13.3 0.7 %collective-permute-start.6 = (f32[2,4,8,2048]{3,2,1,0:T(8,128)S(1)}, f32[2,4,8,2048]{3,2,1,0:T(8,128)S(1)}, u32[]{:S(2)}, u32[]{:S(2)}) collective-permute-start(f32[2,4,8,2048]{3,2,1,0:T(8,128)S(1)} %get-tuple-element.26), channel_id=1, source_target_pairs={{4,8},{8,4},{12,16},{16,12},{20,24},{24,20},{5,9},{9,5},{13,17},{1... | collective-permute-start | bytes 1572872 | tf_op jit(solution)/shard_map/ppermute | solution.py:301
  14.0 0.0 collective-permute-done.near_hbm
  14.0 0.0 collective-permute-done.1.far_hbm
  14.0 0.0 copy-done.1
  14.0 0.0 copy-done.3
  14.0 0.0 copy-done.4
  14.0 0.0 copy-done.5
  14.1 10.9 %march.1 = (f32[4,16,512]{2,1,0:T(8,128)S(1)}, f32[4,16,512]{2,1,0:T(8,128)S(1)}, f32[4,16,512]{2,1,0:T(8,128)S(1)}, f32[4,16,512]{2,1,0:T(8,128)S(1)}, f32[8,16,9,8,128]{4,3,2,1,0:T(8,128)S(1)}) custom-call(s32[2,2,8]{2,1,0:T(2,128)S(1)} %copy-done.4, s32[1]{0:T(128)} %bitcast.depth_ref, f32[16,16,2048]{2,1,0:T(8,128)S(1)} %copy-done.1, ...), custom_call_target="tpu_custom_call" | custom-call | tf_op jit(solution)/shard_map/march/pallas_call | solution.py:339
  25.0 8.1 %collective-permute-start.2 = (f32[4,16,512]{2,1,0:T(8,128)S(1)}, f32[4,16,512]{2,1,0:T(8,128)S(1)}, u32[]{:S(2)}, u32[]{:S(2)}) collective-permute-start(f32[4,16,512]{2,1,0:T(8,128)S(1)} %get-tuple-element.21), channel_id=1, source_target_pairs={{0,1},{1,0},{2,3},{3,2},{4,5},{5,4},{6,7},{7,6},{8,9},{9,8},{10,11... | collective-permute-start | bytes 393224 | tf_op jit(solution)/shard_map/ppermute | solution.py:358
  33.1 0.0 collective-permute-start.3
  33.1 1.4 %collective-permute-start.4 = (f32[4,16,512]{2,1,0:T(8,128)S(1)}, f32[4,16,512]{2,1,0:T(8,128)S(1)}, u32[]{:S(2)}, u32[]{:S(2)}) collective-permute-start(f32[4,16,512]{2,1,0:T(8,128)S(1)} %get-tuple-element.23), channel_id=1, source_target_pairs={{0,3},{1,2},{2,1},{3,0},{4,7},{5,6},{6,5},{7,4},{8,11},{9,10},{10,... | collective-permute-start | bytes 393224 | tf_op jit(solution)/shard_map/ppermute | solution.py:358
  34.6 0.4 collective-permute-done.5.pair_ref
  34.9 0.0 collective-permute-done.6.cross_ref
  34.9 1.3 %edges.1 = (f32[4,8,256]{2,1,0:T(8,128)S(1)}, f32[4,8,256]{2,1,0:T(8,128)S(1)}, f32[4,8,256]{2,1,0:T(8,128)S(1)}, f32[4,8,256]{2,1,0:T(8,128)S(1)}) custom-call(s32[2,2,8]{2,1,0:T(2,128)S(1)} %copy-done.4, s32[1]{0:T(128)} %bitcast.depth_ref, s32[1]{0:T(128)} %bitcast.1.lat_ref, f32[8,16,9,8,128]{4,3,2,1,0:T(8,128)S(1)} %get-tuple-element.24.kept_ref, ...), custom_call_target="tpu_custom_call" | custom-call | tf_op jit(solution)/shard_map/edges/pallas_call | solution.py:363
  36.2 2.1 %collective-permute-start.7 = (f32[4,8,256]{2,1,0:T(8,128)S(1)}, f32[4,8,256]{2,1,0:T(8,128)S(1)}, u32[]{:S(2)}, u32[]{:S(2)}) collective-permute-start(f32[4,8,256]{2,1,0:T(8,128)S(1)} %get-tuple-element.28), channel_id=1, source_target_pairs={{0,1},{1,0},{2,3},{3,2},{4,5},{5,4},{6,7},{7,6},{8,9},{9,8},{10,11... | collective-permute-start | bytes 98312 | tf_op jit(solution)/shard_map/ppermute | solution.py:358
  38.3 1.0 %collective-permute-start.8 = (f32[4,8,256]{2,1,0:T(8,128)S(1)}, f32[4,8,256]{2,1,0:T(8,128)S(1)}, u32[]{:S(2)}, u32[]{:S(2)}) collective-permute-start(f32[4,8,256]{2,1,0:T(8,128)S(1)} %get-tuple-element.29), channel_id=1, source_target_pairs={{0,2},{1,3},{2,0},{3,1},{4,6},{5,7},{6,4},{7,5},{8,10},{9,11},{10,... | collective-permute-start | bytes 98312 | tf_op jit(solution)/shard_map/ppermute | solution.py:358
  39.3 0.0 collective-permute-done.7.refs_5_
  39.3 0.9 %collective-permute-start.9 = (f32[4,8,256]{2,1,0:T(8,128)S(1)}, f32[4,8,256]{2,1,0:T(8,128)S(1)}, u32[]{:S(2)}, u32[]{:S(2)}) collective-permute-start(f32[4,8,256]{2,1,0:T(8,128)S(1)} %get-tuple-element.30), channel_id=1, source_target_pairs={{0,3},{1,2},{2,1},{3,0},{4,7},{5,6},{6,5},{7,4},{8,11},{9,10},{10,... | collective-permute-start | bytes 98312 | tf_op jit(solution)/shard_map/ppermute | solution.py:358
  40.2 2.0 %collective-permute-done.8.refs_6_ = f32[4,8,256]{2,1,0:T(8,128)S(1)} collective-permute-done((f32[4,8,256]{2,1,0:T(8,128)S(1)}, f32[4,8,256]{2,1,0:T(8,128)S(1)}, u32[]{:S(2)}, u32[]{:S(2)}) %collective-permute-start.8) | collective-permute-done | bytes 32800 | tf_op jit(solution)/shard_map/ppermute | solution.py:358
  42.3 0.4 collective-permute-done.9.refs_7_
  42.6 0.0 collective-permute-done.2.refs_1_
  42.7 0.0 collective-permute-done.3.refs_2_
  42.7 0.0 collective-permute-done.4.refs_3_
  42.7 0.7 %finish.1 = f32[4,16,512]{2,1,0:T(8,128)} custom-call(s32[1]{0:T(128)} %bitcast.depth_ref, f32[4,16,512]{2,1,0:T(8,128)S(1)} %get-tuple-element.20.refs_0_, f32[4,16,512]{2,1,0:T(8,128)S(1)} %collective-permute-done.2.refs_1_, f32[4,16,512]{2,1,0:T(8,128)S(1)} %collective-permute-done.3.refs_2_, f32[4,16,512]{2,1,0:T(8,128)S(1)} %collective-permute-done.4.refs_3_, ...), custom_call_target="tpu_custom_call" | custom-call | tf_op jit(solution)/shard_map/finish/pallas_call | solution.py:372
Async XLA Ops:
  0.0 1.6 %copy-start = (f32[16,16,2048]{2,1,0:T(8,128)S(1)}, f32[16,16,2048]{2,1,0:T(8,128)}, u32[]{:S(2)}) copy-start(f32[16,16,2048]{2,1,0:T(8,128)} %grade_hbm.3) | copy-start | bytes 6291460
  1.6 1.6 %copy-start.2 = (f32[16,16,2048]{2,1,0:T(8,128)S(1)}, f32[16,16,2048]{2,1,0:T(8,128)}, u32[]{:S(2)}) copy-start(f32[16,16,2048]{2,1,0:T(8,128)} %amp_hbm.3) | copy-start | bytes 6291460
  3.2 10.8 %copy-start.1 = (f32[16,16,2048]{2,1,0:T(8,128)S(1)}, f32[16,16,2048]{2,1,0:T(8,128)}, u32[]{:S(2)}) copy-start(f32[16,16,2048]{2,1,0:T(8,128)} %grade_hbm.3) | copy-start | bytes 6291460
  3.2 10.8 %copy-start.3 = (f32[16,16,2048]{2,1,0:T(8,128)S(1)}, f32[16,16,2048]{2,1,0:T(8,128)}, u32[]{:S(2)}) copy-start(f32[16,16,2048]{2,1,0:T(8,128)} %amp_hbm.3) | copy-start | bytes 6291460
  3.2 10.9 %copy-start.4 = (s32[2,2,8]{2,1,0:T(2,128)S(1)}, s32[2,2,8]{2,1,0:T(2,128)}, u32[]{:S(2)}) copy-start(s32[2,2,8]{2,1,0:T(2,128)} %mask_ref.3) | copy-start | bytes 388
  3.2 10.9 %copy-start.5 = (s32[4,128]{1,0:T(4,128)S(1)}, s32[4,128]{1,0:T(4,128)}, u32[]{:S(2)}) copy-start(s32[4,128]{1,0:T(4,128)} %table_ref.1) | copy-start | bytes 6148
  9.5 4.5 %collective-permute-start = (f32[2,2,16,2048]{3,2,1,0:T(8,128)S(1)}, f32[2,2,16,2048]{3,2,1,0:T(8,128)S(1)}, u32[]{:S(2)}, u32[]{:S(2)}) collective-permute-start(f32[2,2,16,2048]{3,2,1,0:T(8,128)S(1)} %get-tuple-element.18), channel_id=1, source_target_pairs={{0,1},{1,0},{2,3},{3,2},{4,5},{5,4},{6,7},{7,6},{8,9},{9,8},{10,11... | collective-permute-start | bytes 1572872 | tf_op jit(solution)/shard_map/ppermute | solution.py:296
  10.0 4.0 %collective-permute-start.1 = (f32[2,2,16,2048]{3,2,1,0:T(8,128)S(1)}, f32[2,2,16,2048]{3,2,1,0:T(8,128)S(1)}, u32[]{:S(2)}, u32[]{:S(2)}) collective-permute-start(f32[2,2,16,2048]{3,2,1,0:T(8,128)S(1)} %get-tuple-element.19), channel_id=1, source_target_pairs={{1,2},{2,1},{5,6},{6,5},{9,10},{10,9},{13,14},{14,13},{17,18},{18,... | collective-permute-start | bytes 1572872 | tf_op jit(solution)/shard_map/ppermute | solution.py:301
  10.7 24.2 %collective-permute-start.5 = (f32[2,4,8,2048]{3,2,1,0:T(8,128)S(1)}, f32[2,4,8,2048]{3,2,1,0:T(8,128)S(1)}, u32[]{:S(2)}, u32[]{:S(2)}) collective-permute-start(f32[2,4,8,2048]{3,2,1,0:T(8,128)S(1)} %get-tuple-element.25), channel_id=1, source_target_pairs={{0,4},{4,0},{8,12},{12,8},{16,20},{20,16},{24,28},{28,24},{1,5},{5... | collective-permute-start | bytes 1572872 | tf_op jit(solution)/shard_map/ppermute | solution.py:296
  13.3 21.6 %collective-permute-start.6 = (f32[2,4,8,2048]{3,2,1,0:T(8,128)S(1)}, f32[2,4,8,2048]{3,2,1,0:T(8,128)S(1)}, u32[]{:S(2)}, u32[]{:S(2)}) collective-permute-start(f32[2,4,8,2048]{3,2,1,0:T(8,128)S(1)} %get-tuple-element.26), channel_id=1, source_target_pairs={{4,8},{8,4},{12,16},{16,12},{20,24},{24,20},{5,9},{9,5},{13,17},{1... | collective-permute-start | bytes 1572872 | tf_op jit(solution)/shard_map/ppermute | solution.py:301
  25.0 17.7 %collective-permute-start.2 = (f32[4,16,512]{2,1,0:T(8,128)S(1)}, f32[4,16,512]{2,1,0:T(8,128)S(1)}, u32[]{:S(2)}, u32[]{:S(2)}) collective-permute-start(f32[4,16,512]{2,1,0:T(8,128)S(1)} %get-tuple-element.21), channel_id=1, source_target_pairs={{0,1},{1,0},{2,3},{3,2},{4,5},{5,4},{6,7},{7,6},{8,9},{9,8},{10,11... | collective-permute-start | bytes 393224 | tf_op jit(solution)/shard_map/ppermute | solution.py:358
  33.1 9.5 %collective-permute-start.3 = (f32[4,16,512]{2,1,0:T(8,128)S(1)}, f32[4,16,512]{2,1,0:T(8,128)S(1)}, u32[]{:S(2)}, u32[]{:S(2)}) collective-permute-start(f32[4,16,512]{2,1,0:T(8,128)S(1)} %get-tuple-element.22), channel_id=1, source_target_pairs={{0,2},{1,3},{2,0},{3,1},{4,6},{5,7},{6,4},{7,5},{8,10},{9,11},{10,... | collective-permute-start | bytes 393224 | tf_op jit(solution)/shard_map/ppermute | solution.py:358
  33.1 9.5 %collective-permute-start.4 = (f32[4,16,512]{2,1,0:T(8,128)S(1)}, f32[4,16,512]{2,1,0:T(8,128)S(1)}, u32[]{:S(2)}, u32[]{:S(2)}) collective-permute-start(f32[4,16,512]{2,1,0:T(8,128)S(1)} %get-tuple-element.23), channel_id=1, source_target_pairs={{0,3},{1,2},{2,1},{3,0},{4,7},{5,6},{6,5},{7,4},{8,11},{9,10},{10,... | collective-permute-start | bytes 393224 | tf_op jit(solution)/shard_map/ppermute | solution.py:358
  36.2 3.1 %collective-permute-start.7 = (f32[4,8,256]{2,1,0:T(8,128)S(1)}, f32[4,8,256]{2,1,0:T(8,128)S(1)}, u32[]{:S(2)}, u32[]{:S(2)}) collective-permute-start(f32[4,8,256]{2,1,0:T(8,128)S(1)} %get-tuple-element.28), channel_id=1, source_target_pairs={{0,1},{1,0},{2,3},{3,2},{4,5},{5,4},{6,7},{7,6},{8,9},{9,8},{10,11... | collective-permute-start | bytes 98312 | tf_op jit(solution)/shard_map/ppermute | solution.py:358
  38.3 3.9 %collective-permute-start.8 = (f32[4,8,256]{2,1,0:T(8,128)S(1)}, f32[4,8,256]{2,1,0:T(8,128)S(1)}, u32[]{:S(2)}, u32[]{:S(2)}) collective-permute-start(f32[4,8,256]{2,1,0:T(8,128)S(1)} %get-tuple-element.29), channel_id=1, source_target_pairs={{0,2},{1,3},{2,0},{3,1},{4,6},{5,7},{6,4},{7,5},{8,10},{9,11},{10,... | collective-permute-start | bytes 98312 | tf_op jit(solution)/shard_map/ppermute | solution.py:358
  39.3 3.3 %collective-permute-start.9 = (f32[4,8,256]{2,1,0:T(8,128)S(1)}, f32[4,8,256]{2,1,0:T(8,128)S(1)}, u32[]{:S(2)}, u32[]{:S(2)}) collective-permute-start(f32[4,8,256]{2,1,0:T(8,128)S(1)} %get-tuple-element.30), channel_id=1, source_target_pairs={{0,3},{1,2},{2,1},{3,0},{4,7},{5,6},{6,5},{7,4},{8,11},{9,10},{10,... | collective-permute-start | bytes 98312 | tf_op jit(solution)/shard_map/ppermute | solution.py:358

commit v3 on v2

--- a/solution.py
+++ b/solution.py
@@ -20,48 +20,44 @@
     return lax.broadcasted_iota(jnp.int32, shape, len(shape) - 2)
 
 
-def pack_kernel(lat_ref, depth_ref, grade_hbm, amp_hbm, pair_ref, cross_ref, near_hbm, far_hbm, held, sems, depth_sems):
-    slices, rows, cols = grade_hbm.shape
-    fields = (grade_hbm, amp_hbm)
-    loads = {}
-    for k in range(4):
-        for f, src in enumerate(fields):
+def rows_kernel(lat_ref, grade_hbm, amp_hbm, pair_hbm, cross_hbm, sems):
+    slices, rows = grade_hbm.shape[:2]
+    span = slices // 4
+    even = lax.rem(lat_ref[0], 2) == 0
+
+    def copies(above_dst, below_dst):
+        made = []
+        for f, src in enumerate((grade_hbm, amp_hbm)):
             for q in range(4):
-                z = k + 4 * q
-                loads[f, z] = pltpu.make_async_copy(src.at[z], held.at[f, z], sems.at[f, z])
-                loads[f, z].start()
-    odd_depth = lax.rem(depth_ref[0], 2)
-    last, first = (1 - odd_depth) * (slices - 2), odd_depth * (slices - 2)
-    others = []
-    for f, src in enumerate(fields):
-        others.append(pltpu.make_async_copy(src.at[pl.ds(last, 2)], near_hbm.at[f], depth_sems.at[f, 0]))
-        others.append(pltpu.make_async_copy(src.at[pl.ds(first, 2)], far_hbm.at[f], depth_sems.at[f, 1]))
-    for copy in others:
+                part = src.at[pl.ds(span * q, span)]
+                above = above_dst.at[f, :, pl.ds((0, 6, 4, 2)[q], 2), :]
+                below = below_dst.at[f, :, pl.ds((6, 4, 2, 0)[q], 2), :]
+                made.append(pltpu.make_async_copy(part.at[:, pl.ds(rows - 2, 2), :], above, sems.at[f, q, 0]))
+                made.append(pltpu.make_async_copy(part.at[:, pl.ds(0, 2), :], below, sems.at[f, q, 1]))
+        for copy in made:
+            copy.start()
+        for copy in made:
+            copy.wait()
+
+    @pl.when(even)
+    def _():
+        copies(pair_hbm, cross_hbm)
+
+    @pl.when(jnp.logical_not(even))
+    def _():
+        copies(cross_hbm, pair_hbm)
+
+
+def slices_kernel(depth_ref, grade_hbm, amp_hbm, near_hbm, far_hbm, sems):
+    slices = grade_hbm.shape[0]
+    odd = lax.rem(depth_ref[0], 2)
+    made = []
+    for f, src in enumerate((grade_hbm, amp_hbm)):
+        for n, (dst, at) in enumerate(((near_hbm, 1 - odd), (far_hbm, odd))):
+            made.append(pltpu.make_async_copy(src.at[pl.ds(at * (slices - 2), 2)], dst.at[f], sems.at[f, n]))
+    for copy in made:
         copy.start()
-    sub = sublane((SUB, cols))
-    odd_row = lax.rem(sub, 2) == 1
-    is_even = jnp.broadcast_to(lax.rem(lat_ref[0], 2), (SUB, cols)) == 0
-    for k in range(4):
-        for f in range(2):
-            for q in range(4):
-                loads[f, k + 4 * q].wait()
-            high = [held[f, k + 4 * q, rows - SUB:rows, :] for q in range(4)]
-            low = [held[f, k + 4 * q, 0:SUB, :] for q in range(4)]
-            raw = jnp.where(
-                sub < 4,
-                jnp.where(sub < 2, pltpu.roll(high[0], 2, 0), pltpu.roll(high[3], 4, 0)),
-                jnp.where(sub < 6, pltpu.roll(high[2], 6, 0), high[1]),
-            )
-            above = jnp.where(odd_row, raw, raw - 8.0 * pltpu.roll(raw, SUB - 1, 0))
-            raw = jnp.where(
-                sub < 4,
-                jnp.where(sub < 2, low[3], pltpu.roll(low[2], 2, 0)),
-                jnp.where(sub < 6, pltpu.roll(low[1], 4, 0), pltpu.roll(low[0], 6, 0)),
-            )
-            below = jnp.where(odd_row, 8.0 * pltpu.roll(raw, 1, 0) - raw, -raw)
-            pair_ref[f, k] = jnp.where(is_even, above, below)
-            cross_ref[f, k] = jnp.where(is_even, below, above)
-    for copy in others:
+    for copy in made:
         copy.wait()
 
 
@@ -215,11 +211,19 @@
     piece_strips = strips // pieces
     packs = piece_strips // 2
 
+    above = lax.rem(sub // 2, 2) == 0
+    even_row = lax.rem(sub, 2) == 0
+
+    def outside(raw, above):
+        mate = jnp.where(even_row, pltpu.roll(raw, SUB - 1, 0), pltpu.roll(raw, 1, 0))
+        mate = jnp.where(above == even_row, 8.0 * mate, 0.0)
+        return jnp.where(above, raw - mate, mate - raw)
+
     def halo(f, zi, lanes):
         pair, cross = pair_ref[f, zi % 4, :, lanes], cross_ref[f, zi % 4, :, lanes]
         if zi < 4:
-            return jnp.where(from_pair, pair, cross)
-        return pltpu.roll(jnp.where(from_pair, cross, pair), 2, 0)
+            return outside(jnp.where(from_pair, pair, cross), above)
+        return outside(pltpu.roll(jnp.where(from_pair, cross, pair), 2, 0), above)
 
     def strip(s):
         lanes = pl.ds(pl.multiple_of(s * LANES, LANES), LANES)
@@ -315,19 +319,25 @@
     hbm = pl.BlockSpec(memory_space=pltpu.MemorySpace.HBM)
     lat_halo = jax.ShapeDtypeStruct((2, slices // 4, SUB, cols), f32)
     depth_halo = jax.ShapeDtypeStruct((2, 2, rows, cols), f32)
-    pair, cross, near, far = pl.pallas_call(
-        pack_kernel,
-        out_shape=(lat_halo, lat_halo, depth_halo, depth_halo),
-        in_specs=[smem, smem, hbm, hbm],
-        out_specs=[vmem, vmem, hbm, hbm],
-        scratch_shapes=[
-            pltpu.VMEM((2, slices, rows, cols), f32),
-            pltpu.SemaphoreType.DMA((2, slices)),
-            pltpu.SemaphoreType.DMA((2, 2)),
-        ],
-        compiler_params=pltpu.CompilerParams(vmem_limit_bytes=16 << 20),
-        name="pack",
-    )(lat_rank, depth_rank, grade_field, amplitude)
+    hbm_only = pltpu.MemorySpace.HBM
+    grade_field = pltpu.with_memory_space_constraint(grade_field, hbm_only)
+    amplitude = pltpu.with_memory_space_constraint(amplitude, hbm_only)
+    pair, cross = pl.pallas_call(
+        rows_kernel,
+        out_shape=(lat_halo, lat_halo),
+        in_specs=[smem, hbm, hbm],
+        out_specs=[hbm, hbm],
+        scratch_shapes=[pltpu.SemaphoreType.DMA((2, 4, 2))],
+        name="take_rows",
+    )(lat_rank, grade_field, amplitude)
+    near, far = pl.pallas_call(
+        slices_kernel,
+        out_shape=(depth_halo, depth_halo),
+        in_specs=[smem, hbm, hbm],
+        out_specs=[hbm, hbm],
+        scratch_shapes=[pltpu.SemaphoreType.DMA((2, 2))],
+        name="take_slices",
+    )(depth_rank, grade_field, amplitude)
     pair = swap_near(pair, "lat")
     cross = swap_far(cross, "lat")
     near = swap_near(near, "depth")

time: 43.7 us -> 101 us (2.31)
  Pallas kernels: 19.2 us -> 80.7 us
  starting transfers between devices: 18 us -> 10.4 us
  waiting for transfers between devices: 2.85 us -> 9.18 us
  local copies, waits for them, and re-layouts: 3.2 us -> 0.01 us
    pallas_call x1 -> x2, Pallas kernels: 6.29 us -> 65.9 us  [the longest x1 33 us: local(): pl.pallas_call(rows_kernel, out_shape=(lat_halo, lat_halo), in_specs=[sme...]
    ppermute x6, starting transfers between devices: 13.5 us -> 5.89 us  [exchange(): lax.ppermute(parts[k], 'depth', [(i, i ^ k) for i in range(pieces)])]
    ppermute x2, waiting for transfers between devices: 0.39 us -> 6.72 us  [swap_near(): lax.ppermute(x, axis, [(i, i ^ 1) for i in range(lax.axis_size(axis))])]
    unnamed x12 -> x4, local copies, waits for them, and re-layouts: 3.2 us -> 0.01 us
    pallas_call x1, Pallas kernels: 10.9 us -> 12.6 us  [local(): pl.pallas_call(functools.partial(march_kernel, scale, pieces), out_shape=...]
  transfers between devices with their start and end apart: 10 -> 10, of which waited for: 3 -> 3; matrix products, arithmetic and copies ran while one was open for 0% -> 0% of each run, Pallas kernels for 28% -> 47%
where the time goes in v3:
time: 101 us; the launch traced here: 100 us
  Pallas kernels  80.7 us (80%)
  starting transfers between devices  10.4 us (10%)
  waiting for transfers between devices  9.18 us (9%)
    pallas_call x1, Pallas kernels, local(): pl.pallas_call(rows_kernel, out_shape=(lat_halo, lat_halo), in_specs=[sme...  33 us
    pallas_call x1, Pallas kernels, local(): pl.pallas_call(slices_kernel, out_shape=(depth_halo, depth_halo), in_spec...  32.9 us
    pallas_call x1, Pallas kernels, local(): pl.pallas_call(functools.partial(march_kernel, scale, pieces), out_shape=...  12.6 us
    ppermute x2, waiting for transfers between devices, swap_near(): lax.ppermute(x, axis, [(i, i ^ 1) for i in range(lax.axis_size(axis))])  6.72 us
    ppermute x6, starting transfers between devices, exchange(): lax.ppermute(parts[k], 'depth', [(i, i ^ k) for i in range(pieces)])  5.89 us
    ppermute x2, starting transfers between devices, swap_near(): lax.ppermute(x, axis, [(i, i ^ 1) for i in range(lax.axis_size(axis))])  3.13 us
    ppermute x6, waiting for transfers between devices, exchange(): lax.ppermute(parts[k], 'depth', [(i, i ^ k) for i in range(pieces)])  2.46 us
  transfers between devices with their start and end apart: 10, of which 3 were waited for; matrix products, arithmetic and copies ran while one was open for 0% of the time, Pallas kernels for 47%

profile of v3, /device:TPU:0, one launch (start us, length us, event | category | flops | bytes accessed | tf_op | source)
XLA Modules:
  0.0 100.4 jit_solution(5691672014663118902)
XLA Ops:
  0.0 32.9 %take_slices.1 = (f32[2,2,16,2048]{3,2,1,0:T(8,128)}, f32[2,2,16,2048]{3,2,1,0:T(8,128)}) custom-call(s32[1]{0:T(128)} %bitcast.depth_ref, f32[16,16,2048]{2,1,0:T(8,128)} %grade_hbm.5, f32[16,16,2048]{2,1,0:T(8,128)} %amp_hbm.5), custom_call_target="tpu_custom_call" | custom-call | tf_op jit(solution)/shard_map/take_slices/pallas_call | solution.py:333
  32.9 0.5 collective-permute-start
  33.4 0.7 collective-permute-start.1
  34.1 0.0 copy-start
  34.1 0.0 copy-start.1
  34.1 33.0 %take_rows.1 = (f32[2,4,8,2048]{3,2,1,0:T(8,128)}, f32[2,4,8,2048]{3,2,1,0:T(8,128)}) custom-call(s32[1]{0:T(128)} %bitcast.1.lat_ref, f32[16,16,2048]{2,1,0:T(8,128)} %grade_hbm.5, f32[16,16,2048]{2,1,0:T(8,128)} %amp_hbm.5), custom_call_target="tpu_custom_call" | custom-call | tf_op jit(solution)/shard_map/take_rows/pallas_call | solution.py:325
  67.2 2.6 %collective-permute-start.5 = (f32[2,4,8,2048]{3,2,1,0:T(8,128)}, f32[2,4,8,2048]{3,2,1,0:T(8,128)S(1)}, u32[]{:S(2)}, u32[]{:S(2)}) collective-permute-start(f32[2,4,8,2048]{3,2,1,0:T(8,128)} %get-tuple-element.25), channel_id=1, source_target_pairs={{0,4},{4,0},{8,12},{12,8},{16,20},{20,16},{24,28},{28,24},{1,5},{5... | collective-permute-start | bytes 1572872 | tf_op jit(solution)/shard_map/ppermute | solution.py:300
  69.8 0.7 collective-permute-start.6
  70.5 0.0 collective-permute-done.near_hbm
  70.5 0.0 collective-permute-done.1.far_hbm
  70.5 0.0 copy-done
  70.5 0.0 copy-done.1
  70.5 12.6 %march.1 = (f32[4,16,512]{2,1,0:T(8,128)S(1)}, f32[4,16,512]{2,1,0:T(8,128)S(1)}, f32[4,16,512]{2,1,0:T(8,128)S(1)}, f32[4,16,512]{2,1,0:T(8,128)S(1)}, f32[8,16,9,8,128]{4,3,2,1,0:T(8,128)S(1)}) custom-call(s32[2,2,8]{2,1,0:T(2,128)S(1)} %copy-done, s32[1]{0:T(128)} %bitcast.depth_ref, f32[16,16,2048]{2,1,0:T(8,128)} %grade_hbm.5, f32[16,16,2048]{2,1,0:T(8,128)} %amp_hbm.5, ...), custom_call_target="tpu_custom_call" | custom-call | tf_op jit(solution)/shard_map/march/pallas_call | solution.py:349
  83.1 0.1 collective-permute-start.2
  83.1 0.1 collective-permute-start.3
  83.2 1.8 %collective-permute-start.4 = (f32[4,16,512]{2,1,0:T(8,128)S(1)}, f32[4,16,512]{2,1,0:T(8,128)S(1)}, u32[]{:S(2)}, u32[]{:S(2)}) collective-permute-start(f32[4,16,512]{2,1,0:T(8,128)S(1)} %get-tuple-element.23), channel_id=1, source_target_pairs={{0,3},{1,2},{2,1},{3,0},{4,7},{5,6},{6,5},{7,4},{8,11},{9,10},{10,... | collective-permute-start | bytes 393224 | tf_op jit(solution)/shard_map/ppermute | solution.py:368
  85.0 6.7 %collective-permute-done.5.pair_ref = f32[2,4,8,2048]{3,2,1,0:T(8,128)S(1)} collective-permute-done((f32[2,4,8,2048]{3,2,1,0:T(8,128)}, f32[2,4,8,2048]{3,2,1,0:T(8,128)S(1)}, u32[]{:S(2)}, u32[]{:S(2)}) %collective-permute-start.5) | collective-permute-done | bytes 524320 | tf_op jit(solution)/shard_map/ppermute | solution.py:300
  91.7 0.0 collective-permute-done.6.cross_ref
  91.7 1.5 %edges.1 = (f32[4,8,256]{2,1,0:T(8,128)S(1)}, f32[4,8,256]{2,1,0:T(8,128)S(1)}, f32[4,8,256]{2,1,0:T(8,128)S(1)}, f32[4,8,256]{2,1,0:T(8,128)S(1)}) custom-call(s32[2,2,8]{2,1,0:T(2,128)S(1)} %copy-done, s32[1]{0:T(128)} %bitcast.depth_ref, s32[1]{0:T(128)} %bitcast.1.lat_ref, f32[8,16,9,8,128]{4,3,2,1,0:T(8,128)S(1)} %get-tuple-element.24.kept_ref, ...), custom_call_target="tpu_custom_call" | custom-call | tf_op jit(solution)/shard_map/edges/pallas_call | solution.py:373
  93.3 2.1 %collective-permute-start.7 = (f32[4,8,256]{2,1,0:T(8,128)S(1)}, f32[4,8,256]{2,1,0:T(8,128)S(1)}, u32[]{:S(2)}, u32[]{:S(2)}) collective-permute-start(f32[4,8,256]{2,1,0:T(8,128)S(1)} %get-tuple-element.28), channel_id=1, source_target_pairs={{0,1},{1,0},{2,3},{3,2},{4,5},{5,4},{6,7},{7,6},{8,9},{9,8},{10,11... | collective-permute-start | bytes 98312 | tf_op jit(solution)/shard_map/ppermute | solution.py:368
  95.4 1.0 collective-permute-start.8
  96.4 0.0 collective-permute-done.7.refs_5_
  96.4 0.9 collective-permute-start.9
  97.2 2.0 %collective-permute-done.8.refs_6_ = f32[4,8,256]{2,1,0:T(8,128)S(1)} collective-permute-done((f32[4,8,256]{2,1,0:T(8,128)S(1)}, f32[4,8,256]{2,1,0:T(8,128)S(1)}, u32[]{:S(2)}, u32[]{:S(2)}) %collective-permute-start.8) | collective-permute-done | bytes 32800 | tf_op jit(solution)/shard_map/ppermute | solution.py:368
  99.3 0.4 collective-permute-done.9.refs_7_
  99.7 0.0 collective-permute-done.2.refs_1_
  99.7 0.0 collective-permute-done.3.refs_2_
  99.7 0.0 collective-permute-done.4.refs_3_
  99.7 0.7 finish.1
Async XLA Ops:
  32.9 37.6 %collective-permute-start = (f32[2,2,16,2048]{3,2,1,0:T(8,128)}, f32[2,2,16,2048]{3,2,1,0:T(8,128)S(1)}, u32[]{:S(2)}, u32[]{:S(2)}) collective-permute-start(f32[2,2,16,2048]{3,2,1,0:T(8,128)} %get-tuple-element.18), channel_id=1, source_target_pairs={{0,1},{1,0},{2,3},{3,2},{4,5},{5,4},{6,7},{7,6},{8,9},{9,8},{10,11... | collective-permute-start | bytes 1572872 | tf_op jit(solution)/shard_map/ppermute | solution.py:300
  33.4 37.1 %collective-permute-start.1 = (f32[2,2,16,2048]{3,2,1,0:T(8,128)}, f32[2,2,16,2048]{3,2,1,0:T(8,128)S(1)}, u32[]{:S(2)}, u32[]{:S(2)}) collective-permute-start(f32[2,2,16,2048]{3,2,1,0:T(8,128)} %get-tuple-element.19), channel_id=1, source_target_pairs={{1,2},{2,1},{5,6},{6,5},{9,10},{10,9},{13,14},{14,13},{17,18},{18,... | collective-permute-start | bytes 1572872 | tf_op jit(solution)/shard_map/ppermute | solution.py:305
  34.1 36.4 %copy-start = (s32[2,2,8]{2,1,0:T(2,128)S(1)}, s32[2,2,8]{2,1,0:T(2,128)}, u32[]{:S(2)}) copy-start(s32[2,2,8]{2,1,0:T(2,128)} %mask_ref.3) | copy-start | bytes 388
  34.1 36.4 %copy-start.1 = (s32[4,128]{1,0:T(4,128)S(1)}, s32[4,128]{1,0:T(4,128)}, u32[]{:S(2)}) copy-start(s32[4,128]{1,0:T(4,128)} %table_ref.1) | copy-start | bytes 6148
  67.2 24.6 %collective-permute-start.5 = (f32[2,4,8,2048]{3,2,1,0:T(8,128)}, f32[2,4,8,2048]{3,2,1,0:T(8,128)S(1)}, u32[]{:S(2)}, u32[]{:S(2)}) collective-permute-start(f32[2,4,8,2048]{3,2,1,0:T(8,128)} %get-tuple-element.25), channel_id=1, source_target_pairs={{0,4},{4,0},{8,12},{12,8},{16,20},{20,16},{24,28},{28,24},{1,5},{5... | collective-permute-start | bytes 1572872 | tf_op jit(solution)/shard_map/ppermute | solution.py:300
  69.8 22.0 %collective-permute-start.6 = (f32[2,4,8,2048]{3,2,1,0:T(8,128)}, f32[2,4,8,2048]{3,2,1,0:T(8,128)S(1)}, u32[]{:S(2)}, u32[]{:S(2)}) collective-permute-start(f32[2,4,8,2048]{3,2,1,0:T(8,128)} %get-tuple-element.26), channel_id=1, source_target_pairs={{4,8},{8,4},{12,16},{16,12},{20,24},{24,20},{5,9},{9,5},{13,17},{1... | collective-permute-start | bytes 1572872 | tf_op jit(solution)/shard_map/ppermute | solution.py:305
  83.1 16.6 %collective-permute-start.2 = (f32[4,16,512]{2,1,0:T(8,128)S(1)}, f32[4,16,512]{2,1,0:T(8,128)S(1)}, u32[]{:S(2)}, u32[]{:S(2)}) collective-permute-start(f32[4,16,512]{2,1,0:T(8,128)S(1)} %get-tuple-element.21), channel_id=1, source_target_pairs={{0,1},{1,0},{2,3},{3,2},{4,5},{5,4},{6,7},{7,6},{8,9},{9,8},{10,11... | collective-permute-start | bytes 393224 | tf_op jit(solution)/shard_map/ppermute | solution.py:368
  83.1 16.6 %collective-permute-start.3 = (f32[4,16,512]{2,1,0:T(8,128)S(1)}, f32[4,16,512]{2,1,0:T(8,128)S(1)}, u32[]{:S(2)}, u32[]{:S(2)}) collective-permute-start(f32[4,16,512]{2,1,0:T(8,128)S(1)} %get-tuple-element.22), channel_id=1, source_target_pairs={{0,2},{1,3},{2,0},{3,1},{4,6},{5,7},{6,4},{7,5},{8,10},{9,11},{10,... | collective-permute-start | bytes 393224 | tf_op jit(solution)/shard_map/ppermute | solution.py:368
  83.2 16.5 %collective-permute-start.4 = (f32[4,16,512]{2,1,0:T(8,128)S(1)}, f32[4,16,512]{2,1,0:T(8,128)S(1)}, u32[]{:S(2)}, u32[]{:S(2)}) collective-permute-start(f32[4,16,512]{2,1,0:T(8,128)S(1)} %get-tuple-element.23), channel_id=1, source_target_pairs={{0,3},{1,2},{2,1},{3,0},{4,7},{5,6},{6,5},{7,4},{8,11},{9,10},{10,... | collective-permute-start | bytes 393224 | tf_op jit(solution)/shard_map/ppermute | solution.py:368
  93.3 3.1 %collective-permute-start.7 = (f32[4,8,256]{2,1,0:T(8,128)S(1)}, f32[4,8,256]{2,1,0:T(8,128)S(1)}, u32[]{:S(2)}, u32[]{:S(2)}) collective-permute-start(f32[4,8,256]{2,1,0:T(8,128)S(1)} %get-tuple-element.28), channel_id=1, source_target_pairs={{0,1},{1,0},{2,3},{3,2},{4,5},{5,4},{6,7},{7,6},{8,9},{9,8},{10,11... | collective-permute-start | bytes 98312 | tf_op jit(solution)/shard_map/ppermute | solution.py:368
  95.4 3.9 %collective-permute-start.8 = (f32[4,8,256]{2,1,0:T(8,128)S(1)}, f32[4,8,256]{2,1,0:T(8,128)S(1)}, u32[]{:S(2)}, u32[]{:S(2)}) collective-permute-start(f32[4,8,256]{2,1,0:T(8,128)S(1)} %get-tuple-element.29), channel_id=1, source_target_pairs={{0,2},{1,3},{2,0},{3,1},{4,6},{5,7},{6,4},{7,5},{8,10},{9,11},{10,... | collective-permute-start | bytes 98312 | tf_op jit(solution)/shard_map/ppermute | solution.py:368
  96.4 3.3 %collective-permute-start.9 = (f32[4,8,256]{2,1,0:T(8,128)S(1)}, f32[4,8,256]{2,1,0:T(8,128)S(1)}, u32[]{:S(2)}, u32[]{:S(2)}) collective-permute-start(f32[4,8,256]{2,1,0:T(8,128)S(1)} %get-tuple-element.30), channel_id=1, source_target_pairs={{0,3},{1,2},{2,1},{3,0},{4,7},{5,6},{6,5},{7,4},{8,11},{9,10},{10,... | collective-permute-start | bytes 98312 | tf_op jit(solution)/shard_map/ppermute | solution.py:368

commit v4 on v3

--- a/solution.py
+++ b/solution.py
@@ -20,20 +20,26 @@
     return lax.broadcasted_iota(jnp.int32, shape, len(shape) - 2)
 
 
-def rows_kernel(lat_ref, grade_hbm, amp_hbm, pair_hbm, cross_hbm, sems):
+def take_kernel(lat_ref, depth_ref, grade_hbm, amp_hbm, pair_ref, cross_ref, near_ref, far_ref, sems, depth_sems):
     slices, rows = grade_hbm.shape[:2]
     span = slices // 4
     even = lax.rem(lat_ref[0], 2) == 0
+    odd = lax.rem(depth_ref[0], 2)
+    fields = (grade_hbm, amp_hbm)
 
     def copies(above_dst, below_dst):
         made = []
-        for f, src in enumerate((grade_hbm, amp_hbm)):
+        for f, src in enumerate(fields):
             for q in range(4):
                 part = src.at[pl.ds(span * q, span)]
                 above = above_dst.at[f, :, pl.ds((0, 6, 4, 2)[q], 2), :]
                 below = below_dst.at[f, :, pl.ds((6, 4, 2, 0)[q], 2), :]
                 made.append(pltpu.make_async_copy(part.at[:, pl.ds(rows - 2, 2), :], above, sems.at[f, q, 0]))
                 made.append(pltpu.make_async_copy(part.at[:, pl.ds(0, 2), :], below, sems.at[f, q, 1]))
+        for f, src in enumerate(fields):
+            for n, (dst, at) in enumerate(((near_ref, 1 - odd), (far_ref, odd))):
+                here = src.at[pl.ds(at * (slices - 2), 2)]
+                made.append(pltpu.make_async_copy(here, dst.at[f], depth_sems.at[f, n]))
         for copy in made:
             copy.start()
         for copy in made:
@@ -41,24 +47,11 @@
 
     @pl.when(even)
     def _():
-        copies(pair_hbm, cross_hbm)
+        copies(pair_ref, cross_ref)
 
     @pl.when(jnp.logical_not(even))
     def _():
-        copies(cross_hbm, pair_hbm)
-
-
-def slices_kernel(depth_ref, grade_hbm, amp_hbm, near_hbm, far_hbm, sems):
-    slices = grade_hbm.shape[0]
-    odd = lax.rem(depth_ref[0], 2)
-    made = []
-    for f, src in enumerate((grade_hbm, amp_hbm)):
-        for n, (dst, at) in enumerate(((near_hbm, 1 - odd), (far_hbm, odd))):
-            made.append(pltpu.make_async_copy(src.at[pl.ds(at * (slices - 2), 2)], dst.at[f], sems.at[f, n]))
-    for copy in made:
-        copy.start()
-    for copy in made:
-        copy.wait()
+        copies(cross_ref, pair_ref)
 
 
 def round_weight(w):
@@ -322,22 +315,15 @@
     hbm_only = pltpu.MemorySpace.HBM
     grade_field = pltpu.with_memory_space_constraint(grade_field, hbm_only)
     amplitude = pltpu.with_memory_space_constraint(amplitude, hbm_only)
-    pair, cross = pl.pallas_call(
-        rows_kernel,
-        out_shape=(lat_halo, lat_halo),
-        in_specs=[smem, hbm, hbm],
-        out_specs=[hbm, hbm],
-        scratch_shapes=[pltpu.SemaphoreType.DMA((2, 4, 2))],
-        name="take_rows",
-    )(lat_rank, grade_field, amplitude)
-    near, far = pl.pallas_call(
-        slices_kernel,
-        out_shape=(depth_halo, depth_halo),
-        in_specs=[smem, hbm, hbm],
-        out_specs=[hbm, hbm],
-        scratch_shapes=[pltpu.SemaphoreType.DMA((2, 2))],
-        name="take_slices",
-    )(depth_rank, grade_field, amplitude)
+    pair, cross, near, far = pl.pallas_call(
+        take_kernel,
+        out_shape=(lat_halo, lat_halo, depth_halo, depth_halo),
+        in_specs=[smem, smem, hbm, hbm],
+        out_specs=[vmem] * 4,
+        scratch_shapes=[pltpu.SemaphoreType.DMA((2, 4, 2)), pltpu.SemaphoreType.DMA((2, 2))],
+        compiler_params=pltpu.CompilerParams(vmem_limit_bytes=8 << 20),
+        name="take",
+    )(lat_rank, depth_rank, grade_field, amplitude)
     pair = swap_near(pair, "lat")
     cross = swap_far(cross, "lat")
     near = swap_near(near, "depth")

time: 101 us -> 36.3 us (0.36)
  Pallas kernels: 80.7 us -> 13.3 us
  starting transfers between devices: 10.4 us -> 18.8 us
  waiting for transfers between devices: 9.18 us -> 3.73 us
    pallas_call x2 -> x1, Pallas kernels: 65.9 us -> 1.82 us  [local(): pl.pallas_call(take_kernel, out_shape=(lat_halo, lat_halo, depth_halo, de...]
    ppermute x6, starting transfers between devices: 5.89 us -> 14.3 us  [exchange(): lax.ppermute(parts[k], 'depth', [(i, i ^ k) for i in range(pieces)])]
    ppermute x2, waiting for transfers between devices: 6.72 us -> 1.27 us  [swap_near(): lax.ppermute(x, axis, [(i, i ^ 1) for i in range(lax.axis_size(axis))])]
    pallas_call x1, Pallas kernels: 12.6 us -> 9.24 us  [local(): pl.pallas_call(functools.partial(march_kernel, scale, pieces), out_shape=...]
  transfers between devices with their start and end apart: 10 -> 10, of which waited for: 3 -> 3; matrix products, arithmetic and copies ran while one was open for 0% -> 0% of each run, Pallas kernels for 47% -> 30%
where the time goes in v4:
time: 36.3 us; the launch traced here: 36 us
  starting transfers between devices  18.8 us (52%)
  Pallas kernels  13.3 us (37%)
  waiting for transfers between devices  3.73 us (10%)
    ppermute x6, starting transfers between devices, exchange(): lax.ppermute(parts[k], 'depth', [(i, i ^ k) for i in range(pieces)])  14.3 us
    pallas_call x1, Pallas kernels, local(): pl.pallas_call(functools.partial(march_kernel, scale, pieces), out_shape=...  9.24 us
    ppermute x2, starting transfers between devices, swap_near(): lax.ppermute(x, axis, [(i, i ^ 1) for i in range(lax.axis_size(axis))])  3.13 us
    ppermute x6, waiting for transfers between devices, exchange(): lax.ppermute(parts[k], 'depth', [(i, i ^ k) for i in range(pieces)])  2.46 us
    pallas_call x1, Pallas kernels, local(): pl.pallas_call(take_kernel, out_shape=(lat_halo, lat_halo, depth_halo, de...  1.82 us
    pallas_call x1, Pallas kernels, local(): pl.pallas_call(functools.partial(edge_kernel, pieces), out_shape=(rim,) *...  1.54 us
    ppermute x2, starting transfers between devices, swap_far(): lax.ppermute(x, axis, [(i, j) for k in range(1, size - 1, 2) for i, j in...  1.36 us
    ppermute x2, waiting for transfers between devices, swap_near(): lax.ppermute(x, axis, [(i, i ^ 1) for i in range(lax.axis_size(axis))])  1.27 us
  transfers between devices with their start and end apart: 10, of which 3 were waited for; matrix products, arithmetic and copies ran while one was open for 0% of the time, Pallas kernels for 30%

profile of v4, /device:TPU:0, one launch (start us, length us, event | category | flops | bytes accessed | tf_op | source)
XLA Modules:
  0.0 36.0 jit_solution(12591686799600413796)
XLA Ops:
  0.0 0.0 copy-start
  0.0 0.0 copy-start.1
  0.0 1.8 %take.1 = (f32[2,4,8,2048]{3,2,1,0:T(8,128)S(1)}, f32[2,4,8,2048]{3,2,1,0:T(8,128)S(1)}, f32[2,2,16,2048]{3,2,1,0:T(8,128)S(1)}, f32[2,2,16,2048]{3,2,1,0:T(8,128)S(1)}) custom-call(s32[1]{0:T(128)} %bitcast.1.lat_ref, s32[1]{0:T(128)} %bitcast.depth_ref, f32[16,16,2048]{2,1,0:T(8,128)} %grade_hbm.3, f32[16,16,2048]{2,1,0:T(8,128)} %amp_hbm.3), custom_call_target="tpu_custom_call" | custom-call | tf_op jit(solution)/shard_map/take/pallas_call | solution.py:318
  1.8 0.5 %collective-permute-start = (f32[2,2,16,2048]{3,2,1,0:T(8,128)S(1)}, f32[2,2,16,2048]{3,2,1,0:T(8,128)S(1)}, u32[]{:S(2)}, u32[]{:S(2)}) collective-permute-start(f32[2,2,16,2048]{3,2,1,0:T(8,128)S(1)} %get-tuple-element.18), channel_id=1, source_target_pairs={{0,1},{1,0},{2,3},{3,2},{4,5},{5,4},{6,7},{7,6},{8,9},{9,8},{10,11... | collective-permute-start | bytes 1572872 | tf_op jit(solution)/shard_map/ppermute | solution.py:293
  2.4 0.7 %collective-permute-start.1 = (f32[2,2,16,2048]{3,2,1,0:T(8,128)S(1)}, f32[2,2,16,2048]{3,2,1,0:T(8,128)S(1)}, u32[]{:S(2)}, u32[]{:S(2)}) collective-permute-start(f32[2,2,16,2048]{3,2,1,0:T(8,128)S(1)} %get-tuple-element.19), channel_id=1, source_target_pairs={{1,2},{2,1},{5,6},{6,5},{9,10},{10,9},{13,14},{14,13},{17,18},{18,... | collective-permute-start | bytes 1572872 | tf_op jit(solution)/shard_map/ppermute | solution.py:298
  3.0 2.6 %collective-permute-start.5 = (f32[2,4,8,2048]{3,2,1,0:T(8,128)S(1)}, f32[2,4,8,2048]{3,2,1,0:T(8,128)S(1)}, u32[]{:S(2)}, u32[]{:S(2)}) collective-permute-start(f32[2,4,8,2048]{3,2,1,0:T(8,128)S(1)} %get-tuple-element.25), channel_id=1, source_target_pairs={{0,4},{4,0},{8,12},{12,8},{16,20},{20,16},{24,28},{28,24},{1,5},{5... | collective-permute-start | bytes 1572872 | tf_op jit(solution)/shard_map/ppermute | solution.py:293
  5.7 0.7 %collective-permute-start.6 = (f32[2,4,8,2048]{3,2,1,0:T(8,128)S(1)}, f32[2,4,8,2048]{3,2,1,0:T(8,128)S(1)}, u32[]{:S(2)}, u32[]{:S(2)}) collective-permute-start(f32[2,4,8,2048]{3,2,1,0:T(8,128)S(1)} %get-tuple-element.26), channel_id=1, source_target_pairs={{4,8},{8,4},{12,16},{16,12},{20,24},{24,20},{5,9},{9,5},{13,17},{1... | collective-permute-start | bytes 1572872 | tf_op jit(solution)/shard_map/ppermute | solution.py:298
  6.3 0.0 collective-permute-done.near_hbm
  6.4 0.0 collective-permute-done.1.far_hbm
  6.4 0.0 copy-done
  6.4 0.0 copy-done.1
  6.4 9.2 %march.1 = (f32[4,16,512]{2,1,0:T(8,128)S(1)}, f32[4,16,512]{2,1,0:T(8,128)S(1)}, f32[4,16,512]{2,1,0:T(8,128)S(1)}, f32[4,16,512]{2,1,0:T(8,128)S(1)}, f32[8,16,9,8,128]{4,3,2,1,0:T(8,128)S(1)}) custom-call(s32[2,2,8]{2,1,0:T(2,128)S(1)} %copy-done, s32[1]{0:T(128)} %bitcast.depth_ref, f32[16,16,2048]{2,1,0:T(8,128)} %grade_hbm.3, f32[16,16,2048]{2,1,0:T(8,128)} %amp_hbm.3, ...), custom_call_target="tpu_custom_call" | custom-call | tf_op jit(solution)/shard_map/march/pallas_call | solution.py:335
  15.6 9.0 %collective-permute-start.2 = (f32[4,16,512]{2,1,0:T(8,128)S(1)}, f32[4,16,512]{2,1,0:T(8,128)S(1)}, u32[]{:S(2)}, u32[]{:S(2)}) collective-permute-start(f32[4,16,512]{2,1,0:T(8,128)S(1)} %get-tuple-element.21), channel_id=1, source_target_pairs={{0,1},{1,0},{2,3},{3,2},{4,5},{5,4},{6,7},{7,6},{8,9},{9,8},{10,11... | collective-permute-start | bytes 393224 | tf_op jit(solution)/shard_map/ppermute | solution.py:354
  24.6 0.0 collective-permute-start.3
  24.6 1.4 %collective-permute-start.4 = (f32[4,16,512]{2,1,0:T(8,128)S(1)}, f32[4,16,512]{2,1,0:T(8,128)S(1)}, u32[]{:S(2)}, u32[]{:S(2)}) collective-permute-start(f32[4,16,512]{2,1,0:T(8,128)S(1)} %get-tuple-element.23), channel_id=1, source_target_pairs={{0,3},{1,2},{2,1},{3,0},{4,7},{5,6},{6,5},{7,4},{8,11},{9,10},{10,... | collective-permute-start | bytes 393224 | tf_op jit(solution)/shard_map/ppermute | solution.py:354
  26.0 1.3 %collective-permute-done.5.pair_ref = f32[2,4,8,2048]{3,2,1,0:T(8,128)S(1)} collective-permute-done((f32[2,4,8,2048]{3,2,1,0:T(8,128)S(1)}, f32[2,4,8,2048]{3,2,1,0:T(8,128)S(1)}, u32[]{:S(2)}, u32[]{:S(2)}) %collective-permute-start.5) | collective-permute-done | bytes 524320 | tf_op jit(solution)/shard_map/ppermute | solution.py:293
  27.3 0.0 collective-permute-done.6.cross_ref
  27.3 1.5 %edges.1 = (f32[4,8,256]{2,1,0:T(8,128)S(1)}, f32[4,8,256]{2,1,0:T(8,128)S(1)}, f32[4,8,256]{2,1,0:T(8,128)S(1)}, f32[4,8,256]{2,1,0:T(8,128)S(1)}) custom-call(s32[2,2,8]{2,1,0:T(2,128)S(1)} %copy-done, s32[1]{0:T(128)} %bitcast.depth_ref, s32[1]{0:T(128)} %bitcast.1.lat_ref, f32[8,16,9,8,128]{4,3,2,1,0:T(8,128)S(1)} %get-tuple-element.24.kept_ref, ...), custom_call_target="tpu_custom_call" | custom-call | tf_op jit(solution)/shard_map/edges/pallas_call | solution.py:359
  28.8 2.1 %collective-permute-start.7 = (f32[4,8,256]{2,1,0:T(8,128)S(1)}, f32[4,8,256]{2,1,0:T(8,128)S(1)}, u32[]{:S(2)}, u32[]{:S(2)}) collective-permute-start(f32[4,8,256]{2,1,0:T(8,128)S(1)} %get-tuple-element.28), channel_id=1, source_target_pairs={{0,1},{1,0},{2,3},{3,2},{4,5},{5,4},{6,7},{7,6},{8,9},{9,8},{10,11... | collective-permute-start | bytes 98312 | tf_op jit(solution)/shard_map/ppermute | solution.py:354
  30.9 1.0 %collective-permute-start.8 = (f32[4,8,256]{2,1,0:T(8,128)S(1)}, f32[4,8,256]{2,1,0:T(8,128)S(1)}, u32[]{:S(2)}, u32[]{:S(2)}) collective-permute-start(f32[4,8,256]{2,1,0:T(8,128)S(1)} %get-tuple-element.29), channel_id=1, source_target_pairs={{0,2},{1,3},{2,0},{3,1},{4,6},{5,7},{6,4},{7,5},{8,10},{9,11},{10,... | collective-permute-start | bytes 98312 | tf_op jit(solution)/shard_map/ppermute | solution.py:354
  31.9 0.0 collective-permute-done.7.refs_5_
  31.9 0.9 %collective-permute-start.9 = (f32[4,8,256]{2,1,0:T(8,128)S(1)}, f32[4,8,256]{2,1,0:T(8,128)S(1)}, u32[]{:S(2)}, u32[]{:S(2)}) collective-permute-start(f32[4,8,256]{2,1,0:T(8,128)S(1)} %get-tuple-element.30), channel_id=1, source_target_pairs={{0,3},{1,2},{2,1},{3,0},{4,7},{5,6},{6,5},{7,4},{8,11},{9,10},{10,... | collective-permute-start | bytes 98312 | tf_op jit(solution)/shard_map/ppermute | solution.py:354
  32.8 2.0 %collective-permute-done.8.refs_6_ = f32[4,8,256]{2,1,0:T(8,128)S(1)} collective-permute-done((f32[4,8,256]{2,1,0:T(8,128)S(1)}, f32[4,8,256]{2,1,0:T(8,128)S(1)}, u32[]{:S(2)}, u32[]{:S(2)}) %collective-permute-start.8) | collective-permute-done | bytes 32800 | tf_op jit(solution)/shard_map/ppermute | solution.py:354
  34.9 0.4 %collective-permute-done.9.refs_7_ = f32[4,8,256]{2,1,0:T(8,128)S(1)} collective-permute-done((f32[4,8,256]{2,1,0:T(8,128)S(1)}, f32[4,8,256]{2,1,0:T(8,128)S(1)}, u32[]{:S(2)}, u32[]{:S(2)}) %collective-permute-start.9) | collective-permute-done | bytes 32800 | tf_op jit(solution)/shard_map/ppermute | solution.py:354
  35.3 0.0 collective-permute-done.2.refs_1_
  35.3 0.0 collective-permute-done.3.refs_2_
  35.3 0.0 collective-permute-done.4.refs_3_
  35.3 0.7 %finish.1 = f32[4,16,512]{2,1,0:T(8,128)} custom-call(s32[1]{0:T(128)} %bitcast.depth_ref, f32[4,16,512]{2,1,0:T(8,128)S(1)} %get-tuple-element.20.refs_0_, f32[4,16,512]{2,1,0:T(8,128)S(1)} %collective-permute-done.2.refs_1_, f32[4,16,512]{2,1,0:T(8,128)S(1)} %collective-permute-done.3.refs_2_, f32[4,16,512]{2,1,0:T(8,128)S(1)} %collective-permute-done.4.refs_3_, ...), custom_call_target="tpu_custom_call" | custom-call | tf_op jit(solution)/shard_map/finish/pallas_call | solution.py:368
Async XLA Ops:
  0.0 6.4 %copy-start = (s32[2,2,8]{2,1,0:T(2,128)S(1)}, s32[2,2,8]{2,1,0:T(2,128)}, u32[]{:S(2)}) copy-start(s32[2,2,8]{2,1,0:T(2,128)} %mask_ref.3) | copy-start | bytes 388
  0.0 6.4 %copy-start.1 = (s32[4,128]{1,0:T(4,128)S(1)}, s32[4,128]{1,0:T(4,128)}, u32[]{:S(2)}) copy-start(s32[4,128]{1,0:T(4,128)} %table_ref.1) | copy-start | bytes 6148
  1.8 4.5 %collective-permute-start = (f32[2,2,16,2048]{3,2,1,0:T(8,128)S(1)}, f32[2,2,16,2048]{3,2,1,0:T(8,128)S(1)}, u32[]{:S(2)}, u32[]{:S(2)}) collective-permute-start(f32[2,2,16,2048]{3,2,1,0:T(8,128)S(1)} %get-tuple-element.18), channel_id=1, source_target_pairs={{0,1},{1,0},{2,3},{3,2},{4,5},{5,4},{6,7},{7,6},{8,9},{9,8},{10,11... | collective-permute-start | bytes 1572872 | tf_op jit(solution)/shard_map/ppermute | solution.py:293
  2.4 4.0 %collective-permute-start.1 = (f32[2,2,16,2048]{3,2,1,0:T(8,128)S(1)}, f32[2,2,16,2048]{3,2,1,0:T(8,128)S(1)}, u32[]{:S(2)}, u32[]{:S(2)}) collective-permute-start(f32[2,2,16,2048]{3,2,1,0:T(8,128)S(1)} %get-tuple-element.19), channel_id=1, source_target_pairs={{1,2},{2,1},{5,6},{6,5},{9,10},{10,9},{13,14},{14,13},{17,18},{18,... | collective-permute-start | bytes 1572872 | tf_op jit(solution)/shard_map/ppermute | solution.py:298
  3.0 24.2 %collective-permute-start.5 = (f32[2,4,8,2048]{3,2,1,0:T(8,128)S(1)}, f32[2,4,8,2048]{3,2,1,0:T(8,128)S(1)}, u32[]{:S(2)}, u32[]{:S(2)}) collective-permute-start(f32[2,4,8,2048]{3,2,1,0:T(8,128)S(1)} %get-tuple-element.25), channel_id=1, source_target_pairs={{0,4},{4,0},{8,12},{12,8},{16,20},{20,16},{24,28},{28,24},{1,5},{5... | collective-permute-start | bytes 1572872 | tf_op jit(solution)/shard_map/ppermute | solution.py:293
  5.7 21.6 %collective-permute-start.6 = (f32[2,4,8,2048]{3,2,1,0:T(8,128)S(1)}, f32[2,4,8,2048]{3,2,1,0:T(8,128)S(1)}, u32[]{:S(2)}, u32[]{:S(2)}) collective-permute-start(f32[2,4,8,2048]{3,2,1,0:T(8,128)S(1)} %get-tuple-element.26), channel_id=1, source_target_pairs={{4,8},{8,4},{12,16},{16,12},{20,24},{24,20},{5,9},{9,5},{13,17},{1... | collective-permute-start | bytes 1572872 | tf_op jit(solution)/shard_map/ppermute | solution.py:298
  15.6 19.6 %collective-permute-start.2 = (f32[4,16,512]{2,1,0:T(8,128)S(1)}, f32[4,16,512]{2,1,0:T(8,128)S(1)}, u32[]{:S(2)}, u32[]{:S(2)}) collective-permute-start(f32[4,16,512]{2,1,0:T(8,128)S(1)} %get-tuple-element.21), channel_id=1, source_target_pairs={{0,1},{1,0},{2,3},{3,2},{4,5},{5,4},{6,7},{7,6},{8,9},{9,8},{10,11... | collective-permute-start | bytes 393224 | tf_op jit(solution)/shard_map/ppermute | solution.py:354
  24.6 10.7 %collective-permute-start.3 = (f32[4,16,512]{2,1,0:T(8,128)S(1)}, f32[4,16,512]{2,1,0:T(8,128)S(1)}, u32[]{:S(2)}, u32[]{:S(2)}) collective-permute-start(f32[4,16,512]{2,1,0:T(8,128)S(1)} %get-tuple-element.22), channel_id=1, source_target_pairs={{0,2},{1,3},{2,0},{3,1},{4,6},{5,7},{6,4},{7,5},{8,10},{9,11},{10,... | collective-permute-start | bytes 393224 | tf_op jit(solution)/shard_map/ppermute | solution.py:354
  24.6 10.7 %collective-permute-start.4 = (f32[4,16,512]{2,1,0:T(8,128)S(1)}, f32[4,16,512]{2,1,0:T(8,128)S(1)}, u32[]{:S(2)}, u32[]{:S(2)}) collective-permute-start(f32[4,16,512]{2,1,0:T(8,128)S(1)} %get-tuple-element.23), channel_id=1, source_target_pairs={{0,3},{1,2},{2,1},{3,0},{4,7},{5,6},{6,5},{7,4},{8,11},{9,10},{10,... | collective-permute-start | bytes 393224 | tf_op jit(solution)/shard_map/ppermute | solution.py:354
  28.8 3.1 %collective-permute-start.7 = (f32[4,8,256]{2,1,0:T(8,128)S(1)}, f32[4,8,256]{2,1,0:T(8,128)S(1)}, u32[]{:S(2)}, u32[]{:S(2)}) collective-permute-start(f32[4,8,256]{2,1,0:T(8,128)S(1)} %get-tuple-element.28), channel_id=1, source_target_pairs={{0,1},{1,0},{2,3},{3,2},{4,5},{5,4},{6,7},{7,6},{8,9},{9,8},{10,11... | collective-permute-start | bytes 98312 | tf_op jit(solution)/shard_map/ppermute | solution.py:354
  30.9 3.9 %collective-permute-start.8 = (f32[4,8,256]{2,1,0:T(8,128)S(1)}, f32[4,8,256]{2,1,0:T(8,128)S(1)}, u32[]{:S(2)}, u32[]{:S(2)}) collective-permute-start(f32[4,8,256]{2,1,0:T(8,128)S(1)} %get-tuple-element.29), channel_id=1, source_target_pairs={{0,2},{1,3},{2,0},{3,1},{4,6},{5,7},{6,4},{7,5},{8,10},{9,11},{10,... | collective-permute-start | bytes 98312 | tf_op jit(solution)/shard_map/ppermute | solution.py:354
  31.9 3.3 %collective-permute-start.9 = (f32[4,8,256]{2,1,0:T(8,128)S(1)}, f32[4,8,256]{2,1,0:T(8,128)S(1)}, u32[]{:S(2)}, u32[]{:S(2)}) collective-permute-start(f32[4,8,256]{2,1,0:T(8,128)S(1)} %get-tuple-element.30), channel_id=1, source_target_pairs={{0,3},{1,2},{2,1},{3,0},{4,7},{5,6},{6,5},{7,4},{8,11},{9,10},{10,... | collective-permute-start | bytes 98312 | tf_op jit(solution)/shard_map/ppermute | solution.py:354

commit v5 on v4

v5 whole, which is shorter than its diff:
```python
import functools

import jax
import jax.numpy as jnp
from jax import lax
from jax.experimental import pallas as pl
from jax.experimental.pallas import tpu as pltpu
from jax.sharding import PartitionSpec as P

MZ = 8
MX = 8
MY = 256
LANES = 128
SUB = 8
TERMS = 9


def sublane(shape):
    return lax.broadcasted_iota(jnp.int32, shape, len(shape) - 2)


def take_kernel(lat_ref, depth_ref, grade_hbm, amp_hbm, pair_ref, cross_ref, near_ref, far_ref, sems, depth_sems):
    slices, rows = grade_hbm.shape[:2]
    span = slices // 4
    even = lax.rem(lat_ref[0], 2) == 0
    odd = lax.rem(depth_ref[0], 2)
    fields = (grade_hbm, amp_hbm)

    def copies(above_dst, below_dst):
        made = []
        for f, src in enumerate(fields):
            for q in range(4):
                part = src.at[pl.ds(span * q, span)]
                above = above_dst.at[f, :, pl.ds((0, 6, 4, 2)[q], 2), :]
                below = below_dst.at[f, :, pl.ds((6, 4, 2, 0)[q], 2), :]
                made.append(pltpu.make_async_copy(part.at[:, pl.ds(rows - 2, 2), :], above, sems.at[f, q, 0]))
                made.append(pltpu.make_async_copy(part.at[:, pl.ds(0, 2), :], below, sems.at[f, q, 1]))
        for f, src in enumerate(fields):
            for n, (dst, at) in enumerate(((near_ref, 1 - odd), (far_ref, odd))):
                here = src.at[pl.ds(at * (slices - 2), 2)]
                made.append(pltpu.make_async_copy(here, dst.at[f], depth_sems.at[f, n]))
        for copy in made:
            copy.start()
        for copy in made:
            copy.wait()

    @pl.when(even)
    def _():
        copies(pair_ref, cross_ref)

    @pl.when(jnp.logical_not(even))
    def _():
        copies(cross_ref, pair_ref)


def round_weight(w):
    return w.astype(jnp.bfloat16).astype(jnp.float32)


def stencil(m2, m1, p1, p2):
    return (m2 - p2) + 8.0 * (p1 - m1)


def fill_tables(scale, table_ref, low_ref, high_ref):
    bins = table_ref.shape[1]
    table = (table_ref[...].astype(jnp.float32) / 65535.0).astype(jnp.bfloat16).astype(jnp.float32)
    table = jnp.where(sublane(table.shape) == 3, table * scale, table)
    column = lax.broadcasted_iota(jnp.int32, table.shape, 1)
    following = jnp.where(column == bins - 1, 0.0, pltpu.roll(table, bins - 1, 1))
    for c in range(4):
        low_ref[c] = jnp.broadcast_to(table[c:c + 1, :], (SUB, bins))
        high_ref[c] = jnp.broadcast_to(following[c:c + 1, :], (SUB, bins))


class Field:
    def __init__(self, ref, slices, strips, s):
        self.ref, self.strips = ref, strips
        self.per_slice = ref.shape[0] // slices
        self.s = s

    def load(self, z, rt, ds=0, k=0):
        start = pl.multiple_of((self.s + ds) * SUB, SUB) + (z * self.per_slice + rt * self.strips * SUB + k)
        return self.ref[pl.ds(start, SUB), :]

    def columns(self, z, rt, mid, lane):
        left = jnp.where(self.s > 0, self.load(z, rt, -jnp.minimum(self.s, 1)), 0.0)
        right = jnp.where(self.s < self.strips - 1, self.load(z, rt, jnp.minimum(self.strips - 1 - self.s, 1)), 0.0)
        return stencil(
            pltpu.roll(jnp.where(lane >= LANES - 2, left, mid), 2, 1),
            pltpu.roll(jnp.where(lane >= LANES - 1, left, mid), 1, 1),
            pltpu.roll(jnp.where(lane < 1, right, mid), LANES - 1, 1),
            pltpu.roll(jnp.where(lane < 2, right, mid), LANES - 2, 1),
        )

    def rows(self, z, rt, mid, sub, roll):
        def shifted(k):
            if k > 0:
                inside = sub < SUB - k
                if rt == 0:
                    return jnp.where(inside, self.load(z, 0, 0, k), self.load(z, 1, 0, k - SUB))
                return jnp.where(inside, pltpu.roll(mid, SUB - k, 0) if roll else self.load(z, 1, 0, k), 0.0)
            inside = sub >= -k
            if rt == 1:
                return jnp.where(inside, self.load(z, 1, 0, k), self.load(z, 0, 0, SUB + k))
            return jnp.where(inside, pltpu.roll(mid, -k, 0) if roll else self.load(z, 0, 0, k), 0.0)

        return stencil(*(shifted(k) for k in (-2, -1, 1, 2)))


def classify(grade, bins, low_ref, high_ref):
    position = grade * (bins - 1.0)
    index = jnp.minimum(position.astype(jnp.int32), bins - 1)
    w_low = 1.0 - (position - index.astype(jnp.float32))
    w_high = round_weight(1.0 - w_low)
    w_low = round_weight(w_low)

    def gather(ref, c):
        return jnp.take_along_axis(ref[c], index, axis=1)

    return [w_low * gather(low_ref, c) + w_high * gather(high_ref, c) for c in range(4)]


def step(state, terms):
    red, green, blue, trans = state
    g_x, a_x, g_yz, a_yz, steep, *cls = terms
    edge = 1.0 - 12.0 * lax.rsqrt(a_x * a_x + a_yz)
    shade = 0.3 + steep * lax.rsqrt(g_x * g_x + g_yz)
    weight = trans * (cls[3] * edge)
    trans = trans - weight
    weight = weight * shade
    return (red + weight * cls[0], green + weight * cls[1], blue + weight * cls[2], trans)


def cell_terms(fields, z, rt, along, roll, bins, low_ref, high_ref):
    lane = lax.broadcasted_iota(jnp.int32, (SUB, LANES), 1)
    sub = sublane((SUB, LANES))
    parts = []
    for field, near in zip(fields, along):
        mid = field.load(z, rt)
        dy = field.columns(z, rt, mid, lane)
        dz = stencil(*near)
        parts.append((mid, field.rows(z, rt, mid, sub, roll), dy * dy + dz * dz, dz))
    (grade, g_x, g_yz, g_z), (_, a_x, a_yz, _) = parts
    cls = classify(grade, bins, low_ref, high_ref)
    return (g_x, a_x, g_yz + 36.0, a_yz + 144.0, 0.7 * jnp.abs(g_z), *cls)


KEPT_AT = ((0, 4), (6, 2))


def keep(kept_ref, zi, s, rt, zb, terms):
    rows = slice(0, 2) if rt == 0 else slice(SUB - 2, SUB)
    at = KEPT_AT[rt][zb]
    for n, term in enumerate(terms):
        kept_ref[zi, s, n, at:at + 2, :] = term[rows, :]


def middle_kernel(scale, slices, strips, mask_ref, grade_ref, amp_ref, table_ref, mid_ref, kept_ref, low_ref, high_ref):
    bins = table_ref.shape[1]
    fill_tables(scale, table_ref, low_ref, high_ref)
    per_block = MY // LANES
    zero = jnp.zeros((SUB, LANES), jnp.float32)

    def block(cb, carry):
        for rt in range(2):
            for j in range(per_block):
                s = cb * per_block + j
                for c in range(3):
                    mid_ref[rt, s, c] = zero
                mid_ref[rt, s, 3] = zero + 1.0
            for zb in range(2):
                @pl.when(mask_ref[zb, rt, cb] != 0)
                def _():
                    for j in range(per_block):
                        s = cb * per_block + j
                        fields = [Field(ref, slices, strips, s) for ref in (grade_ref, amp_ref)]
                        state = tuple(mid_ref[rt, s, c] for c in range(4))
                        for zi in range(2 - 2 * zb, MZ - 2 * zb):
                            z = zb * MZ + zi
                            along = [[field.load(z + k, rt) for k in (-2, -1, 1, 2)] for field in fields]
                            terms = cell_terms(fields, z, rt, along, False, bins, low_ref, high_ref)
                            keep(kept_ref, zi, s, rt, zb, terms)
                            state = step(state, terms)
                        for c in range(4):
                            mid_ref[rt, s, c] = state[c]
        return carry

    lax.fori_loop(0, strips // per_block, block, 0)


def ends_kernel(scale, pieces, slices, strips, mask_ref, depth_ref, grade_ref, amp_ref, near_ref, far_ref, table_ref,
                mid_ref, *rest):
    outs, (kept_ref, acc_ref, low_ref, high_ref) = rest[:pieces], rest[pieces:]
    bins = table_ref.shape[1]
    fill_tables(scale, table_ref, low_ref, high_ref)
    per_block = MY // LANES
    piece_strips = strips // pieces
    piece_blocks = piece_strips // per_block
    zero = jnp.zeros((SUB, LANES), jnp.float32)
    odd = jnp.broadcast_to(lax.rem(depth_ref[0], 2), (SUB, LANES)) == 1

    def block(cb, carry):
        owner = lax.bitwise_xor(cb // piece_blocks, depth_ref[0])
        for rt in range(2):
            for zb in range(2):
                if zb == 0:
                    for j in range(per_block):
                        for c in range(3):
                            acc_ref[j, c] = zero
                        acc_ref[j, 3] = zero + 1.0
                else:
                    for j in range(per_block):
                        s = cb * per_block + j
                        trans = acc_ref[j, 3]
                        for c in range(3):
                            acc_ref[j, c] = acc_ref[j, c] + trans * mid_ref[rt, s, c]
                        acc_ref[j, 3] = trans * mid_ref[rt, s, 3]

                @pl.when(mask_ref[zb, rt, cb] != 0)
                def _():
                    for j in range(per_block):
                        s = cb * per_block + j
                        fields = [Field(ref, slices, strips, s) for ref in (grade_ref, amp_ref)]
                        halos = [[Field(ref, 4, strips, s) for ref in (near_ref, far_ref)]] * 2
                        state = tuple(acc_ref[j, c] for c in range(4))
                        for zi in (0, 1) if zb == 0 else (MZ - 2, MZ - 1):
                            z = zb * MZ + zi
                            along = []
                            for f in range(2):
                                near, far = halos[f]

                                def at(z):
                                    if 0 <= z < slices:
                                        return fields[f].load(z, rt)
                                    k = 2 * f + z % slices % 2
                                    one, two = near.load(k, rt), far.load(k, rt)
                                    return jnp.where(odd, one, two) if z < 0 else jnp.where(odd, two, one)

                                along.append([at(z + k) for k in (-2, -1, 1, 2)])
                            terms = cell_terms(fields, z, rt, along, True, bins, low_ref, high_ref)
                            keep(kept_ref, zi if zb == 0 else zi - 4, s, rt, zb, terms)
                            state = step(state, terms)
                        for c in range(4):
                            acc_ref[j, c] = state[c]
            for k in range(pieces):
                @pl.when(owner == k)
                def _():
                    for c in range(4):
                        for j in range(per_block):
                            part = lax.rem(cb, piece_blocks) * MY + j * LANES
                            lanes = pl.ds(pl.multiple_of(part, LANES), LANES)
                            outs[k][c, rt * SUB:(rt + 1) * SUB, lanes] = acc_ref[j, c]
        return carry

    lax.fori_loop(0, strips // per_block, block, 0)


def edge_kernel(pieces, mask_ref, depth_ref, lat_ref, kept_ref, ends_ref, pair_ref, cross_ref, *outs):
    half = kept_ref.shape[0]
    strips = kept_ref.shape[1]
    sub = sublane((SUB, LANES))
    is_first = lax.rem((sub + 2) // 4, 2) == 0
    odd_lat = jnp.broadcast_to(lax.rem(lat_ref[0], 2), (SUB, LANES))
    from_pair = lax.rem(sub // 2, 2) != odd_lat
    piece_strips = strips // pieces
    packs = piece_strips // 2

    above = lax.rem(sub // 2, 2) == 0
    even_row = lax.rem(sub, 2) == 0

    def outside(raw, above):
        mate = jnp.where(even_row, pltpu.roll(raw, SUB - 1, 0), pltpu.roll(raw, 1, 0))
        mate = jnp.where(above == even_row, 8.0 * mate, 0.0)
        return jnp.where(above, raw - mate, mate - raw)

    def halo(f, zi, lanes):
        pair, cross = pair_ref[f, zi % 4, :, lanes], cross_ref[f, zi % 4, :, lanes]
        if zi < 4:
            return outside(jnp.where(from_pair, pair, cross), above)
        return outside(pltpu.roll(jnp.where(from_pair, cross, pair), 2, 0), above)

    def strip(s):
        lanes = pl.ds(pl.multiple_of(s * LANES, LANES), LANES)
        cb = s // (MY // LANES)
        full = [[jnp.broadcast_to(mask_ref[zb, rt, cb], (SUB, LANES)) for rt in range(2)] for zb in range(2)]
        live = jnp.where(
            sub < 4, jnp.where(sub < 2, full[0][0], full[1][1]), jnp.where(sub < 6, full[1][0], full[0][1])
        ) != 0
        zero = jnp.zeros((SUB, LANES), jnp.float32)
        total = [zero, zero, zero]
        trans = zero + 1.0
        for zi in range(half):
            terms = [kept_ref[zi, s, n] for n in range(TERMS)]
            if zi < 2:
                terms = [jnp.where(is_first, ends_ref[zi, s, n], term) for n, term in enumerate(terms)]
            if zi >= half - 2:
                terms = [jnp.where(is_first, term, ends_ref[zi - half + 4, s, n]) for n, term in enumerate(terms)]
            g_x, a_x, g_yz, a_yz, steep, red, green, blue, alpha = terms
            g_x = g_x + halo(0, zi, lanes)
            a_x = a_x + halo(1, zi, lanes)
            edge = 1.0 - 12.0 * lax.rsqrt(a_x * a_x + a_yz)
            shade = 0.3 + steep * lax.rsqrt(g_x * g_x + g_yz)
            weight = jnp.where(live, trans * (alpha * edge), 0.0)
            trans = trans - weight
            weight = weight * shade
            total = [t + jnp.where(live, weight * c, 0.0) for t, c in zip(total, (red, green, blue))]
        out = [t + trans * pltpu.roll(t, 4, 0) for t in total]
        return out + [trans * pltpu.roll(trans, 4, 0)]

    def piece(p, carry):
        results = [strip(p * piece_strips + j) for j in range(piece_strips)]
        owner = lax.bitwise_xor(p, depth_ref[0])
        for j in range(packs):
            packed = [
                jnp.where(is_first, one, pltpu.roll(two, 4, 0)) for one, two in zip(results[j], results[j + packs])
            ]
            for k in range(pieces):
                @pl.when(owner == k)
                def _():
                    for c in range(4):
                        outs[k][c, :, j * LANES:(j + 1) * LANES] = packed[c]
        return carry

    lax.fori_loop(0, pieces, piece, 0)


def fold(parts, rank):
    level = 0
    while len(parts) > 1:
        first = lax.rem(lax.shift_right_logical(rank, level), 2) == 0
        merged = []
        for mine, other in zip(parts[0::2], parts[1::2]):
            first_here = jnp.broadcast_to(first, mine[3].shape)
            clear = jnp.where(first_here, mine[3], other[3])
            merged.append(
                [jnp.where(first_here, m, o) + clear * jnp.where(first_here, o, m) for m, o in zip(mine[:3], other[:3])]
                + [mine[3] * other[3]]
            )
        parts = merged
        level += 1
    return parts[0][:3] + [1.0 - parts[0][3]]


def finish_kernel(pieces, depth_ref, *refs):
    inner, edges, out_ref = refs[:pieces], refs[pieces:2 * pieces], refs[-1]
    rows, cols = out_ref.shape[1:]
    rank = depth_ref[0]
    frame = fold([[ref[c] for c in range(4)] for ref in inner], rank)
    rim = fold([[ref[c] for c in range(4)] for ref in edges], rank)
    for c in range(4):
        packed = rim[c]
        wide = jnp.concatenate([packed, pltpu.roll(packed, 4, 0)], axis=1)
        sub = sublane(wide.shape)
        out_ref[c, 0:SUB, :] = jnp.where(sub < 2, wide, frame[c][0:SUB, :])
        out_ref[c, rows - SUB:rows, :] = jnp.where(sub >= SUB - 2, wide, frame[c][rows - SUB:rows, :])


def swap_near(x, axis):
    return lax.ppermute(x, axis, [(i, i ^ 1) for i in range(lax.axis_size(axis))])


def swap_far(x, axis):
    size = lax.axis_size(axis)
    return lax.ppermute(x, axis, [(i, j) for k in range(1, size - 1, 2) for i, j in ((k, k + 1), (k + 1, k))])


def by_strips(array):
    rows, cols = array.shape[-2:]
    split = array.reshape(-1, rows // SUB, SUB, cols // LANES, LANES)
    return split.transpose(0, 1, 3, 2, 4).reshape(-1, LANES)


def local(grade_field, amplitude, tf_table, brick_mask):
    slices, rows, cols = grade_field.shape
    assert (slices, rows) == (2 * MZ, 2 * MX)
    pieces = lax.axis_size("depth")
    depth_rank = lax.axis_index("depth").astype(jnp.int32).reshape(1)
    lat_rank = lax.axis_index("lat").astype(jnp.int32).reshape(1)
    f32 = jnp.float32
    vmem = pl.BlockSpec(memory_space=pltpu.VMEM)
    smem = pl.BlockSpec(memory_space=pltpu.SMEM)
    hbm = pl.BlockSpec(memory_space=pltpu.MemorySpace.HBM)
    lat_halo = jax.ShapeDtypeStruct((2, slices // 4, SUB, cols), f32)
    depth_halo = jax.ShapeDtypeStruct((2, 2, rows, cols), f32)
    hbm_only = pltpu.MemorySpace.HBM
    fields = (grade_field, amplitude)
    grade_field = pltpu.with_memory_space_constraint(grade_field, hbm_only)
    amplitude = pltpu.with_memory_space_constraint(amplitude, hbm_only)
    pair, cross, near, far = pl.pallas_call(
        take_kernel,
        out_shape=(lat_halo, lat_halo, depth_halo, depth_halo),
        in_specs=[smem, smem, hbm, hbm],
        out_specs=[vmem] * 4,
        scratch_shapes=[pltpu.SemaphoreType.DMA((2, 4, 2)), pltpu.SemaphoreType.DMA((2, 2))],
        compiler_params=pltpu.CompilerParams(vmem_limit_bytes=8 << 20),
        name="take",
    )(lat_rank, depth_rank, grade_field, amplitude)
    pair = swap_near(pair, "lat")
    cross = swap_far(cross, "lat")
    near = swap_near(near, "depth")
    far = swap_far(far, "depth")
    piece = jax.ShapeDtypeStruct((4, rows, cols // pieces), f32)
    scale = 4.0 / (slices * pieces)
    strips = cols // LANES
    table = pltpu.VMEM((4, SUB, tf_table.shape[1]), f32)
    grade_strips, amp_strips = by_strips(fields[0]), by_strips(fields[1])
    mid, kept = pl.pallas_call(
        functools.partial(middle_kernel, scale, slices, strips),
        out_shape=(
            jax.ShapeDtypeStruct((2, strips, 4, SUB, LANES), f32),
            jax.ShapeDtypeStruct((MZ, strips, TERMS, SUB, LANES), f32),
        ),
        in_specs=[smem, vmem, vmem, vmem],
        out_specs=[vmem, vmem],
        scratch_shapes=[table, table],
        compiler_params=pltpu.CompilerParams(vmem_limit_bytes=8 << 20),
        name="middle",
    )(brick_mask, grade_strips, amp_strips, tf_table)
    *parts, kept_ends = pl.pallas_call(
        functools.partial(ends_kernel, scale, pieces, slices, strips),
        out_shape=(piece,) * pieces + (jax.ShapeDtypeStruct((4, strips, TERMS, SUB, LANES), f32),),
        in_specs=[smem, smem] + [vmem] * 6,
        out_specs=[vmem] * (pieces + 1),
        scratch_shapes=[pltpu.VMEM((MY // LANES, 4, SUB, LANES), f32), table, table],
        compiler_params=pltpu.CompilerParams(vmem_limit_bytes=8 << 20),
        name="ends",
    )(brick_mask, depth_rank, grade_strips, amp_strips, by_strips(near), by_strips(far), tf_table, mid)

    def exchange(parts):
        return [parts[0]] + [
            lax.ppermute(parts[k], "depth", [(i, i ^ k) for i in range(pieces)]) for k in range(1, pieces)
        ]

    inner = exchange(parts)
    rim = jax.ShapeDtypeStruct((4, SUB, cols // pieces // 2), f32)
    rims = pl.pallas_call(
        functools.partial(edge_kernel, pieces),
        out_shape=(rim,) * pieces,
        in_specs=[smem, smem, smem, vmem, vmem, vmem, vmem],
        out_specs=[vmem] * pieces,
        compiler_params=pltpu.CompilerParams(vmem_limit_bytes=4 << 20),
        name="edges",
    )(brick_mask, depth_rank, lat_rank, kept, kept_ends, pair, cross)
    edges = exchange(rims)
    return pl.pallas_call(
        functools.partial(finish_kernel, pieces),
        out_shape=piece,
        in_specs=[smem] + [vmem] * (2 * pieces),
        out_specs=vmem,
        compiler_params=pltpu.CompilerParams(vmem_limit_bytes=4 << 20),
        name="finish",
    )(depth_rank, *inner, *edges)


def solution(mesh):
    placed = (P("depth", "lat", None), P("depth", "lat", None), P(), P("depth", "lat", None))
    return jax.shard_map(
        local, mesh=mesh, in_specs=placed, out_specs=P(None, "lat", "depth"), check_vma=False
    )
```

time: 36.3 us -> 36.4 us (level)
  starting transfers between devices: 18.8 us -> 11.6 us
  waiting for transfers between devices: 3.73 us -> 8.62 us
  Pallas kernels: 13.3 us -> 15.9 us
    ppermute x6, starting transfers between devices: 14.3 us -> 7.07 us  [exchange(): lax.ppermute(parts[k], 'depth', [(i, i ^ k) for i in range(pieces)])]
    ppermute x2, waiting for transfers between devices: 1.27 us -> 6.16 us  [swap_near(): lax.ppermute(x, axis, [(i, i ^ 1) for i in range(lax.axis_size(axis))])]
    pallas_call x1 -> x2, Pallas kernels: 9.24 us -> 11.6 us  [the longest x1 7.25 us: local(): pl.pallas_call(functools.partial(middle_kernel, scale, slices, strips), o...]
  transfers between devices with their start and end apart: 10 -> 10, of which waited for: 3 -> 3; matrix products, arithmetic and copies ran while one was open for 0% -> 0% of each run, Pallas kernels for 30% -> 37%
where the time goes in v5:
time: 36.4 us; the launch traced here: 36.3 us
  Pallas kernels  15.9 us (44%)
  starting transfers between devices  11.6 us (32%)
  waiting for transfers between devices  8.62 us (24%)
    pallas_call x1, Pallas kernels, local(): pl.pallas_call(functools.partial(middle_kernel, scale, slices, strips), o...  7.25 us
    ppermute x6, starting transfers between devices, exchange(): lax.ppermute(parts[k], 'depth', [(i, i ^ k) for i in range(pieces)])  7.07 us
    ppermute x2, waiting for transfers between devices, swap_near(): lax.ppermute(x, axis, [(i, i ^ 1) for i in range(lax.axis_size(axis))])  6.16 us
    pallas_call x1, Pallas kernels, local(): pl.pallas_call(functools.partial(ends_kernel, scale, pieces, slices, stri...  4.35 us
    ppermute x2, starting transfers between devices, swap_near(): lax.ppermute(x, axis, [(i, i ^ 1) for i in range(lax.axis_size(axis))])  3.15 us
    ppermute x6, waiting for transfers between devices, exchange(): lax.ppermute(parts[k], 'depth', [(i, i ^ k) for i in range(pieces)])  2.46 us
    pallas_call x1, Pallas kernels, local(): pl.pallas_call(take_kernel, out_shape=(lat_halo, lat_halo, depth_halo, de...  1.93 us
    pallas_call x1, Pallas kernels, local(): pl.pallas_call(functools.partial(edge_kernel, pieces), out_shape=(rim,) *...  1.68 us
  transfers between devices with their start and end apart: 10, of which 3 were waited for; matrix products, arithmetic and copies ran while one was open for 0% of the time, Pallas kernels for 37%

profile of v5, /device:TPU:0, one launch (start us, length us, event | category | flops | bytes accessed | tf_op | source)
XLA Modules:
  0.0 36.3 jit_solution(11648164082705300558)
XLA Ops:
  0.0 0.0 copy-start
  0.0 0.0 copy-start.2
  0.0 0.0 copy-start.3
  0.0 0.0 copy-start.1
  0.0 1.9 %take.1 = (f32[2,4,8,2048]{3,2,1,0:T(8,128)S(1)}, f32[2,4,8,2048]{3,2,1,0:T(8,128)S(1)}, f32[2,2,16,2048]{3,2,1,0:T(8,128)S(1)}, f32[2,2,16,2048]{3,2,1,0:T(8,128)S(1)}) custom-call(s32[1]{0:T(128)} %bitcast.7.lat_ref, s32[1]{0:T(128)} %bitcast.depth_ref, f32[16,16,2048]{2,1,0:T(8,128)} %grade_hbm.1, f32[16,16,2048]{2,1,0:T(8,128)} %amp_hbm.1), custom_call_target="tpu_custom_call" | custom-call | tf_op jit(solution)/shard_map/take/pallas_call | solution.py:389
  1.9 0.5 %collective-permute-start = (f32[2,2,16,2048]{3,2,1,0:T(8,128)S(1)}, f32[2,2,16,2048]{3,2,1,0:T(8,128)S(1)}, u32[]{:S(2)}, u32[]{:S(2)}) collective-permute-start(f32[2,2,16,2048]{3,2,1,0:T(8,128)S(1)} %get-tuple-element.20), channel_id=1, source_target_pairs={{0,1},{1,0},{2,3},{3,2},{4,5},{5,4},{6,7},{7,6},{8,9},{9,8},{10,11... | collective-permute-start | bytes 1572872 | tf_op jit(solution)/shard_map/ppermute | solution.py:359
  2.5 0.7 %collective-permute-start.1 = (f32[2,2,16,2048]{3,2,1,0:T(8,128)S(1)}, f32[2,2,16,2048]{3,2,1,0:T(8,128)S(1)}, u32[]{:S(2)}, u32[]{:S(2)}) collective-permute-start(f32[2,2,16,2048]{3,2,1,0:T(8,128)S(1)} %get-tuple-element.21), channel_id=1, source_target_pairs={{1,2},{2,1},{5,6},{6,5},{9,10},{10,9},{13,14},{14,13},{17,18},{18,... | collective-permute-start | bytes 1572872 | tf_op jit(solution)/shard_map/ppermute | solution.py:364
  3.2 2.6 %collective-permute-start.5 = (f32[2,4,8,2048]{3,2,1,0:T(8,128)S(1)}, f32[2,4,8,2048]{3,2,1,0:T(8,128)S(1)}, u32[]{:S(2)}, u32[]{:S(2)}) collective-permute-start(f32[2,4,8,2048]{3,2,1,0:T(8,128)S(1)} %get-tuple-element.29), channel_id=1, source_target_pairs={{0,4},{4,0},{8,12},{12,8},{16,20},{20,16},{24,28},{28,24},{1,5},{5... | collective-permute-start | bytes 1572872 | tf_op jit(solution)/shard_map/ppermute | solution.py:359
  5.8 0.7 %collective-permute-start.6 = (f32[2,4,8,2048]{3,2,1,0:T(8,128)S(1)}, f32[2,4,8,2048]{3,2,1,0:T(8,128)S(1)}, u32[]{:S(2)}, u32[]{:S(2)}) collective-permute-start(f32[2,4,8,2048]{3,2,1,0:T(8,128)S(1)} %get-tuple-element.30), channel_id=1, source_target_pairs={{4,8},{8,4},{12,16},{16,12},{20,24},{24,20},{5,9},{9,5},{13,17},{1... | collective-permute-start | bytes 1572872 | tf_op jit(solution)/shard_map/ppermute | solution.py:364
  6.5 0.0 copy-done
  6.5 0.0 copy-done.2
  6.5 0.0 copy-done.3
  6.5 0.0 copy-done.1
  6.5 7.3 %middle.1 = (f32[2,16,4,8,128]{4,3,2,1,0:T(8,128)S(1)}, f32[8,16,9,8,128]{4,3,2,1,0:T(8,128)S(1)}) custom-call(s32[2,2,8]{2,1,0:T(2,128)S(1)} %copy-done.2, f32[4096,128]{1,0:T(8,128)S(1)} %bitcast.22, f32[4096,128]{1,0:T(8,128)S(1)} %bitcast.24, s32[4,128]{1,0:T(4,128)S(1)} %copy-done.3), custom_call_target="tpu_custom_call" | custom-call | tf_op jit(solution)/shard_map/middle/pallas_call | solution.py:407
  13.8 0.0 collective-permute-done
  13.8 0.0 collective-permute-done.1
  13.8 4.3 %ends.1 = (f32[4,16,512]{2,1,0:T(8,128)S(1)}, f32[4,16,512]{2,1,0:T(8,128)S(1)}, f32[4,16,512]{2,1,0:T(8,128)S(1)}, f32[4,16,512]{2,1,0:T(8,128)S(1)}, f32[4,16,9,8,128]{4,3,2,1,0:T(8,128)S(1)}) custom-call(s32[2,2,8]{2,1,0:T(2,128)S(1)} %copy-done.2, s32[1]{0:T(128)} %bitcast.depth_ref, f32[4096,128]{1,0:T(8,128)S(1)} %bitcast.23, ...), custom_call_target="tpu_custom_call" | custom-call | tf_op jit(solution)/shard_map/ends/pallas_call | solution.py:419
  18.2 1.7 %collective-permute-start.2 = (f32[4,16,512]{2,1,0:T(8,128)S(1)}, f32[4,16,512]{2,1,0:T(8,128)S(1)}, u32[]{:S(2)}, u32[]{:S(2)}) collective-permute-start(f32[4,16,512]{2,1,0:T(8,128)S(1)} %get-tuple-element.24), channel_id=1, source_target_pairs={{0,1},{1,0},{2,3},{3,2},{4,5},{5,4},{6,7},{7,6},{8,9},{9,8},{10,11... | collective-permute-start | bytes 393224 | tf_op jit(solution)/shard_map/ppermute | solution.py:431
  19.8 1.4 %collective-permute-start.3 = (f32[4,16,512]{2,1,0:T(8,128)S(1)}, f32[4,16,512]{2,1,0:T(8,128)S(1)}, u32[]{:S(2)}, u32[]{:S(2)}) collective-permute-start(f32[4,16,512]{2,1,0:T(8,128)S(1)} %get-tuple-element.25), channel_id=1, source_target_pairs={{0,2},{1,3},{2,0},{3,1},{4,6},{5,7},{6,4},{7,5},{8,10},{9,11},{10,... | collective-permute-start | bytes 393224 | tf_op jit(solution)/shard_map/ppermute | solution.py:431
  21.2 0.1 collective-permute-start.4
  21.3 6.2 %collective-permute-done.5.pair_ref = f32[2,4,8,2048]{3,2,1,0:T(8,128)S(1)} collective-permute-done((f32[2,4,8,2048]{3,2,1,0:T(8,128)S(1)}, f32[2,4,8,2048]{3,2,1,0:T(8,128)S(1)}, u32[]{:S(2)}, u32[]{:S(2)}) %collective-permute-start.5) | collective-permute-done | bytes 524320 | tf_op jit(solution)/shard_map/ppermute | solution.py:359
  27.4 0.0 collective-permute-done.6.cross_ref
  27.4 1.7 %edges.1 = (f32[4,8,256]{2,1,0:T(8,128)S(1)}, f32[4,8,256]{2,1,0:T(8,128)S(1)}, f32[4,8,256]{2,1,0:T(8,128)S(1)}, f32[4,8,256]{2,1,0:T(8,128)S(1)}) custom-call(s32[2,2,8]{2,1,0:T(2,128)S(1)} %copy-done.2, s32[1]{0:T(128)} %bitcast.depth_ref, s32[1]{0:T(128)} %bitcast.7.lat_ref, f32[8,16,9,8,128]{4,3,2,1,0:T(8,128)S(1)} %get-tuple-element.27.kept_ref, ...), custom_call_target="tpu_custom_call" | custom-call | tf_op jit(solution)/shard_map/edges/pallas_call | solution.py:436
  29.1 2.1 %collective-permute-start.7 = (f32[4,8,256]{2,1,0:T(8,128)S(1)}, f32[4,8,256]{2,1,0:T(8,128)S(1)}, u32[]{:S(2)}, u32[]{:S(2)}) collective-permute-start(f32[4,8,256]{2,1,0:T(8,128)S(1)} %get-tuple-element.32), channel_id=1, source_target_pairs={{0,1},{1,0},{2,3},{3,2},{4,5},{5,4},{6,7},{7,6},{8,9},{9,8},{10,11... | collective-permute-start | bytes 98312 | tf_op jit(solution)/shard_map/ppermute | solution.py:431
  31.2 1.0 %collective-permute-start.8 = (f32[4,8,256]{2,1,0:T(8,128)S(1)}, f32[4,8,256]{2,1,0:T(8,128)S(1)}, u32[]{:S(2)}, u32[]{:S(2)}) collective-permute-start(f32[4,8,256]{2,1,0:T(8,128)S(1)} %get-tuple-element.33), channel_id=1, source_target_pairs={{0,2},{1,3},{2,0},{3,1},{4,6},{5,7},{6,4},{7,5},{8,10},{9,11},{10,... | collective-permute-start | bytes 98312 | tf_op jit(solution)/shard_map/ppermute | solution.py:431
  32.2 0.0 collective-permute-done.7.refs_5_
  32.2 0.9 %collective-permute-start.9 = (f32[4,8,256]{2,1,0:T(8,128)S(1)}, f32[4,8,256]{2,1,0:T(8,128)S(1)}, u32[]{:S(2)}, u32[]{:S(2)}) collective-permute-start(f32[4,8,256]{2,1,0:T(8,128)S(1)} %get-tuple-element.34), channel_id=1, source_target_pairs={{0,3},{1,2},{2,1},{3,0},{4,7},{5,6},{6,5},{7,4},{8,11},{9,10},{10,... | collective-permute-start | bytes 98312 | tf_op jit(solution)/shard_map/ppermute | solution.py:431
  33.1 2.0 %collective-permute-done.8.refs_6_ = f32[4,8,256]{2,1,0:T(8,128)S(1)} collective-permute-done((f32[4,8,256]{2,1,0:T(8,128)S(1)}, f32[4,8,256]{2,1,0:T(8,128)S(1)}, u32[]{:S(2)}, u32[]{:S(2)}) %collective-permute-start.8) | collective-permute-done | bytes 32800 | tf_op jit(solution)/shard_map/ppermute | solution.py:431
  35.1 0.4 %collective-permute-done.9.refs_7_ = f32[4,8,256]{2,1,0:T(8,128)S(1)} collective-permute-done((f32[4,8,256]{2,1,0:T(8,128)S(1)}, f32[4,8,256]{2,1,0:T(8,128)S(1)}, u32[]{:S(2)}, u32[]{:S(2)}) %collective-permute-start.9) | collective-permute-done | bytes 32800 | tf_op jit(solution)/shard_map/ppermute | solution.py:431
  35.5 0.0 collective-permute-done.2.refs_1_
  35.5 0.0 collective-permute-done.3.refs_2_
  35.5 0.0 collective-permute-done.4.refs_3_
  35.5 0.7 %finish.1 = f32[4,16,512]{2,1,0:T(8,128)} custom-call(s32[1]{0:T(128)} %bitcast.depth_ref, f32[4,16,512]{2,1,0:T(8,128)S(1)} %get-tuple-element.23.refs_0_, f32[4,16,512]{2,1,0:T(8,128)S(1)} %collective-permute-done.2.refs_1_, f32[4,16,512]{2,1,0:T(8,128)S(1)} %collective-permute-done.3.refs_2_, f32[4,16,512]{2,1,0:T(8,128)S(1)} %collective-permute-done.4.refs_3_, ...), custom_call_target="tpu_custom_call" | custom-call | tf_op jit(solution)/shard_map/finish/pallas_call | solution.py:445
Async XLA Ops:
  0.0 6.5 %copy-start = (f32[16,16,2048]{2,1,0:T(8,128)S(1)}, f32[16,16,2048]{2,1,0:T(8,128)}, u32[]{:S(2)}) copy-start(f32[16,16,2048]{2,1,0:T(8,128)} %grade_hbm.1) | copy-start | bytes 6291460
  0.0 6.5 %copy-start.2 = (s32[2,2,8]{2,1,0:T(2,128)S(1)}, s32[2,2,8]{2,1,0:T(2,128)}, u32[]{:S(2)}) copy-start(s32[2,2,8]{2,1,0:T(2,128)} %mask_ref.5) | copy-start | bytes 388
  0.0 6.5 %copy-start.3 = (s32[4,128]{1,0:T(4,128)S(1)}, s32[4,128]{1,0:T(4,128)}, u32[]{:S(2)}) copy-start(s32[4,128]{1,0:T(4,128)} %table_ref.3) | copy-start | bytes 6148
  0.0 6.5 %copy-start.1 = (f32[16,16,2048]{2,1,0:T(8,128)S(1)}, f32[16,16,2048]{2,1,0:T(8,128)}, u32[]{:S(2)}) copy-start(f32[16,16,2048]{2,1,0:T(8,128)} %amp_hbm.1) | copy-start | bytes 6291460
  1.9 11.8 %collective-permute-start = (f32[2,2,16,2048]{3,2,1,0:T(8,128)S(1)}, f32[2,2,16,2048]{3,2,1,0:T(8,128)S(1)}, u32[]{:S(2)}, u32[]{:S(2)}) collective-permute-start(f32[2,2,16,2048]{3,2,1,0:T(8,128)S(1)} %get-tuple-element.20), channel_id=1, source_target_pairs={{0,1},{1,0},{2,3},{3,2},{4,5},{5,4},{6,7},{7,6},{8,9},{9,8},{10,11... | collective-permute-start | bytes 1572872 | tf_op jit(solution)/shard_map/ppermute | solution.py:359
  2.5 11.3 %collective-permute-start.1 = (f32[2,2,16,2048]{3,2,1,0:T(8,128)S(1)}, f32[2,2,16,2048]{3,2,1,0:T(8,128)S(1)}, u32[]{:S(2)}, u32[]{:S(2)}) collective-permute-start(f32[2,2,16,2048]{3,2,1,0:T(8,128)S(1)} %get-tuple-element.21), channel_id=1, source_target_pairs={{1,2},{2,1},{5,6},{6,5},{9,10},{10,9},{13,14},{14,13},{17,18},{18,... | collective-permute-start | bytes 1572872 | tf_op jit(solution)/shard_map/ppermute | solution.py:364
  3.2 24.2 %collective-permute-start.5 = (f32[2,4,8,2048]{3,2,1,0:T(8,128)S(1)}, f32[2,4,8,2048]{3,2,1,0:T(8,128)S(1)}, u32[]{:S(2)}, u32[]{:S(2)}) collective-permute-start(f32[2,4,8,2048]{3,2,1,0:T(8,128)S(1)} %get-tuple-element.29), channel_id=1, source_target_pairs={{0,4},{4,0},{8,12},{12,8},{16,20},{20,16},{24,28},{28,24},{1,5},{5... | collective-permute-start | bytes 1572872 | tf_op jit(solution)/shard_map/ppermute | solution.py:359
  5.8 21.6 %collective-permute-start.6 = (f32[2,4,8,2048]{3,2,1,0:T(8,128)S(1)}, f32[2,4,8,2048]{3,2,1,0:T(8,128)S(1)}, u32[]{:S(2)}, u32[]{:S(2)}) collective-permute-start(f32[2,4,8,2048]{3,2,1,0:T(8,128)S(1)} %get-tuple-element.30), channel_id=1, source_target_pairs={{4,8},{8,4},{12,16},{16,12},{20,24},{24,20},{5,9},{9,5},{13,17},{1... | collective-permute-start | bytes 1572872 | tf_op jit(solution)/shard_map/ppermute | solution.py:364
  18.2 17.4 %collective-permute-start.2 = (f32[4,16,512]{2,1,0:T(8,128)S(1)}, f32[4,16,512]{2,1,0:T(8,128)S(1)}, u32[]{:S(2)}, u32[]{:S(2)}) collective-permute-start(f32[4,16,512]{2,1,0:T(8,128)S(1)} %get-tuple-element.24), channel_id=1, source_target_pairs={{0,1},{1,0},{2,3},{3,2},{4,5},{5,4},{6,7},{7,6},{8,9},{9,8},{10,11... | collective-permute-start | bytes 393224 | tf_op jit(solution)/shard_map/ppermute | solution.py:431
  19.8 15.7 %collective-permute-start.3 = (f32[4,16,512]{2,1,0:T(8,128)S(1)}, f32[4,16,512]{2,1,0:T(8,128)S(1)}, u32[]{:S(2)}, u32[]{:S(2)}) collective-permute-start(f32[4,16,512]{2,1,0:T(8,128)S(1)} %get-tuple-element.25), channel_id=1, source_target_pairs={{0,2},{1,3},{2,0},{3,1},{4,6},{5,7},{6,4},{7,5},{8,10},{9,11},{10,... | collective-permute-start | bytes 393224 | tf_op jit(solution)/shard_map/ppermute | solution.py:431
  21.2 14.3 %collective-permute-start.4 = (f32[4,16,512]{2,1,0:T(8,128)S(1)}, f32[4,16,512]{2,1,0:T(8,128)S(1)}, u32[]{:S(2)}, u32[]{:S(2)}) collective-permute-start(f32[4,16,512]{2,1,0:T(8,128)S(1)} %get-tuple-element.26), channel_id=1, source_target_pairs={{0,3},{1,2},{2,1},{3,0},{4,7},{5,6},{6,5},{7,4},{8,11},{9,10},{10,... | collective-permute-start | bytes 393224 | tf_op jit(solution)/shard_map/ppermute | solution.py:431
  29.1 3.1 %collective-permute-start.7 = (f32[4,8,256]{2,1,0:T(8,128)S(1)}, f32[4,8,256]{2,1,0:T(8,128)S(1)}, u32[]{:S(2)}, u32[]{:S(2)}) collective-permute-start(f32[4,8,256]{2,1,0:T(8,128)S(1)} %get-tuple-element.32), channel_id=1, source_target_pairs={{0,1},{1,0},{2,3},{3,2},{4,5},{5,4},{6,7},{7,6},{8,9},{9,8},{10,11... | collective-permute-start | bytes 98312 | tf_op jit(solution)/shard_map/ppermute | solution.py:431
  31.2 3.9 %collective-permute-start.8 = (f32[4,8,256]{2,1,0:T(8,128)S(1)}, f32[4,8,256]{2,1,0:T(8,128)S(1)}, u32[]{:S(2)}, u32[]{:S(2)}) collective-permute-start(f32[4,8,256]{2,1,0:T(8,128)S(1)} %get-tuple-element.33), channel_id=1, source_target_pairs={{0,2},{1,3},{2,0},{3,1},{4,6},{5,7},{6,4},{7,5},{8,10},{9,11},{10,... | collective-permute-start | bytes 98312 | tf_op jit(solution)/shard_map/ppermute | solution.py:431
  32.2 3.3 %collective-permute-start.9 = (f32[4,8,256]{2,1,0:T(8,128)S(1)}, f32[4,8,256]{2,1,0:T(8,128)S(1)}, u32[]{:S(2)}, u32[]{:S(2)}) collective-permute-start(f32[4,8,256]{2,1,0:T(8,128)S(1)} %get-tuple-element.34), channel_id=1, source_target_pairs={{0,3},{1,2},{2,1},{3,0},{4,7},{5,6},{6,5},{7,4},{8,11},{9,10},{10,... | collective-permute-start | bytes 98312 | tf_op jit(solution)/shard_map/ppermute | solution.py:431

commit v6 on v5

--- a/solution.py
+++ b/solution.py
@@ -19,26 +19,20 @@
     return lax.broadcasted_iota(jnp.int32, shape, len(shape) - 2)
 
 
-def take_kernel(lat_ref, depth_ref, grade_hbm, amp_hbm, pair_ref, cross_ref, near_ref, far_ref, sems, depth_sems):
+def rows_kernel(lat_ref, grade_hbm, amp_hbm, pair_ref, cross_ref, sems):
     slices, rows = grade_hbm.shape[:2]
     span = slices // 4
     even = lax.rem(lat_ref[0], 2) == 0
-    odd = lax.rem(depth_ref[0], 2)
-    fields = (grade_hbm, amp_hbm)
 
     def copies(above_dst, below_dst):
         made = []
-        for f, src in enumerate(fields):
+        for f, src in enumerate((grade_hbm, amp_hbm)):
             for q in range(4):
                 part = src.at[pl.ds(span * q, span)]
                 above = above_dst.at[f, :, pl.ds((0, 6, 4, 2)[q], 2), :]
                 below = below_dst.at[f, :, pl.ds((6, 4, 2, 0)[q], 2), :]
                 made.append(pltpu.make_async_copy(part.at[:, pl.ds(rows - 2, 2), :], above, sems.at[f, q, 0]))
                 made.append(pltpu.make_async_copy(part.at[:, pl.ds(0, 2), :], below, sems.at[f, q, 1]))
-        for f, src in enumerate(fields):
-            for n, (dst, at) in enumerate(((near_ref, 1 - odd), (far_ref, odd))):
-                here = src.at[pl.ds(at * (slices - 2), 2)]
-                made.append(pltpu.make_async_copy(here, dst.at[f], depth_sems.at[f, n]))
         for copy in made:
             copy.start()
         for copy in made:
@@ -51,6 +45,20 @@
     @pl.when(jnp.logical_not(even))
     def _():
         copies(cross_ref, pair_ref)
+
+
+def slices_kernel(depth_ref, grade_hbm, amp_hbm, after_ref, near_ref, far_ref, sems):
+    del after_ref
+    slices = grade_hbm.shape[0]
+    odd = lax.rem(depth_ref[0], 2)
+    made = []
+    for f, src in enumerate((grade_hbm, amp_hbm)):
+        for n, (dst, at) in enumerate(((near_ref, 1 - odd), (far_ref, odd))):
+            made.append(pltpu.make_async_copy(src.at[pl.ds(at * (slices - 2), 2)], dst.at[f], sems.at[f, n]))
+    for copy in made:
+        copy.start()
+    for copy in made:
+        copy.wait()
 
 
 def round_weight(w):
@@ -386,15 +394,25 @@
     fields = (grade_field, amplitude)
     grade_field = pltpu.with_memory_space_constraint(grade_field, hbm_only)
     amplitude = pltpu.with_memory_space_constraint(amplitude, hbm_only)
-    pair, cross, near, far = pl.pallas_call(
-        take_kernel,
-        out_shape=(lat_halo, lat_halo, depth_halo, depth_halo),
-        in_specs=[smem, smem, hbm, hbm],
-        out_specs=[vmem] * 4,
-        scratch_shapes=[pltpu.SemaphoreType.DMA((2, 4, 2)), pltpu.SemaphoreType.DMA((2, 2))],
-        compiler_params=pltpu.CompilerParams(vmem_limit_bytes=8 << 20),
-        name="take",
-    )(lat_rank, depth_rank, grade_field, amplitude)
+    small = pltpu.CompilerParams(vmem_limit_bytes=4 << 20)
+    pair, cross = pl.pallas_call(
+        rows_kernel,
+        out_shape=(lat_halo, lat_halo),
+        in_specs=[smem, hbm, hbm],
+        out_specs=[vmem, vmem],
+        scratch_shapes=[pltpu.SemaphoreType.DMA((2, 4, 2))],
+        compiler_params=small,
+        name="take_rows",
+    )(lat_rank, grade_field, amplitude)
+    near, far = pl.pallas_call(
+        slices_kernel,
+        out_shape=(depth_halo, depth_halo),
+        in_specs=[smem, hbm, hbm, pl.BlockSpec(memory_space=pl.ANY)],
+        out_specs=[vmem, vmem],
+        scratch_shapes=[pltpu.SemaphoreType.DMA((2, 2))],
+        compiler_params=small,
+        name="take_slices",
+    )(depth_rank, grade_field, amplitude, pair)
     pair = swap_near(pair, "lat")
     cross = swap_far(cross, "lat")
     near = swap_near(near, "depth")
@@ -414,6 +432,7 @@
         out_specs=[vmem, vmem],
         scratch_shapes=[table, table],
         compiler_params=pltpu.CompilerParams(vmem_limit_bytes=8 << 20),
+        cost_estimate=pl.CostEstimate(flops=10**10, bytes_accessed=10**8, transcendentals=0),
         name="middle",
     )(brick_mask, grade_strips, amp_strips, tf_table)
     *parts, kept_ends = pl.pallas_call(

time: 36.4 us -> 37.2 us (1.022)
  starting transfers between devices: 11.6 us -> 14.5 us
  waiting for transfers between devices: 8.62 us -> 5.85 us
  Pallas kernels: 15.9 us -> 16.3 us
    ppermute x2, waiting for transfers between devices: 6.16 us -> 3.38 us  [swap_near(): lax.ppermute(x, axis, [(i, i ^ 1) for i in range(lax.axis_size(axis))])]
    ppermute x2, starting transfers between devices: 3.15 us -> 5.84 us  [swap_near(): lax.ppermute(x, axis, [(i, i ^ 1) for i in range(lax.axis_size(axis))])]
    pallas_call x1 -> x2, Pallas kernels: 1.93 us -> 2.76 us  [the longest x1 1.38 us: local(): pl.pallas_call(rows_kernel, out_shape=(lat_halo, lat_halo), in_specs=[sme...]
  transfers between devices with their start and end apart: 10 -> 10, of which waited for: 3 -> 3; matrix products, arithmetic and copies ran while one was open for 0% -> 0% of each run, Pallas kernels for 37% -> 38%
where the time goes in v6:
time: 37.2 us; the launch traced here: 37 us
  Pallas kernels  16.3 us (44%)
  starting transfers between devices  14.5 us (39%)
  waiting for transfers between devices  5.85 us (16%)
    ppermute x6, starting transfers between devices, exchange(): lax.ppermute(parts[k], 'depth', [(i, i ^ k) for i in range(pieces)])  7.16 us
    pallas_call x1, Pallas kernels, local(): pl.pallas_call(functools.partial(middle_kernel, scale, slices, strips), o...  6.92 us
    ppermute x2, starting transfers between devices, swap_near(): lax.ppermute(x, axis, [(i, i ^ 1) for i in range(lax.axis_size(axis))])  5.84 us
    pallas_call x1, Pallas kernels, local(): pl.pallas_call(functools.partial(ends_kernel, scale, pieces, slices, stri...  4.2 us
    ppermute x2, waiting for transfers between devices, swap_near(): lax.ppermute(x, axis, [(i, i ^ 1) for i in range(lax.axis_size(axis))])  3.38 us
    ppermute x6, waiting for transfers between devices, exchange(): lax.ppermute(parts[k], 'depth', [(i, i ^ k) for i in range(pieces)])  2.46 us
    pallas_call x1, Pallas kernels, local(): pl.pallas_call(functools.partial(edge_kernel, pieces), out_shape=(rim,) *...  1.69 us
    ppermute x2, starting transfers between devices, swap_far(): lax.ppermute(x, axis, [(i, j) for k in range(1, size - 1, 2) for i, j in...  1.52 us
  transfers between devices with their start and end apart: 10, of which 3 were waited for; matrix products, arithmetic and copies ran while one was open for 0% of the time, Pallas kernels for 38%

profile of v6, /device:TPU:0, one launch (start us, length us, event | category | flops | bytes accessed | tf_op | source)
XLA Modules:
  0.0 37.0 jit_solution(12680008435218393383)
XLA Ops:
  0.0 1.4 %take_rows.1 = (f32[2,4,8,2048]{3,2,1,0:T(8,128)S(1)}, f32[2,4,8,2048]{3,2,1,0:T(8,128)S(1)}) custom-call(s32[1]{0:T(128)} %bitcast.7.lat_ref, f32[16,16,2048]{2,1,0:T(8,128)} %grade_hbm.3, f32[16,16,2048]{2,1,0:T(8,128)} %amp_hbm.3), custom_call_target="tpu_custom_call" | custom-call | tf_op jit(solution)/shard_map/take_rows/pallas_call | solution.py:398
  1.4 0.7 %collective-permute-start.6 = (f32[2,4,8,2048]{3,2,1,0:T(8,128)S(1)}, f32[2,4,8,2048]{3,2,1,0:T(8,128)S(1)}, u32[]{:S(2)}, u32[]{:S(2)}) collective-permute-start(f32[2,4,8,2048]{3,2,1,0:T(8,128)S(1)} %get-tuple-element.30), channel_id=1, source_target_pairs={{4,8},{8,4},{12,16},{16,12},{20,24},{24,20},{5,9},{9,5},{13,17},{1... | collective-permute-start | bytes 1572872 | tf_op jit(solution)/shard_map/ppermute | solution.py:372
  2.1 5.8 %collective-permute-start.5 = (f32[2,4,8,2048]{3,2,1,0:T(8,128)S(1)}, f32[2,4,8,2048]{3,2,1,0:T(8,128)S(1)}, u32[]{:S(2)}, u32[]{:S(2)}) collective-permute-start(f32[2,4,8,2048]{3,2,1,0:T(8,128)S(1)} %get-tuple-element.20.after_ref), channel_id=1, source_target_pairs={{0,4},{4,0},{8,12},{12,8},{16,20},{20,16},{24,28},{28,24},{1,5},{5... | collective-permute-start | bytes 1572872 | tf_op jit(solution)/shard_map/ppermute | solution.py:367
  7.9 0.0 copy-start
  7.9 0.0 copy-start.1
  7.9 0.0 copy-start.2
  7.9 0.0 copy-start.3
  7.9 1.4 %take_slices.1 = (f32[2,2,16,2048]{3,2,1,0:T(8,128)S(1)}, f32[2,2,16,2048]{3,2,1,0:T(8,128)S(1)}) custom-call(s32[1]{0:T(128)} %bitcast.depth_ref, f32[16,16,2048]{2,1,0:T(8,128)} %grade_hbm.3, f32[16,16,2048]{2,1,0:T(8,128)} %amp_hbm.3, f32[2,4,8,2048]{3,2,1,0:T(8,128)S(1)} %get-tuple-element.20.after_ref), custom_call_target="tpu_custom_call" | custom-call | tf_op jit(solution)/shard_map/take_slices/pallas_call | solution.py:407
  9.3 0.1 collective-permute-start
  9.3 0.8 %collective-permute-start.1 = (f32[2,2,16,2048]{3,2,1,0:T(8,128)S(1)}, f32[2,2,16,2048]{3,2,1,0:T(8,128)S(1)}, u32[]{:S(2)}, u32[]{:S(2)}) collective-permute-start(f32[2,2,16,2048]{3,2,1,0:T(8,128)S(1)} %get-tuple-element.22), channel_id=1, source_target_pairs={{1,2},{2,1},{5,6},{6,5},{9,10},{10,9},{13,14},{14,13},{17,18},{18,... | collective-permute-start | bytes 1572872 | tf_op jit(solution)/shard_map/ppermute | solution.py:372
  10.2 0.0 copy-done
  10.2 0.2 copy-done.1
  10.4 0.0 copy-done.2
  10.4 0.0 copy-done.3
  10.4 6.9 %middle.1 = (f32[2,16,4,8,128]{4,3,2,1,0:T(8,128)S(1)}, f32[8,16,9,8,128]{4,3,2,1,0:T(8,128)S(1)}) custom-call(s32[2,2,8]{2,1,0:T(2,128)S(1)} %copy-done.2, f32[4096,128]{1,0:T(8,128)S(1)} %bitcast.22, f32[4096,128]{1,0:T(8,128)S(1)} %bitcast.24, s32[4,128]{1,0:T(4,128)S(1)} %copy-done.3), custom_call_target="tpu_custom_call" | custom-call | flops 10000000000 | bytes 100000000 | tf_op jit(solution)/shard_map/middle/pallas_call | solution.py:425
  17.3 0.0 collective-permute-done
  17.3 0.0 collective-permute-done.1
  17.4 4.2 %ends.1 = (f32[4,16,512]{2,1,0:T(8,128)S(1)}, f32[4,16,512]{2,1,0:T(8,128)S(1)}, f32[4,16,512]{2,1,0:T(8,128)S(1)}, f32[4,16,512]{2,1,0:T(8,128)S(1)}, f32[4,16,9,8,128]{4,3,2,1,0:T(8,128)S(1)}) custom-call(s32[2,2,8]{2,1,0:T(2,128)S(1)} %copy-done.2, s32[1]{0:T(128)} %bitcast.depth_ref, f32[4096,128]{1,0:T(8,128)S(1)} %bitcast.23, ...), custom_call_target="tpu_custom_call" | custom-call | tf_op jit(solution)/shard_map/ends/pallas_call | solution.py:438
  21.6 3.2 %collective-permute-start.2 = (f32[4,16,512]{2,1,0:T(8,128)S(1)}, f32[4,16,512]{2,1,0:T(8,128)S(1)}, u32[]{:S(2)}, u32[]{:S(2)}) collective-permute-start(f32[4,16,512]{2,1,0:T(8,128)S(1)} %get-tuple-element.25), channel_id=1, source_target_pairs={{0,1},{1,0},{2,3},{3,2},{4,5},{5,4},{6,7},{7,6},{8,9},{9,8},{10,11... | collective-permute-start | bytes 393224 | tf_op jit(solution)/shard_map/ppermute | solution.py:450
  24.8 0.4 %collective-permute-start.3 = (f32[4,16,512]{2,1,0:T(8,128)S(1)}, f32[4,16,512]{2,1,0:T(8,128)S(1)}, u32[]{:S(2)}, u32[]{:S(2)}) collective-permute-start(f32[4,16,512]{2,1,0:T(8,128)S(1)} %get-tuple-element.26), channel_id=1, source_target_pairs={{0,2},{1,3},{2,0},{3,1},{4,6},{5,7},{6,4},{7,5},{8,10},{9,11},{10,... | collective-permute-start | bytes 393224 | tf_op jit(solution)/shard_map/ppermute | solution.py:450
  25.2 1.0 %collective-permute-start.4 = (f32[4,16,512]{2,1,0:T(8,128)S(1)}, f32[4,16,512]{2,1,0:T(8,128)S(1)}, u32[]{:S(2)}, u32[]{:S(2)}) collective-permute-start(f32[4,16,512]{2,1,0:T(8,128)S(1)} %get-tuple-element.27), channel_id=1, source_target_pairs={{0,3},{1,2},{2,1},{3,0},{4,7},{5,6},{6,5},{7,4},{8,11},{9,10},{10,... | collective-permute-start | bytes 393224 | tf_op jit(solution)/shard_map/ppermute | solution.py:450
  26.2 0.0 collective-permute-done.6.cross_ref
  26.2 3.4 %collective-permute-done.5.pair_ref = f32[2,4,8,2048]{3,2,1,0:T(8,128)S(1)} collective-permute-done((f32[2,4,8,2048]{3,2,1,0:T(8,128)S(1)}, f32[2,4,8,2048]{3,2,1,0:T(8,128)S(1)}, u32[]{:S(2)}, u32[]{:S(2)}) %collective-permute-start.5) | collective-permute-done | bytes 524320 | tf_op jit(solution)/shard_map/ppermute | solution.py:367
  29.6 1.7 %edges.1 = (f32[4,8,256]{2,1,0:T(8,128)S(1)}, f32[4,8,256]{2,1,0:T(8,128)S(1)}, f32[4,8,256]{2,1,0:T(8,128)S(1)}, f32[4,8,256]{2,1,0:T(8,128)S(1)}) custom-call(s32[2,2,8]{2,1,0:T(2,128)S(1)} %copy-done.2, s32[1]{0:T(128)} %bitcast.depth_ref, s32[1]{0:T(128)} %bitcast.7.lat_ref, f32[8,16,9,8,128]{4,3,2,1,0:T(8,128)S(1)} %get-tuple-element.28.kept_ref, ...), custom_call_target="tpu_custom_call" | custom-call | tf_op jit(solution)/shard_map/edges/pallas_call | solution.py:455
  31.3 0.1 collective-permute-start.7
  31.3 1.6 %collective-permute-start.8 = (f32[4,8,256]{2,1,0:T(8,128)S(1)}, f32[4,8,256]{2,1,0:T(8,128)S(1)}, u32[]{:S(2)}, u32[]{:S(2)}) collective-permute-start(f32[4,8,256]{2,1,0:T(8,128)S(1)} %get-tuple-element.33), channel_id=1, source_target_pairs={{0,2},{1,3},{2,0},{3,1},{4,6},{5,7},{6,4},{7,5},{8,10},{9,11},{10,... | collective-permute-start | bytes 98312 | tf_op jit(solution)/shard_map/ppermute | solution.py:450
  32.9 0.0 collective-permute-done.7.refs_5_
  32.9 0.9 %collective-permute-start.9 = (f32[4,8,256]{2,1,0:T(8,128)S(1)}, f32[4,8,256]{2,1,0:T(8,128)S(1)}, u32[]{:S(2)}, u32[]{:S(2)}) collective-permute-start(f32[4,8,256]{2,1,0:T(8,128)S(1)} %get-tuple-element.34), channel_id=1, source_target_pairs={{0,3},{1,2},{2,1},{3,0},{4,7},{5,6},{6,5},{7,4},{8,11},{9,10},{10,... | collective-permute-start | bytes 98312 | tf_op jit(solution)/shard_map/ppermute | solution.py:450
  33.8 1.5 %collective-permute-done.8.refs_6_ = f32[4,8,256]{2,1,0:T(8,128)S(1)} collective-permute-done((f32[4,8,256]{2,1,0:T(8,128)S(1)}, f32[4,8,256]{2,1,0:T(8,128)S(1)}, u32[]{:S(2)}, u32[]{:S(2)}) %collective-permute-start.8) | collective-permute-done | bytes 32800 | tf_op jit(solution)/shard_map/ppermute | solution.py:450
  35.3 0.9 %collective-permute-done.9.refs_7_ = f32[4,8,256]{2,1,0:T(8,128)S(1)} collective-permute-done((f32[4,8,256]{2,1,0:T(8,128)S(1)}, f32[4,8,256]{2,1,0:T(8,128)S(1)}, u32[]{:S(2)}, u32[]{:S(2)}) %collective-permute-start.9) | collective-permute-done | bytes 32800 | tf_op jit(solution)/shard_map/ppermute | solution.py:450
  36.2 0.0 collective-permute-done.2.refs_1_
  36.3 0.0 collective-permute-done.3.refs_2_
  36.3 0.0 collective-permute-done.4.refs_3_
  36.3 0.7 %finish.1 = f32[4,16,512]{2,1,0:T(8,128)} custom-call(s32[1]{0:T(128)} %bitcast.depth_ref, f32[4,16,512]{2,1,0:T(8,128)S(1)} %get-tuple-element.24.refs_0_, f32[4,16,512]{2,1,0:T(8,128)S(1)} %collective-permute-done.2.refs_1_, f32[4,16,512]{2,1,0:T(8,128)S(1)} %collective-permute-done.3.refs_2_, f32[4,16,512]{2,1,0:T(8,128)S(1)} %collective-permute-done.4.refs_3_, ...), custom_call_target="tpu_custom_call" | custom-call | tf_op jit(solution)/shard_map/finish/pallas_call | solution.py:464
Async XLA Ops:
  1.4 24.8 %collective-permute-start.6 = (f32[2,4,8,2048]{3,2,1,0:T(8,128)S(1)}, f32[2,4,8,2048]{3,2,1,0:T(8,128)S(1)}, u32[]{:S(2)}, u32[]{:S(2)}) collective-permute-start(f32[2,4,8,2048]{3,2,1,0:T(8,128)S(1)} %get-tuple-element.30), channel_id=1, source_target_pairs={{4,8},{8,4},{12,16},{16,12},{20,24},{24,20},{5,9},{9,5},{13,17},{1... | collective-permute-start | bytes 1572872 | tf_op jit(solution)/shard_map/ppermute | solution.py:372
  2.1 27.5 %collective-permute-start.5 = (f32[2,4,8,2048]{3,2,1,0:T(8,128)S(1)}, f32[2,4,8,2048]{3,2,1,0:T(8,128)S(1)}, u32[]{:S(2)}, u32[]{:S(2)}) collective-permute-start(f32[2,4,8,2048]{3,2,1,0:T(8,128)S(1)} %get-tuple-element.20.after_ref), channel_id=1, source_target_pairs={{0,4},{4,0},{8,12},{12,8},{16,20},{20,16},{24,28},{28,24},{1,5},{5... | collective-permute-start | bytes 1572872 | tf_op jit(solution)/shard_map/ppermute | solution.py:367
  7.9 2.3 %copy-start = (f32[16,16,2048]{2,1,0:T(8,128)S(1)}, f32[16,16,2048]{2,1,0:T(8,128)}, u32[]{:S(2)}) copy-start(f32[16,16,2048]{2,1,0:T(8,128)} %grade_hbm.3) | copy-start | bytes 6291460
  7.9 2.5 %copy-start.1 = (f32[16,16,2048]{2,1,0:T(8,128)S(1)}, f32[16,16,2048]{2,1,0:T(8,128)}, u32[]{:S(2)}) copy-start(f32[16,16,2048]{2,1,0:T(8,128)} %amp_hbm.3) | copy-start | bytes 6291460
  7.9 2.5 %copy-start.2 = (s32[2,2,8]{2,1,0:T(2,128)S(1)}, s32[2,2,8]{2,1,0:T(2,128)}, u32[]{:S(2)}) copy-start(s32[2,2,8]{2,1,0:T(2,128)} %mask_ref.5) | copy-start | bytes 388
  7.9 2.5 %copy-start.3 = (s32[4,128]{1,0:T(4,128)S(1)}, s32[4,128]{1,0:T(4,128)}, u32[]{:S(2)}) copy-start(s32[4,128]{1,0:T(4,128)} %table_ref.3) | copy-start | bytes 6148
  9.3 8.1 %collective-permute-start = (f32[2,2,16,2048]{3,2,1,0:T(8,128)S(1)}, f32[2,2,16,2048]{3,2,1,0:T(8,128)S(1)}, u32[]{:S(2)}, u32[]{:S(2)}) collective-permute-start(f32[2,2,16,2048]{3,2,1,0:T(8,128)S(1)} %get-tuple-element.21), channel_id=1, source_target_pairs={{0,1},{1,0},{2,3},{3,2},{4,5},{5,4},{6,7},{7,6},{8,9},{9,8},{10,11... | collective-permute-start | bytes 1572872 | tf_op jit(solution)/shard_map/ppermute | solution.py:367
  9.3 8.0 %collective-permute-start.1 = (f32[2,2,16,2048]{3,2,1,0:T(8,128)S(1)}, f32[2,2,16,2048]{3,2,1,0:T(8,128)S(1)}, u32[]{:S(2)}, u32[]{:S(2)}) collective-permute-start(f32[2,2,16,2048]{3,2,1,0:T(8,128)S(1)} %get-tuple-element.22), channel_id=1, source_target_pairs={{1,2},{2,1},{5,6},{6,5},{9,10},{10,9},{13,14},{14,13},{17,18},{18,... | collective-permute-start | bytes 1572872 | tf_op jit(solution)/shard_map/ppermute | solution.py:372
  21.6 14.7 %collective-permute-start.2 = (f32[4,16,512]{2,1,0:T(8,128)S(1)}, f32[4,16,512]{2,1,0:T(8,128)S(1)}, u32[]{:S(2)}, u32[]{:S(2)}) collective-permute-start(f32[4,16,512]{2,1,0:T(8,128)S(1)} %get-tuple-element.25), channel_id=1, source_target_pairs={{0,1},{1,0},{2,3},{3,2},{4,5},{5,4},{6,7},{7,6},{8,9},{9,8},{10,11... | collective-permute-start | bytes 393224 | tf_op jit(solution)/shard_map/ppermute | solution.py:450
  24.8 11.5 %collective-permute-start.3 = (f32[4,16,512]{2,1,0:T(8,128)S(1)}, f32[4,16,512]{2,1,0:T(8,128)S(1)}, u32[]{:S(2)}, u32[]{:S(2)}) collective-permute-start(f32[4,16,512]{2,1,0:T(8,128)S(1)} %get-tuple-element.26), channel_id=1, source_target_pairs={{0,2},{1,3},{2,0},{3,1},{4,6},{5,7},{6,4},{7,5},{8,10},{9,11},{10,... | collective-permute-start | bytes 393224 | tf_op jit(solution)/shard_map/ppermute | solution.py:450
  25.2 11.1 %collective-permute-start.4 = (f32[4,16,512]{2,1,0:T(8,128)S(1)}, f32[4,16,512]{2,1,0:T(8,128)S(1)}, u32[]{:S(2)}, u32[]{:S(2)}) collective-permute-start(f32[4,16,512]{2,1,0:T(8,128)S(1)} %get-tuple-element.27), channel_id=1, source_target_pairs={{0,3},{1,2},{2,1},{3,0},{4,7},{5,6},{6,5},{7,4},{8,11},{9,10},{10,... | collective-permute-start | bytes 393224 | tf_op jit(solution)/shard_map/ppermute | solution.py:450
  31.3 1.6 %collective-permute-start.7 = (f32[4,8,256]{2,1,0:T(8,128)S(1)}, f32[4,8,256]{2,1,0:T(8,128)S(1)}, u32[]{:S(2)}, u32[]{:S(2)}) collective-permute-start(f32[4,8,256]{2,1,0:T(8,128)S(1)} %get-tuple-element.32), channel_id=1, source_target_pairs={{0,1},{1,0},{2,3},{3,2},{4,5},{5,4},{6,7},{7,6},{8,9},{9,8},{10,11... | collective-permute-start | bytes 98312 | tf_op jit(solution)/shard_map/ppermute | solution.py:450
  31.3 4.0 %collective-permute-start.8 = (f32[4,8,256]{2,1,0:T(8,128)S(1)}, f32[4,8,256]{2,1,0:T(8,128)S(1)}, u32[]{:S(2)}, u32[]{:S(2)}) collective-permute-start(f32[4,8,256]{2,1,0:T(8,128)S(1)} %get-tuple-element.33), channel_id=1, source_target_pairs={{0,2},{1,3},{2,0},{3,1},{4,6},{5,7},{6,4},{7,5},{8,10},{9,11},{10,... | collective-permute-start | bytes 98312 | tf_op jit(solution)/shard_map/ppermute | solution.py:450
  32.9 3.3 %collective-permute-start.9 = (f32[4,8,256]{2,1,0:T(8,128)S(1)}, f32[4,8,256]{2,1,0:T(8,128)S(1)}, u32[]{:S(2)}, u32[]{:S(2)}) collective-permute-start(f32[4,8,256]{2,1,0:T(8,128)S(1)} %get-tuple-element.34), channel_id=1, source_target_pairs={{0,3},{1,2},{2,1},{3,0},{4,7},{5,6},{6,5},{7,4},{8,11},{9,10},{10,... | collective-permute-start | bytes 98312 | tf_op jit(solution)/shard_map/ppermute | solution.py:450
